TPU v7x, 256 devices: a whole 4x4x8 slice. The times are simulated.
256 devices in a mesh: seq: 16 (over y_hi, x, core), dp: 16 (over y_lo, z).
Axes of the slice: x: 4, y: 4 (y_hi: 2, y_lo: 2; y = y_hi * 2 + y_lo), z: 8, core: 2. Of those that a mesh axis runs over, the one named last changes fastest.
Arguments:
- query: bfloat16 [16, 3072, 1280], P('dp', 'seq'), may hold values from -52 to 52, as said below
- keys: bfloat16 [16, 3072, 1280], P('dp', 'seq'), may hold values from -6 to 6, as said below
- values: bfloat16 [16, 3072, 1280], P('dp', 'seq'), may hold values from -6 to 6
- attn: bfloat16 [16, 3072, 1280], P('dp', 'seq'), may hold values from -6 to 6
- d_block: bfloat16 [16, 3072, 1280], P('dp', 'seq'), may hold values from -6 to 6
- w_out: bfloat16 [1280, 1280], P('dp'), may hold values from -0.15625 to 0.15625
Outputs:
- d_query: bfloat16 [16, 3072, 1280], P('dp', 'seq')
- d_keys: bfloat16 [16, 3072, 1280], P('dp', 'seq')
- d_values: bfloat16 [16, 3072, 1280], P('dp', 'seq')
- d_weight: float32 [1280, 1280], P('dp')
Inputs may be any that keep to these rules, and one draw needn't show every extreme that they name: Some query patches may lie along the sum of two keys of the same video. keys has entries of order one.
All inputs are finite; a program needn't handle non-finite values.
Results may differ from a plain program's by a relative error of at most 0.0058.
Values may be sent and summed in bfloat16 or wider, within the bound.
No kernel may reach another device: no remote copies, remote signals or barrier semaphores. Data moves between devices by JAX's collectives and lax.ppermute only.
A program may use at most 64 MiB of HBM per device.

v0:
```python
import jax
import jax.numpy as jnp
from jax import lax
from jax.sharding import Mesh
from jax.sharding import PartitionSpec as P

HEAD_DIM = 80
DP = ("dp_0", "dp_1")


def reduced_to_own(blocks, axes, order):
    lengths = [lax.axis_size(a) for a in axes]
    blocks = blocks.reshape(*lengths, *blocks.shape[1:])
    blocks = blocks.transpose(*order, *range(len(axes), blocks.ndim))
    blocks = blocks.reshape(-1, *blocks.shape[len(axes) :])
    for k in order:
        blocks = lax.psum_scatter(blocks, axes[k], scatter_dimension=0, tiled=True)
    return blocks[0]


def split_up(x, dim, size):
    before, after = (x.shape[:dim], x.shape[dim + 1 :])
    return jnp.moveaxis(x.reshape(*before, size, -1, *after), dim, 0)


def scatter_axes(x, axes, order, dim):
    size = lax.axis_size(axes)
    return reduced_to_own(split_up(x, dim, size), axes, order)


def over_pieces(x, axis):
    blocks = lax.all_gather(x, axis)
    return blocks.sum(axis=0)


def head_backward(query_h, keys_h, values_h, dout_h, delta_h):
    patch_total = query_h.shape[0]
    block_rows = min(512, patch_total)
    while patch_total % block_rows != 0:
        block_rows = block_rows // 2
    block_total = patch_total // block_rows
    score_scale = HEAD_DIM ** (-0.5)
    contract_last = (((1,), (1,)), ((), ()))
    contract_first = (((0,), (0,)), ((), ()))

    def one_block(carry, inputs):
        keys_grad, values_grad = carry
        query_block, dout_block, delta_block = inputs
        scores = (
            lax.dot_general(query_block, keys_h, contract_last, preferred_element_type=jnp.float32)
            * score_scale
        )
        row_max = jnp.max(scores, axis=1, keepdims=True)
        lse = row_max + jnp.log(jnp.sum(jnp.exp(scores - row_max), axis=1, keepdims=True))
        probs = jnp.exp(scores - lse)
        probs_low = probs.astype(jnp.bfloat16)
        values_grad = values_grad + lax.dot_general(
            probs_low, dout_block, contract_first, preferred_element_type=jnp.float32
        )
        d_probs = lax.dot_general(
            dout_block, values_h, contract_last, preferred_element_type=jnp.float32
        )
        d_scores = (score_scale * probs * (d_probs - delta_block[:, None])).astype(jnp.bfloat16)
        query_grad = jnp.dot(d_scores, keys_h, preferred_element_type=jnp.float32)
        keys_grad = keys_grad + lax.dot_general(
            d_scores, query_block, contract_first, preferred_element_type=jnp.float32
        )
        return ((keys_grad, values_grad), query_grad.astype(jnp.bfloat16))

    empty = jnp.zeros((patch_total, HEAD_DIM), jnp.float32)
    blocked = (
        query_h.reshape(block_total, block_rows, HEAD_DIM),
        dout_h.reshape(block_total, block_rows, HEAD_DIM),
        delta_h.reshape(block_total, block_rows),
    )
    (keys_grad, values_grad), query_blocks = lax.scan(one_block, (empty, empty), blocked)
    return (
        query_blocks.reshape(patch_total, HEAD_DIM),
        keys_grad.astype(jnp.bfloat16),
        values_grad.astype(jnp.bfloat16),
    )


def body(query, keys, values, attn, d_block, w_out):
    seq_count = lax.axis_size("seq")
    dp_count = lax.axis_size(DP)
    tok_rows = query.shape[1]
    features = query.shape[2]
    head_here = features // HEAD_DIM // seq_count
    grad_y = d_block.reshape(tok_rows, features)
    attn_rows = attn.reshape(tok_rows, features)
    d_out = lax.dot_general(
        grad_y,
        lax.all_gather(w_out, DP, axis=0, tiled=True),
        (((1,), (1,)), ((), ())),
        preferred_element_type=jnp.float32,
    ).astype(jnp.bfloat16)

    def split_heads(array):
        return array.reshape(tok_rows, seq_count, head_here, HEAD_DIM)

    row_local = jnp.sum(
        split_heads(d_out).astype(jnp.float32) * split_heads(attn_rows).astype(jnp.float32), axis=3
    )
    row_terms = lax.all_to_all(row_local, "seq", split_axis=1, concat_axis=0, tiled=True)
    query_all, keys_all, values_all, dout_all = (
        lax.all_to_all(split_heads(query), "seq", split_axis=1, concat_axis=0, tiled=True),
        lax.all_to_all(split_heads(keys), "seq", split_axis=1, concat_axis=0, tiled=True),
        lax.all_to_all(split_heads(values), "seq", split_axis=1, concat_axis=0, tiled=True),
        lax.all_to_all(split_heads(d_out), "seq", split_axis=1, concat_axis=0, tiled=True),
    )
    gradient = head_backward(
        query_all[:, 0, 0],
        keys_all[:, 0, 0],
        values_all[:, 0, 0],
        dout_all[:, 0, 0],
        row_terms[:, 0, 0],
    )
    query_list = [gradient[0]]
    keys_list = [gradient[1]]
    values_list = [gradient[2]]
    query_heads = jnp.stack(query_list, axis=1)[:, None]
    keys_heads = jnp.stack(keys_list, axis=1)[:, None]
    values_heads = jnp.stack(values_list, axis=1)[:, None]
    query_back, keys_back, values_back = (
        lax.all_to_all(query_heads, "seq", split_axis=0, concat_axis=1, tiled=True),
        lax.all_to_all(keys_heads, "seq", split_axis=0, concat_axis=1, tiled=True),
        lax.all_to_all(values_heads, "seq", split_axis=0, concat_axis=1, tiled=True),
    )
    factor = 1.0 / float(dp_count * tok_rows * seq_count) ** 0.5
    contract_first = (((0,), (0,)), ((), ()))
    partial_rows = scatter_axes(
        lax.dot_general(attn_rows, grad_y, contract_first, preferred_element_type=jnp.float32)
        * factor,
        DP,
        (1, 0),
        0,
    )
    d_weight = over_pieces(partial_rows, "seq")
    shape_out = (1, tok_rows, features)
    return (
        query_back.reshape(shape_out),
        keys_back.reshape(shape_out),
        values_back.reshape(shape_out),
        d_weight,
    )


def solution(mesh):
    finer = Mesh(mesh.devices.reshape(mesh.shape["seq"], 2, 8), ("seq", "dp_0", "dp_1"))
    in_specs = (
        P(DP, "seq", None),
        P(DP, "seq", None),
        P(DP, "seq", None),
        P(DP, "seq", None),
        P(DP, "seq", None),
        P(DP, None),
    )
    out_specs = (P(DP, "seq", None), P(DP, "seq", None), P(DP, "seq", None), P(DP, None))
    return jax.shard_map(body, mesh=finer, in_specs=in_specs, out_specs=out_specs, check_vma=False)
```

profile of v0, /device:TPU:1, one launch (start us, length us, event | category | flops | bytes accessed | tf_op | source)
XLA Modules:
  0.0 369.2 jit_solution(4399982114246284704)
XLA Ops:
  11.1 3.2 copy.106
  16.5 8.4 %all-to-all-start.3 = ((bf16[192,16,1,80]{0,3,2,1:T(8,128)(2,1)}), bf16[192,16,1,80]{0,3,2,1:T(8,128)(2,1)S(1)}, u32[]{:S(2)}, u32[]{:S(2)}) async-start(bf16[192,16,1,80]{0,3,2,1:T(8,128)(2,1)} %bitcast.17), calls=%async_computation.3 | async-start | bytes 1310720 | tf_op jit(solution)/shard_map/all_to_all | solution.py:109
  25.0 84.7 %reduce-scatter.3.cloned.1.call-done = f32[2,80,1280]{2,1,0:T(8,128)} async-done(((f32[16,80,1280]{2,1,0:T(8,128)}), f32[2,80,1280]{2,1,0:T(8,128)}) %reduce-scatter.3.cloned.1.call-update) | async-done | bytes 819216 | tf_op jit(solution)/shard_map/reduce_scatter | solution.py:17
  110.8 7.6 %all-to-all-start = ((bf16[192,16,1,80]{0,3,2,1:T(8,128)(2,1)}), bf16[192,16,1,80]{0,3,2,1:T(8,128)(2,1)S(1)}, u32[]{:S(2)}, u32[]{:S(2)}) async-start(bf16[192,16,1,80]{0,3,2,1:T(8,128)(2,1)} %bitcast.1), calls=%async_computation | async-start | bytes 1310720 | tf_op jit(solution)/shard_map/all_to_all | solution.py:107
  120.6 18.7 %all-to-all-done = bf16[192,16,1,80]{0,3,2,1:T(8,128)(2,1)S(1)} async-done(((bf16[192,16,1,80]{0,3,2,1:T(8,128)(2,1)}), bf16[192,16,1,80]{0,3,2,1:T(8,128)(2,1)S(1)}, u32[]{:S(2)}, u32[]{:S(2)}) %all-to-all-start) | async-done | bytes 491552 | tf_op jit(solution)/shard_map/all_to_all | solution.py:107
  139.3 4.8 %all-to-all-start.1 = ((bf16[192,16,1,80]{0,3,2,1:T(8,128)(2,1)}), bf16[192,16,1,80]{0,3,2,1:T(8,128)(2,1)S(1)}, u32[]{:S(2)}, u32[]{:S(2)}) async-start(bf16[192,16,1,80]{0,3,2,1:T(8,128)(2,1)} %bitcast.124), calls=%async_computation.1 | async-start | bytes 1310720 | tf_op jit(solution)/shard_map/all_to_all | solution.py:108
  144.1 3.2 convolution_convert_fusion.1
  149.9 7.1 %all-to-all-done.1 = bf16[192,16,1,80]{0,3,2,1:T(8,128)(2,1)S(1)} async-done(((bf16[192,16,1,80]{0,3,2,1:T(8,128)(2,1)}), bf16[192,16,1,80]{0,3,2,1:T(8,128)(2,1)S(1)}, u32[]{:S(2)}, u32[]{:S(2)}) %all-to-all-start.1) | async-done | bytes 491552 | tf_op jit(solution)/shard_map/all_to_all | solution.py:108
  157.0 11.4 %all_to_all.120 = f32[192,16,1]{0,2,1:T(1,128)S(1)} all-to-all(f32[192,16,1]{0,2,1:T(1,128)S(1)} %reduce_sum.30), channel_id=1, replica_groups=mesh['seq'=16,'dp_0'=2,'dp_1'=8] {'seq'}, dimensions={1} | all-to-all | bytes 24576 | tf_op jit(solution)/shard_map/all_to_all | solution.py:105
  168.4 4.4 %all-to-all-start.2 = ((bf16[192,16,1,80]{0,3,2,1:T(8,128)(2,1)}), bf16[192,16,1,80]{0,3,2,1:T(8,128)(2,1)}, u32[]{:S(2)}, u32[]{:S(2)}) async-start(bf16[192,16,1,80]{0,3,2,1:T(8,128)(2,1)} %bitcast.12), calls=%async_computation.2 | async-start | bytes 1310720 | tf_op jit(solution)/shard_map/all_to_all | solution.py:110
  178.3 7.7 %all-to-all-done.2 = bf16[192,16,1,80]{0,3,2,1:T(8,128)(2,1)} async-done(((bf16[192,16,1,80]{0,3,2,1:T(8,128)(2,1)}), bf16[192,16,1,80]{0,3,2,1:T(8,128)(2,1)}, u32[]{:S(2)}, u32[]{:S(2)}) %all-to-all-start.2) | async-done | bytes 491552 | tf_op jit(solution)/shard_map/all_to_all | solution.py:110
  188.3 101.8 %while.15 = (s32[]{:T(128)}, f32[3072,80]{0,1:T(8,128)S(1)}, f32[3072,80]{0,1:T(8,128)S(1)}, bf16[6,512,80]{1,2,0:T(8,128)(2,1)}, bf16[6,512,80]{2,1,0:T(8,128)(...) while((s32[]{:T(128)}, f32[3072,80]{0,1:T(8,128)S(1)}, ...), condition=%wide.region_4.5_spmd.clone, body=%wide.region_1.4_spmd.clone.sunk | while | flops 1281334784 | bytes 91267760 | solution.py:76
  194.1 4.5 %convolution_add_fusion.5 = f32[3072,80]{0,1:T(8,128)S(1)} fusion(f32[512,3072]{1,0:T(8,128)} %copy-done.2, f32[512]{0:T(512)S(1)} %log_add_fusion.2, f32[3072,80]{0,1:T(8,128)S(1)} %get-tuple-element.223, pred[]{:T(512)S(6)} %compare.3, bf16[6,512,80]{2,1,0:T(8,128)(2,1)} %get-tuple-element.238, s32[]{:T(128)} %get-tuple-element.221), kind=kOutput, calls=%fused_computation.5.clone.1 | convolution fusion | flops 256868352 | bytes 8391169 | tf_op jit(solution)/shard_map/while/body/eval_jaxpr/dot_general | solution.py:57
  211.1 4.3 %convolution_add_fusion.5 = f32[3072,80]{0,1:T(8,128)S(1)} fusion(f32[512,3072]{1,0:T(8,128)} %copy-done.2, f32[512]{0:T(512)S(1)} %log_add_fusion.2, f32[3072,80]{0,1:T(8,128)S(1)} %get-tuple-element.223, pred[]{:T(512)S(6)} %compare.3, bf16[6,512,80]{2,1,0:T(8,128)(2,1)} %get-tuple-element.238, s32[]{:T(128)} %get-tuple-element.221), kind=kOutput, calls=%fused_computation.5.clone.1 | convolution fusion | flops 256868352 | bytes 8391169 | tf_op jit(solution)/shard_map/while/body/eval_jaxpr/dot_general | solution.py:57
  228.0 4.4 %convolution_add_fusion.5 = f32[3072,80]{0,1:T(8,128)S(1)} fusion(f32[512,3072]{1,0:T(8,128)} %copy-done.2, f32[512]{0:T(512)S(1)} %log_add_fusion.2, f32[3072,80]{0,1:T(8,128)S(1)} %get-tuple-element.223, pred[]{:T(512)S(6)} %compare.3, bf16[6,512,80]{2,1,0:T(8,128)(2,1)} %get-tuple-element.238, s32[]{:T(128)} %get-tuple-element.221), kind=kOutput, calls=%fused_computation.5.clone.1 | convolution fusion | flops 256868352 | bytes 8391169 | tf_op jit(solution)/shard_map/while/body/eval_jaxpr/dot_general | solution.py:57
  244.9 4.4 %convolution_add_fusion.5 = f32[3072,80]{0,1:T(8,128)S(1)} fusion(f32[512,3072]{1,0:T(8,128)} %copy-done.2, f32[512]{0:T(512)S(1)} %log_add_fusion.2, f32[3072,80]{0,1:T(8,128)S(1)} %get-tuple-element.223, pred[]{:T(512)S(6)} %compare.3, bf16[6,512,80]{2,1,0:T(8,128)(2,1)} %get-tuple-element.238, s32[]{:T(128)} %get-tuple-element.221), kind=kOutput, calls=%fused_computation.5.clone.1 | convolution fusion | flops 256868352 | bytes 8391169 | tf_op jit(solution)/shard_map/while/body/eval_jaxpr/dot_general | solution.py:57
  262.1 4.3 %convolution_add_fusion.5 = f32[3072,80]{0,1:T(8,128)S(1)} fusion(f32[512,3072]{1,0:T(8,128)} %copy-done.2, f32[512]{0:T(512)S(1)} %log_add_fusion.2, f32[3072,80]{0,1:T(8,128)S(1)} %get-tuple-element.223, pred[]{:T(512)S(6)} %compare.3, bf16[6,512,80]{2,1,0:T(8,128)(2,1)} %get-tuple-element.238, s32[]{:T(128)} %get-tuple-element.221), kind=kOutput, calls=%fused_computation.5.clone.1 | convolution fusion | flops 256868352 | bytes 8391169 | tf_op jit(solution)/shard_map/while/body/eval_jaxpr/dot_general | solution.py:57
  279.0 4.3 %convolution_add_fusion.5 = f32[3072,80]{0,1:T(8,128)S(1)} fusion(f32[512,3072]{1,0:T(8,128)} %copy-done.2, f32[512]{0:T(512)S(1)} %log_add_fusion.2, f32[3072,80]{0,1:T(8,128)S(1)} %get-tuple-element.223, pred[]{:T(512)S(6)} %compare.3, bf16[6,512,80]{2,1,0:T(8,128)(2,1)} %get-tuple-element.238, s32[]{:T(128)} %get-tuple-element.221), kind=kOutput, calls=%fused_computation.5.clone.1 | convolution fusion | flops 256868352 | bytes 8391169 | tf_op jit(solution)/shard_map/while/body/eval_jaxpr/dot_general | solution.py:57
  294.3 4.1 %all-to-all-start.7 = ((bf16[16,2,7680]{2,1,0:T(2,128)(2,1)}), bf16[16,2,7680]{2,1,0:T(2,128)(2,1)S(1)}, u32[]{:S(2)}, u32[]{:S(2)}) async-start(bf16[16,2,7680]{2,1,0:T(2,128)(2,1)} %reshape.106), calls=%async_computation.7 | async-start | bytes 983040 | tf_op jit(solution)/shard_map/all_to_all | solution.py:128
  301.9 7.6 %all-to-all-done.7 = bf16[16,2,7680]{2,1,0:T(2,128)(2,1)S(1)} async-done(((bf16[16,2,7680]{2,1,0:T(2,128)(2,1)}), bf16[16,2,7680]{2,1,0:T(2,128)(2,1)S(1)}, u32[]{:S(2)}, u32[]{:S(2)}) %all-to-all-start.7) | async-done | bytes 491552 | tf_op jit(solution)/shard_map/all_to_all | solution.py:128
  309.5 4.4 %all-to-all-start.6 = ((bf16[16,2,7680]{2,1,0:T(2,128)(2,1)}), bf16[16,2,7680]{2,1,0:T(2,128)(2,1)S(1)}, u32[]{:S(2)}, u32[]{:S(2)}) async-start(bf16[16,2,7680]{2,1,0:T(2,128)(2,1)} %reshape.104), calls=%async_computation.6 | async-start | bytes 983040 | tf_op jit(solution)/shard_map/all_to_all | solution.py:127
  315.7 17.0 %reduce.3 = bf16[3072,80]{1,0:T(8,128)(2,1)S(1)} reduce(bf16[3072,1,1,80]{3,2,1,0:T(2,128)(2,1)S(1)} %reshape.100, bf16[]{:T(256)} %broadcast.25), dimensions={1,2}, to_apply=%reshape.100.reduce_sub_computation | reduce | bytes 983042 | tf_op jit(solution)/shard_map/broadcast_in_dim;stack;reshape | solution.py:122
  334.9 7.3 %all-to-all-start.5 = ((bf16[16,2,7680]{2,1,0:T(2,128)(2,1)}), bf16[16,2,7680]{2,1,0:T(2,128)(2,1)S(1)}, u32[]{:S(2)}, u32[]{:S(2)}) async-start(bf16[16,2,7680]{2,1,0:T(2,128)(2,1)} %reshape.102), calls=%async_computation.5 | async-start | bytes 983040 | tf_op jit(solution)/shard_map/all_to_all | solution.py:126
  358.1 4.0 %reduce_sum.31 = f32[80,1280]{1,0:T(8,128)} reduce(f32[16,80,1280]{2,1,0:T(8,128)} %all-gather.5.cloned.1.call-done, f32[]{:T(128)} %constant.13.clone.1), dimensions={0}, to_apply=%region_7.8 | reduce | flops 1536000 | bytes 6963204 | tf_op jit(solution)/shard_map/reduce_sum | solution.py:33
  (139 shorter events, 121.6 us)
Async XLA Ops:
  8.0 101.7 %reduce-scatter.3.cloned.1.call-start = ((), (), s32[]{:S(2)}) async-start(), calls=%async_computation.11 | async-start | bytes 7372800 | tf_op jit(solution)/shard_map/reduce_scatter | solution.py:17
  14.3 95.4 %copy-start.8 = (bf16[1,192,1280]{2,1,0:T(8,128)(2,1)S(1)}, bf16[1,192,1280]{2,1,0:T(8,128)(2,1)}, u32[]{:S(2)}) copy-start(bf16[1,192,1280]{2,1,0:T(8,128)(2,1)} %param.8) | copy-start | bytes 1474564
  14.3 104.1 %copy-start.4 = (bf16[1,192,1280]{2,1,0:T(8,128)(2,1)S(1)}, bf16[1,192,1280]{2,1,0:T(8,128)(2,1)}, u32[]{:S(2)}) copy-start(bf16[1,192,1280]{2,1,0:T(8,128)(2,1)} %param.11) | copy-start | bytes 1474564
  14.4 105.1 %copy-start.9 = (bf16[1,192,1280]{2,1,0:T(8,128)(2,1)S(1)}, bf16[1,192,1280]{2,1,0:T(8,128)(2,1)}, u32[]{:S(2)}) copy-start(bf16[1,192,1280]{2,1,0:T(8,128)(2,1)} %param.9) | copy-start | bytes 1474564
  14.4 129.7 %all-gather.3.cloned.1.call-start = ((), (), s32[]{:S(2)}) async-start(), calls=%async_computation.10 | async-start | bytes 3481600 | tf_op jit(solution)/shard_map/all_gather | solution.py:94
  16.5 94.4 %all-to-all-start.3 = ((bf16[192,16,1,80]{0,3,2,1:T(8,128)(2,1)}), bf16[192,16,1,80]{0,3,2,1:T(8,128)(2,1)S(1)}, u32[]{:S(2)}, u32[]{:S(2)}) async-start(bf16[192,16,1,80]{0,3,2,1:T(8,128)(2,1)} %bitcast.17), calls=%async_computation.3 | async-start | bytes 1310720 | tf_op jit(solution)/shard_map/all_to_all | solution.py:109
  24.9 163.4 %reduce-scatter.5.cloned.1.call-start = ((), (), s32[]{:S(2)}) async-start(), calls=%async_computation.12 | async-start | bytes 1228800 | tf_op jit(solution)/shard_map/reduce_scatter | solution.py:17
  110.8 28.5 %all-to-all-start = ((bf16[192,16,1,80]{0,3,2,1:T(8,128)(2,1)}), bf16[192,16,1,80]{0,3,2,1:T(8,128)(2,1)S(1)}, u32[]{:S(2)}, u32[]{:S(2)}) async-start(bf16[192,16,1,80]{0,3,2,1:T(8,128)(2,1)} %bitcast.1), calls=%async_computation | async-start | bytes 1310720 | tf_op jit(solution)/shard_map/all_to_all | solution.py:107
  139.3 33.5 %copy-start.5 = (bf16[192,16,1,80]{0,3,2,1:T(8,128)(2,1)}, bf16[192,16,1,80]{0,3,2,1:T(8,128)(2,1)S(1)}, u32[]{:S(2)}) copy-start(bf16[192,16,1,80]{0,3,2,1:T(8,128)(2,1)S(1)} %all-to-all-done) | copy-start | bytes 1474564
  139.3 17.7 %all-to-all-start.1 = ((bf16[192,16,1,80]{0,3,2,1:T(8,128)(2,1)}), bf16[192,16,1,80]{0,3,2,1:T(8,128)(2,1)S(1)}, u32[]{:S(2)}, u32[]{:S(2)}) async-start(bf16[192,16,1,80]{0,3,2,1:T(8,128)(2,1)} %bitcast.124), calls=%async_computation.1 | async-start | bytes 1310720 | tf_op jit(solution)/shard_map/all_to_all | solution.py:108
  157.0 16.1 %copy-start.6 = (bf16[192,16,1,80]{0,3,2,1:T(8,128)(2,1)}, bf16[192,16,1,80]{0,3,2,1:T(8,128)(2,1)S(1)}, u32[]{:S(2)}) copy-start(bf16[192,16,1,80]{0,3,2,1:T(8,128)(2,1)S(1)} %all-to-all-done.1) | copy-start | bytes 1474564
  168.4 17.6 %all-to-all-start.2 = ((bf16[192,16,1,80]{0,3,2,1:T(8,128)(2,1)}), bf16[192,16,1,80]{0,3,2,1:T(8,128)(2,1)}, u32[]{:S(2)}, u32[]{:S(2)}) async-start(bf16[192,16,1,80]{0,3,2,1:T(8,128)(2,1)} %bitcast.12), calls=%async_computation.2 | async-start | bytes 1310720 | tf_op jit(solution)/shard_map/all_to_all | solution.py:110
  172.8 185.3 %all-gather.5.cloned.1.call-start = ((), (), s32[]{:S(2)}) async-start(), calls=%async_computation.13 | async-start | bytes 6963200 | tf_op jit(solution)/shard_map/all_gather | solution.py:32
  190.3 2.6 copy-start.2
  194.1 4.9 %copy-start.3 = (f32[512,3072]{1,0:T(8,128)S(1)}, f32[512,3072]{1,0:T(8,128)}, u32[]{:S(2)}) copy-start(f32[512,3072]{1,0:T(8,128)} %copy-done.2) | copy-start | bytes 18874372 | tf_op jit(solution)/shard_map/while
  211.1 4.6 %copy-start.3 = (f32[512,3072]{1,0:T(8,128)S(1)}, f32[512,3072]{1,0:T(8,128)}, u32[]{:S(2)}) copy-start(f32[512,3072]{1,0:T(8,128)} %copy-done.2) | copy-start | bytes 18874372 | tf_op jit(solution)/shard_map/while
  228.0 4.7 %copy-start.3 = (f32[512,3072]{1,0:T(8,128)S(1)}, f32[512,3072]{1,0:T(8,128)}, u32[]{:S(2)}) copy-start(f32[512,3072]{1,0:T(8,128)} %copy-done.2) | copy-start | bytes 18874372 | tf_op jit(solution)/shard_map/while
  244.9 5.0 %copy-start.3 = (f32[512,3072]{1,0:T(8,128)S(1)}, f32[512,3072]{1,0:T(8,128)}, u32[]{:S(2)}) copy-start(f32[512,3072]{1,0:T(8,128)} %copy-done.2) | copy-start | bytes 18874372 | tf_op jit(solution)/shard_map/while
  262.1 4.6 %copy-start.3 = (f32[512,3072]{1,0:T(8,128)S(1)}, f32[512,3072]{1,0:T(8,128)}, u32[]{:S(2)}) copy-start(f32[512,3072]{1,0:T(8,128)} %copy-done.2) | copy-start | bytes 18874372 | tf_op jit(solution)/shard_map/while
  279.0 4.6 %copy-start.3 = (f32[512,3072]{1,0:T(8,128)S(1)}, f32[512,3072]{1,0:T(8,128)}, u32[]{:S(2)}) copy-start(f32[512,3072]{1,0:T(8,128)} %copy-done.2) | copy-start | bytes 18874372 | tf_op jit(solution)/shard_map/while
  294.3 15.2 %all-to-all-start.7 = ((bf16[16,2,7680]{2,1,0:T(2,128)(2,1)}), bf16[16,2,7680]{2,1,0:T(2,128)(2,1)S(1)}, u32[]{:S(2)}, u32[]{:S(2)}) async-start(bf16[16,2,7680]{2,1,0:T(2,128)(2,1)} %reshape.106), calls=%async_computation.7 | async-start | bytes 983040 | tf_op jit(solution)/shard_map/all_to_all | solution.py:128
  309.5 25.4 %all-to-all-start.6 = ((bf16[16,2,7680]{2,1,0:T(2,128)(2,1)}), bf16[16,2,7680]{2,1,0:T(2,128)(2,1)S(1)}, u32[]{:S(2)}, u32[]{:S(2)}) async-start(bf16[16,2,7680]{2,1,0:T(2,128)(2,1)} %reshape.104), calls=%async_computation.6 | async-start | bytes 983040 | tf_op jit(solution)/shard_map/all_to_all | solution.py:127
  334.9 18.1 %all-to-all-start.5 = ((bf16[16,2,7680]{2,1,0:T(2,128)(2,1)}), bf16[16,2,7680]{2,1,0:T(2,128)(2,1)S(1)}, u32[]{:S(2)}, u32[]{:S(2)}) async-start(bf16[16,2,7680]{2,1,0:T(2,128)(2,1)} %reshape.102), calls=%async_computation.5 | async-start | bytes 983040 | tf_op jit(solution)/shard_map/all_to_all | solution.py:126
  353.0 9.0 %copy-start.1 = (bf16[1,192,1280]{2,1,0:T(8,128)(2,1)S(1)}, bf16[1,192,1280]{2,1,0:T(8,128)(2,1)}, u32[]{:S(2)}) copy-start(bf16[1,192,1280]{2,1,0:T(8,128)(2,1)} %param.12) | copy-start | bytes 1474564
  (7 other events, 15.1 us)
Sparse Core Ops, SparseCore 0:
  14.5 95.1 reduce-scatter.2
  112.2 40.2 reduce-scatter.4
  188.4 64.1 all-gather.4
Sparse Core Ops, SparseCore 1:
  16.6 123.8 all-gather.2
where the time goes:
time: 371 us; the launch traced here: 369 us
  waiting for transfers between devices  127 us (34%)
  matrix products  81.9 us (22%)
  local copies, waits for them, and re-layouts  60.2 us (16%)
  starting transfers between devices  41.3 us (11%)
  other arithmetic  31.5 us (8%)
  between operations  15.4 us (4%)
  blocking collectives  11.4 us (3%)
    reduce_scatter x2, waiting for transfers between devices, reduced_to_own(): blocks = lax.psum_scatter(blocks, axes[k], scatter_dimension=0, tiled=True)  84.7 us
    unnamed x35, local copies, waits for them, and re-layouts  28.3 us
    dot_general x6, matrix products, one_block(): lax.dot_general(probs_low, dout_block, contract_first, preferred_element_...  26.2 us
    all_to_all x1, waiting for transfers between devices, body(): lax.all_to_all(split_heads(query), 'seq', split_axis=1, concat_axis=0, ti...  18.7 us
    dot_general x6, matrix products, one_block(): lax.dot_general(dout_block, values_h, contract_last, preferred_element_ty...  17.9 us
    while x24, local copies, waits for them, and re-layouts  17.7 us
    another operation x1, other arithmetic, body(): query_heads = jnp.stack(query_list, axis=1)[:, None]  17 us
    dot_general x6, matrix products, one_block(): lax.dot_general(query_block, keys_h, contract_last, preferred_element_typ...  11.8 us
  transfers between devices with their start and end apart: 11, of which 6 were waited for; matrix products, arithmetic and copies ran while one was open for 39% of the time, Pallas kernels for 0%

commit v1 on v0

v1 whole, which is shorter than its diff:
```python
import functools

import jax
import jax.numpy as jnp
from jax import lax
from jax.experimental import pallas as pl
from jax.experimental.pallas import tpu as pltpu
from jax.sharding import Mesh
from jax.sharding import PartitionSpec as P

BF = jnp.bfloat16
F32 = jnp.float32
HD = 80
HALF = 40
HEADS = 16
SRC = 16
N = 3072
TOK = 192
BIG = 128
SMALL = 64
EXT = 96
D = 1280
SCALE = HD**-0.5
LOG2E = 1.4426950408889634
VMEM_LIMIT = 56 * 1024 * 1024
SEQ = ("yh", "x", "c")
DP = ("yl", "z")
OFFSETS = (0, -1, 1, -2, 2, -3, 3, -4)


def params(limit=VMEM_LIMIT):
    return pltpu.CompilerParams(vmem_limit_bytes=limit)


def cost(flops, read, exps=0):
    return pl.CostEstimate(flops=flops, bytes_accessed=read, transcendentals=exps)


def whole(*shape):
    return pl.BlockSpec(shape, lambda *_: (0,) * len(shape))


def dot(a, b, ca, cb):
    return lax.dot_general(a, b, (((ca,), (cb,)), ((), ())), preferred_element_type=F32)


def lanes3(a, b):
    return jnp.concatenate([a[:, :BIG], b[:, :BIG], a[:, BIG:], b[:, BIG:]], axis=1)


def pack_qkv_body(q_ref, k_ref, v_ref, out_ref):
    qt, kt, vt = q_ref[0].T, k_ref[0].T, v_ref[0].T
    for h in range(HEADS):
        a = h * HD
        out_ref[h, 0:HD, :] = lanes3(qt[a : a + HD], kt[a : a + HD])
        v = vt[a : a + HD].astype(F32)
        out_ref[h, HD : HD + HALF, :] = lanes3(v[:HALF], v[HALF:]).astype(BF)


def pack_qkv(q, k, v):
    return pl.pallas_call(
        pack_qkv_body,
        out_shape=jax.ShapeDtypeStruct((HEADS, HD + HALF, 384), BF),
        compiler_params=params(),
        cost_estimate=cost(0, 3 * 10**6),
        name="pack_qkv",
    )(q, k, v)


def split_attn_body(c_ref, a_ref, own_ref, send_ref, at):
    at[...] = a_ref[0].T.astype(F32)
    c = c_ref[0]
    for h in range(HEADS):
        keep = pl.multiple_of(h * HD + c * HALF, 8)
        give = pl.multiple_of(h * HD + (1 - c) * HALF, 8)
        own_ref[h] = at[pl.ds(keep, HALF), :].astype(BF)
        send_ref[h] = at[pl.ds(give, HALF), :].astype(BF)


def split_attn(c, attn):
    vm = pl.BlockSpec(memory_space=pltpu.VMEM)
    shape = jax.ShapeDtypeStruct((HEADS, HALF, TOK), BF)
    return pl.pallas_call(
        split_attn_body,
        in_specs=[pl.BlockSpec(memory_space=pltpu.SMEM), vm],
        out_specs=[vm, vm],
        out_shape=[shape, shape],
        scratch_shapes=[pltpu.VMEM((D, TOK), F32)],
        compiler_params=params(),
        cost_estimate=cost(0, 10**6),
        name="split_attn",
    )(c, attn)


def weight_share_body(y_ref, g_own, g_oth, a_own, a_oth, keep_ref, give_ref, gx_ref, ax_ref, acc):
    gx_ref[0:128] = g_own[0, 0:128]
    gx_ref[128:256] = g_oth[0, 0:128]
    gx_ref[256:320] = g_own[0, 128:192]
    gx_ref[320:384] = g_oth[0, 128:192]
    for h in range(HEADS):
        ax_ref[h] = lanes3(a_own[h].astype(F32), a_oth[h].astype(F32)).astype(BF)
    rows = jnp.concatenate([ax_ref[h].astype(F32) for h in range(HEADS)], axis=0).astype(BF)
    acc[...] = dot(rows, gx_ref[...], 1, 0)
    y = y_ref[0]
    for k in range(8):
        keep = pl.multiple_of((y * 8 + k) * HALF, 8)
        give = pl.multiple_of(((1 - y) * 8 + k) * HALF, 8)
        keep_ref[k] = acc[pl.ds(keep, HALF), :].astype(BF)
        give_ref[k] = acc[pl.ds(give, HALF), :].astype(BF)


def weight_share(y, g_own, g_oth, a_own, a_oth):
    vm = pl.BlockSpec(memory_space=pltpu.VMEM)
    return pl.pallas_call(
        weight_share_body,
        in_specs=[pl.BlockSpec(memory_space=pltpu.SMEM)] + [vm] * 4,
        out_specs=[vm] * 4,
        out_shape=[
            jax.ShapeDtypeStruct((8, HALF, D), BF),
            jax.ShapeDtypeStruct((8, HALF, D), BF),
            jax.ShapeDtypeStruct((384, D), BF),
            jax.ShapeDtypeStruct((HEADS, HALF, 384), BF),
        ],
        scratch_shapes=[pltpu.VMEM((640, D), F32)],
        compiler_params=params(),
        cost_estimate=cost(2 * 640 * 384 * D, 6 * 10**6),
        name="weight_share",
    )(y, g_own, g_oth, a_own, a_oth)


def sum_z_body(x_ref, out_ref):
    t = x_ref[0].astype(F32)
    for k in range(1, 8):
        t = t + x_ref[k].astype(F32)
    pad = jnp.zeros((7, 128), F32)
    for g in range(8):
        rows = t[5 * g : 5 * g + 5]
        for half in range(2):
            a = half * 640
            p = jnp.concatenate([rows[:, a + 128 * j : a + 128 * j + 128] for j in range(5)] + [pad], axis=0)
            out_ref[2 * g + half] = jnp.concatenate([p[:16], p[16:]], axis=1).astype(BF)


def sum_z(x):
    return pl.pallas_call(
        sum_z_body,
        out_shape=jax.ShapeDtypeStruct((SRC, 16, 256), BF),
        compiler_params=params(),
        cost_estimate=cost(0, 10**6),
        name="sum_z",
    )(x)


def sum_seq_body(x_ref, out_ref):
    halves = []
    for c in range(2):
        t = x_ref[c].astype(F32)
        for k in range(1, 8):
            t = t + x_ref[2 * k + c].astype(F32)
        halves.append(jnp.concatenate([t[:, :128], t[:9, 128:]], axis=0))
    t = jnp.concatenate(halves + [jnp.zeros((6, 128), F32)], axis=0) * (1.0 / float(16 * N) ** 0.5)
    low = t.astype(BF)
    for s in range(SRC):
        out_ref[s] = low


def sum_seq(x):
    return pl.pallas_call(
        sum_seq_body,
        out_shape=jax.ShapeDtypeStruct((SRC, 56, 128), BF),
        compiler_params=params(),
        cost_estimate=cost(0, 10**6),
        name="sum_seq",
    )(x)


def out_grad_body(ids, *refs):
    w_refs, (gx_ref, ax_ref, out_ref, w, acc) = refs[:8], refs[8:]
    for r in range(8):
        both = jnp.concatenate([w_refs[r][0].astype(F32), w_refs[r][1].astype(F32)], axis=0)
        w[r * HD : (r + 1) * HD] = both.astype(BF)
    acc[...] = dot(w[...], gx_ref[...], 1, 1)
    for r in range(HEADS):
        h = ids[r]
        low = acc[r * HALF : (r + 1) * HALF].astype(BF).astype(F32)
        minus = -jnp.sum(low * ax_ref[h].astype(F32), axis=0, keepdims=True)
        p1 = minus.astype(BF).astype(F32)
        p2 = (minus - p1).astype(BF).astype(F32)
        p3 = minus - p1 - p2
        pad = jnp.zeros((5, 384), F32)
        out_ref[h] = jnp.concatenate([low, p1, p2, p3, pad], axis=0).astype(BF)


def out_grad(ids, blocks, gx, ax):
    vm = pl.BlockSpec(memory_space=pltpu.VMEM)
    return pl.pallas_call(
        out_grad_body,
        in_specs=[pl.BlockSpec(memory_space=pltpu.SMEM)] + [vm] * 10,
        out_specs=vm,
        out_shape=jax.ShapeDtypeStruct((HEADS, 48, 384), BF),
        scratch_shapes=[pltpu.VMEM((640, D), BF), pltpu.VMEM((640, 384), F32)],
        compiler_params=params(),
        cost_estimate=cost(2 * 640 * 384 * D, 4 * 10**6),
        name="out_grad",
    )(ids, *blocks, gx, ax)


def each_place(put):
    for s in range(SRC):
        put(s * BIG, ((s, 0),))
    for s in range(0, SRC, 2):
        put(SRC * BIG + s * SMALL, ((s, 1), (s + 1, 1)))


def piece(x_ref, s, rows, col, small):
    if small:
        a = 2 * BIG + col * SMALL
        return x_ref[s, rows, a : a + SMALL]
    return x_ref[s, rows, col * BIG : (col + 1) * BIG]


def joined(parts):
    return parts[0] if len(parts) == 1 else jnp.concatenate(parts, axis=1)


def score_half(kn, q, s_new, s_old, m_old, emit, chunk, cols):
    m = jnp.full((8, cols), -jnp.inf, F32)
    total = jnp.zeros((8, cols), F32)
    for r in range(0, N, chunk):
        if q is not None:
            s = dot(kn[r : r + chunk, :], q, 1, 0)
            s_new[r : r + chunk, :] = s
            m = jnp.maximum(m, jnp.max(s.reshape(chunk // 8, 8, cols), axis=0))
        if s_old is not None:
            e = jnp.exp2((s_old[r : r + chunk, :] - m_old) * (SCALE * LOG2E))
            total = total + jnp.sum(e.reshape(chunk // 8, 8, cols), axis=0)
            emit(r, e.astype(BF))
    return jnp.max(m, axis=0, keepdims=True), jnp.sum(total, axis=0, keepdims=True)


def scores_body(cols, chunk, x_ref, e_ref, inv_ref, qn_ref, kt_ref, vn_ref, qt, kn, sa, sb, ma):
    i = pl.program_id(0)
    blocks = N // cols

    @pl.when(i == 0)
    def _():
        ones = jnp.concatenate([jnp.ones((8, 128), F32), jnp.zeros((8, 128), F32)], axis=0)

        def put(a, pieces):
            q = joined([piece(x_ref, s, slice(0, HD), 0, small) for s, small in pieces])
            k = joined([piece(x_ref, s, slice(0, HD), 1, small) for s, small in pieces])
            qt[:, a : a + 128] = q
            qn_ref[a : a + 128, :] = q.T
            kt_ref[:, a : a + 128] = k
            kn[a : a + 128, :] = k.T
            rows = slice(HD, HD + HALF)
            low = joined([piece(x_ref, s, rows, 0, small).astype(F32) for s, small in pieces])
            high = joined([piece(x_ref, s, rows, 1, small).astype(F32) for s, small in pieces])
            v = jnp.concatenate([low, high, ones], axis=0)
            vn_ref[a : a + 128, :] = v.T.astype(BF)

        each_place(put)
        m, _ = score_half(kn, qt[:, 0:cols], sa, None, None, None, chunk, cols)
        ma[...] = jnp.broadcast_to(m, ma.shape)

    def q_block(b):
        return qt[:, pl.ds(pl.multiple_of(b * cols, cols), cols)]

    def emit0(r, v):
        e_ref[r : r + chunk, 0:cols] = v

    def emit1(r, v):
        e_ref[r : r + chunk, cols : 2 * cols] = v

    mb, l0 = score_half(kn, q_block(2 * i + 1), sb, sa, ma[0:1, :], emit0, chunk, cols)
    nxt = jnp.minimum(2 * i + 2, blocks - 1)
    mn, l1 = score_half(kn, q_block(nxt), sa, sb, mb, emit1, chunk, cols)
    ma[...] = jnp.broadcast_to(mn, ma.shape)
    inv_ref[...] = jnp.broadcast_to(1.0 / jnp.concatenate([l0, l1], axis=1), (8, 2 * cols))


def scores(qkv, cols=256, chunk=128):
    return pl.pallas_call(
        functools.partial(scores_body, cols, chunk),
        grid=(N // cols // 2,),
        in_specs=[whole(SRC, HD + HALF, 384)],
        out_specs=[
            pl.BlockSpec((N, 2 * cols), lambda i: (0, i)),
            pl.BlockSpec((8, 2 * cols), lambda i: (0, i)),
            whole(N, HD),
            whole(HD, N),
            whole(N, EXT),
        ],
        out_shape=[
            jax.ShapeDtypeStruct((N, N), BF),
            jax.ShapeDtypeStruct((8, N), F32),
            jax.ShapeDtypeStruct((N, HD), BF),
            jax.ShapeDtypeStruct((HD, N), BF),
            jax.ShapeDtypeStruct((N, EXT), BF),
        ],
        scratch_shapes=[
            pltpu.VMEM((HD, N), BF),
            pltpu.VMEM((N, HD), BF),
            pltpu.VMEM((N, cols), F32),
            pltpu.VMEM((N, cols), F32),
            pltpu.VMEM((8, cols), F32),
        ],
        compiler_params=params(),
        cost_estimate=cost(2 * N * N * HD, 24 * 10**6, N * N),
        name="scores",
    )(qkv)


def grads_block(k0, rows, e_ref, inv_ref, qn_ref, kt_ref, vn, dot_t, dot_n, acc):
    e = e_ref[...]
    dp = dot(vn[pl.ds(k0, rows), :], dot_t[...], 1, 0)
    ds = (e.astype(F32) * dp * inv_ref[0:1, :]).astype(BF)
    dv = dot(e, dot_n[...], 1, 0)
    dk = dot(ds, qn_ref[...], 1, 0) * SCALE
    acc[...] += dot(kt_ref[:, pl.ds(k0, rows)], ds, 1, 0)
    return dv.T.astype(BF), dk.T.astype(BF)


def grads_a_body(rows, x_ref, e_ref, inv_ref, qn_ref, kt_ref, vn_ref, out_ref, dq_ref, dot_t, dot_n):
    i = pl.program_id(0)

    @pl.when(i == 0)
    def _():
        def side(s, small, sl):
            own = piece(x_ref, s, sl, 0, small).astype(F32)
            other = piece(x_ref, s ^ 1, sl, 1, small).astype(F32)
            return own, other

        def put(a, pieces):
            feats = []
            sums = []
            for s, small in pieces:
                own, other = side(s, small, slice(0, 48))
                first, second = (own, other) if s % 2 == 0 else (other, own)
                feats.append(jnp.concatenate([first[:HALF], second[:HALF]], axis=0))
                sums.append(own[HALF:] + jnp.concatenate([jnp.zeros((3, own.shape[1]), F32), other[HALF : HALF + 3], jnp.zeros((2, own.shape[1]), F32)], axis=0))
            f = joined(feats)
            t = joined(sums)
            dot_t[:, a : a + 128] = jnp.concatenate([f, t, jnp.zeros((8, 128), F32)], axis=0).astype(BF)
            dot_n[a : a + 128, :] = (f * inv_ref[0:1, a : a + 128]).T.astype(BF)

        each_place(put)
        dq_ref[...] = jnp.zeros_like(dq_ref)

    k0 = pl.multiple_of(i * rows, 128)
    dv, dk = grads_block(k0, rows, e_ref, inv_ref, qn_ref, kt_ref, vn_ref, dot_t, dot_n, dq_ref)
    for j in range(rows // BIG):
        out_ref[j, 0:HD, 0:BIG] = dv[:, j * BIG : (j + 1) * BIG]
        out_ref[j, 0:HD, BIG : 2 * BIG] = dk[:, j * BIG : (j + 1) * BIG]


def grads_a(dout, e, inv, qn, kt, vn, rows=256):
    return pl.pallas_call(
        functools.partial(grads_a_body, rows),
        grid=(SRC * BIG // rows,),
        in_specs=[
            whole(SRC, 48, 384),
            pl.BlockSpec((rows, N), lambda i: (i, 0)),
            whole(8, N),
            whole(N, HD),
            whole(HD, N),
            whole(N, EXT),
        ],
        out_specs=[
            pl.BlockSpec((rows // BIG, HD + 16, 2 * BIG), lambda i: (i, 0, 0)),
            whole(HD, N),
            whole(EXT, N),
            whole(N, HD),
        ],
        out_shape=[
            jax.ShapeDtypeStruct((SRC, HD + 16, 2 * BIG), BF),
            jax.ShapeDtypeStruct((HD, N), F32),
            jax.ShapeDtypeStruct((EXT, N), BF),
            jax.ShapeDtypeStruct((N, HD), BF),
        ],
        compiler_params=params(),
        cost_estimate=cost(8 * N * SRC * BIG * HD, 18 * 10**6),
        name="grads_a",
    )(dout, e, inv, qn, kt, vn)


def grads_b_body(rows, e_ref, inv_ref, qn_ref, kt_ref, vn_ref, dot_t, dot_n, dq_ref, out_ref, acc):
    i = pl.program_id(0)
    base = SRC * BIG

    @pl.when(i == 0)
    def _():
        acc[...] = dq_ref[...]

    k0 = pl.multiple_of(base + i * rows, 128)
    dv, dk = grads_block(k0, rows, e_ref, inv_ref, qn_ref, kt_ref, vn_ref, dot_t, dot_n, acc)
    for j in range(rows // SMALL):
        a = j * SMALL
        out_ref[i * (rows // SMALL) + j, 0:HD, :] = jnp.concatenate(
            [dv[:, a : a + SMALL], dk[:, a : a + SMALL]], axis=1
        )

    @pl.when(i == pl.num_programs(0) - 1)
    def _():
        for s in range(SRC):
            out_ref[s, HD : 2 * HD, :] = (acc[:, s * BIG : (s + 1) * BIG] * SCALE).astype(BF)
            a = base + s * SMALL
            b = acc[:, a : a + SMALL] * SCALE
            out_ref[s, 2 * HD : 2 * HD + HALF, :] = jnp.concatenate(
                [b[:HALF], b[HALF:]], axis=1
            ).astype(BF)


def grads_b(e, inv, qn, kt, vn, dot_t, dot_n, dq, rows=256):
    off = SRC * BIG // rows
    return pl.pallas_call(
        functools.partial(grads_b_body, rows),
        grid=(SRC * SMALL // rows,),
        in_specs=[
            pl.BlockSpec((rows, N), lambda i: (i + off, 0)),
            whole(8, N),
            whole(N, HD),
            whole(HD, N),
            whole(N, EXT),
            whole(EXT, N),
            whole(N, HD),
            whole(HD, N),
        ],
        out_specs=whole(SRC, 256, 128),
        out_shape=jax.ShapeDtypeStruct((SRC, 256, 128), BF),
        scratch_shapes=[pltpu.VMEM((HD, N), F32)],
        compiler_params=params(),
        cost_estimate=cost(8 * N * SRC * SMALL * HD, 11 * 10**6),
        name="grads_b",
    )(e, inv, qn, kt, vn, dot_t, dot_n, dq)


def unpack_body(a_ref, b_ref, dq_ref, dk_ref, dv_ref, dw_ref):
    def rows(ref, sl, lanes):
        return jnp.concatenate([ref[h, sl, lanes] for h in range(HEADS)], axis=0).T

    dv_ref[0, 0:BIG] = rows(a_ref, slice(0, HD), slice(0, BIG))
    dk_ref[0, 0:BIG] = rows(a_ref, slice(0, HD), slice(BIG, 2 * BIG))
    both = rows(b_ref, slice(0, HD), slice(0, BIG))
    dv_ref[0, BIG:TOK] = both[:SMALL]
    dk_ref[0, BIG:TOK] = both[SMALL:]
    dq_ref[0, 0:BIG] = rows(b_ref, slice(HD, 2 * HD), slice(0, BIG))
    tail = []
    for h in range(HEADS):
        t = b_ref[h, 2 * HD : 2 * HD + HALF, :].astype(F32)
        tail += [t[:, :SMALL], t[:, SMALL:]]
    dq_ref[0, BIG:TOK] = jnp.concatenate(tail, axis=0).T.astype(BF)
    for half in range(2):
        pieces = [b_ref[2 * g + half, 200:256, :].astype(F32) for g in range(8)]
        for c in range(2):
            for j in range(5):
                r = c * 25 + j * 5
                a = half * 640 + j * 128
                dw_ref[c * HALF : (c + 1) * HALF, a : a + 128] = jnp.concatenate(
                    [p[r : r + 5] for p in pieces], axis=0
                )


def unpack(a, b):
    shape = jax.ShapeDtypeStruct((1, TOK, D), BF)
    return pl.pallas_call(
        unpack_body,
        out_shape=[shape] * 3 + [jax.ShapeDtypeStruct((HD, D), F32)],
        compiler_params=params(),
        cost_estimate=cost(0, 3 * 10**6),
        name="unpack",
    )(a, b)


UP = [(i, (i + 1) % 8) for i in range(8)]
DOWN = [(i, (i - 1) % 8) for i in range(8)]


def body(query, keys, values, attn, d_block, w_out):
    c = lax.axis_index("c")
    yl = lax.axis_index("yl")
    z = lax.axis_index("z")
    swap = [(0, 1), (1, 0)]

    def exchange(x):
        return lax.all_to_all(x, SEQ, 0, 0, tiled=True)

    w_half = lax.dynamic_slice_in_dim(w_out, c * HALF, HALF, 0)
    pair = jnp.stack([w_half, lax.ppermute(w_half, "yl", swap)])
    query, keys, values, attn, d_block, pair = lax.optimization_barrier(
        (query, keys, values, attn, d_block, pair)
    )
    def scalar(i):
        return i.reshape(1).astype(jnp.int32)

    def up(block):
        return lax.ppermute(block, "z", UP)

    def down(block):
        return lax.ppermute(block, "z", DOWN)

    hold = lax.optimization_barrier
    g_oth = lax.ppermute(d_block, "c", swap)
    f1, g1, packed = hold((up(pair), down(pair), pack_qkv(query, keys, values)))
    qkv = exchange(packed)
    f2, g2, attn = hold((up(f1), down(g1), attn))
    a_own, a_send = split_attn(scalar(c), attn)
    f3, g3, a_oth, g_oth = hold((up(f2), down(g2), lax.ppermute(a_send, "c", swap), g_oth))
    keep, give, gx, ax = weight_share(scalar(yl), d_block, g_oth, a_own, a_oth)
    came = lax.ppermute(give, "yl", swap)
    blocks = [pair, f1, g1, f2, g2, f3, g3, up(f3)]

    zs = [(z + o) % 8 for o in OFFSETS]
    ids = jnp.stack([y * 8 + k for k in zs for y in (yl, 1 - yl)]).astype(jnp.int32)
    dout, qkv = lax.optimization_barrier((out_grad(ids, blocks, gx, ax), qkv))
    dout = exchange(dout)

    e, inv, qn, kt, vn = scores(qkv)
    both = (keep.astype(F32) + came.astype(F32)).astype(BF)
    both, e = lax.optimization_barrier((both, e))
    part = lax.all_to_all(both, "z", 0, 0, tiled=True)
    first, dq, dot_t, dot_n = grads_a(dout, e, inv, qn, kt, vn)
    first = exchange(lax.dynamic_update_slice(first, sum_z(part), (0, HD, 0)))
    second = grads_b(e, inv, qn, kt, vn, dot_t, dot_n, dq)
    second = exchange(lax.dynamic_update_slice(second, sum_seq(first[:, HD:]), (0, 200, 0)))
    d_query, d_keys, d_values, d_weight = unpack(first, second)
    return d_query, d_keys, d_values, d_weight


def solution(mesh):
    finer = Mesh(mesh.devices.reshape(2, 4, 2, 2, 8), ("yh", "x", "c", "yl", "z"))
    rows = P(DP, SEQ, None)
    weight = P(DP, None)
    return jax.shard_map(
        body,
        mesh=finer,
        in_specs=(rows,) * 5 + (weight,),
        out_specs=(rows,) * 3 + (weight,),
        check_vma=False,
    )
```

time: 371 us -> 175 us (0.47)
  waiting for transfers between devices: 127 us -> 31.1 us
  matrix products: 81.9 us -> 0 us
  Pallas kernels: 0 us -> 64.6 us
  local copies, waits for them, and re-layouts: 60.2 us -> 7.22 us
  other arithmetic: 31.5 us -> 2.31 us
  between operations: 15.4 us -> 0.76 us
  blocking collectives: 11.4 us -> 22 us
  starting transfers between devices: 41.3 us -> 46.1 us
    reduce_scatter x2 -> x0, waiting for transfers between devices: 84.7 us -> none  [reduced_to_own(): blocks = lax.psum_scatter(blocks, axes[k], scatter_dimension=0, tiled=True)]
    dot_general x32 -> x0, matrix products: 81.9 us -> none  [the longest x6 26.2 us: one_block(): lax.dot_general(probs_low, dout_block, contract_first, preferred_element_...]
    pallas_call x0 -> x10, Pallas kernels: none -> 64.6 us  [the longest x1 17.5 us: grads_a(): pl.pallas_call(functools.partial(grads_a_body, rows), grid=(SRC * BIG //...]
    all_to_all x7 -> x4, waiting for transfers between devices: 41.8 us -> 10.5 us  [the longest x1 6.72 us: body(): part = lax.all_to_all(both, 'z', 0, 0, tiled=True)]
    unnamed x35 -> x32, local copies, waits for them, and re-layouts: 28.3 us -> 2.56 us
    ppermute x0 -> x11, waiting for transfers between devices: none -> 20.6 us  [the longest x4 18.6 us: up(): return lax.ppermute(block, 'z', UP)]
    another operation x4 -> x1, other arithmetic: 19 us -> 0.02 us  [body(): pair = jnp.stack([w_half, lax.ppermute(w_half, 'yl', swap)])]
    while x24 -> x0, local copies, waits for them, and re-layouts: 17.7 us -> none
  transfers between devices with their start and end apart: 11 -> 15, of which waited for: 6 -> 7; matrix products, arithmetic and copies ran while one was open for 39% -> 2% of each run, Pallas kernels for 0% -> 33%
where the time goes in v1:
time: 175 us; the launch traced here: 174 us
  Pallas kernels  64.6 us (37%)
  starting transfers between devices  46.1 us (26%)
  waiting for transfers between devices  31.1 us (18%)
  blocking collectives  22 us (13%)
  local copies, waits for them, and re-layouts  7.22 us (4%)
  other arithmetic  2.31 us (1%)
    all_to_all x3, starting transfers between devices, exchange(): return lax.all_to_all(x, SEQ, 0, 0, tiled=True)  27.3 us
    all_to_all x1, blocking collectives, exchange(): return lax.all_to_all(x, SEQ, 0, 0, tiled=True)  22 us
    ppermute x4, waiting for transfers between devices, up(): return lax.ppermute(block, 'z', UP)  18.6 us
    pallas_call x1, Pallas kernels, grads_a(): pl.pallas_call(functools.partial(grads_a_body, rows), grid=(SRC * BIG //...  17.5 us
    pallas_call x1, Pallas kernels, scores(): pl.pallas_call(functools.partial(scores_body, cols, chunk), grid=(N // co...  16 us
    ppermute x3, starting transfers between devices, down(): return lax.ppermute(block, 'z', DOWN)  11.2 us
    pallas_call x1, Pallas kernels, grads_b(): pl.pallas_call(functools.partial(grads_b_body, rows), grid=(SRC * SMALL /...  10.7 us
    all_to_all x1, waiting for transfers between devices, body(): part = lax.all_to_all(both, 'z', 0, 0, tiled=True)  6.72 us
  transfers between devices with their start and end apart: 15, of which 7 were waited for; matrix products, arithmetic and copies ran while one was open for 2% of the time, Pallas kernels for 33%

profile of v1, /device:TPU:1, one launch (start us, length us, event | category | flops | bytes accessed | tf_op | source)
XLA Modules:
  0.0 174.2 jit_solution(13090136276293310263)
XLA Ops:
  1.6 2.2 %collective-permute-start = (bf16[40,1280]{1,0:T(8,128)(2,1)S(1)}, bf16[40,1280]{1,0:T(8,128)(2,1)S(1)}, u32[]{:S(2)}, u32[]{:S(2)}) collective-permute-start(bf16[40,1280]{1,0:T(8,128)(2,1)S(1)} %constant_dynamic-slice_fusion), channel_id=1, source_target_pairs={{0,8},{8,0},{1,9},{9,1},{2,10},{10,2},{3,11},{11,3},{4,12},{12,4},... | collective-permute-start | bytes 307208 | tf_op jit(solution)/shard_map/ppermute | solution.py:489
  5.9 5.8 %collective-permute-start.2 = (bf16[2,40,1280]{2,1,0:T(8,128)(2,1)S(1)}, bf16[2,40,1280]{2,1,0:T(8,128)(2,1)S(1)}, u32[]{:S(2)}, u32[]{:S(2)}) collective-permute-start(bf16[2,40,1280]{2,1,0:T(8,128)(2,1)S(1)} %pad_maximum_fusion.refs_0_), channel_id=1, source_target_pairs={{0,7},{1,0},{2,1},{3,2},{4,3},{5,4},{6,5},{7,6},{8,15},{9,8},{10,9... | collective-permute-start | bytes 614408 | tf_op jit(solution)/shard_map/ppermute | solution.py:500
  11.7 3.2 %pack_qkv.1 = bf16[16,120,384]{2,1,0:T(8,128)(2,1)} custom-call(bf16[1,192,1280]{2,1,0:T(8,128)(2,1)} %q_ref, bf16[1,192,1280]{2,1,0:T(8,128)(2,1)} %k_ref, bf16[1,192,1280]{2,1,0:T(8,128)(2,1)} %v_ref), custom_call_target="tpu_custom_call" | custom-call | bytes 3000000 | tf_op jit(solution)/shard_map/pack_qkv/pallas_call | solution.py:61
  14.9 2.6 %collective-permute-done.1.refs_1_ = bf16[2,40,1280]{2,1,0:T(8,128)(2,1)S(1)} collective-permute-done((bf16[2,40,1280]{2,1,0:T(8,128)(2,1)S(1)}, bf16[2,40,1280]{2,1,0:T(8,128)(2,1)S(1)}, u32[]{:S(2)}, u32[]{:S(2)}) %collective-permute-start.1) | collective-permute-done | bytes 204832 | tf_op jit(solution)/shard_map/ppermute | solution.py:497
  17.5 10.2 %all-to-all-start = ((bf16[16,120,384]{2,1,0:T(8,128)(2,1)}), bf16[16,120,384]{2,1,0:T(8,128)(2,1)S(1)}, u32[]{:S(2)}, u32[]{:S(2)}) async-start(bf16[16,120,384]{2,1,0:T(8,128)(2,1)} %pack_qkv.1), calls=%async_computation | async-start | bytes 2949120 | tf_op jit(solution)/shard_map/all_to_all | solution.py:486
  27.9 2.7 %collective-permute-start.4 = (bf16[2,40,1280]{2,1,0:T(8,128)(2,1)S(1)}, bf16[2,40,1280]{2,1,0:T(8,128)(2,1)S(1)}, u32[]{:S(2)}, u32[]{:S(2)}) collective-permute-start(bf16[2,40,1280]{2,1,0:T(8,128)(2,1)S(1)} %collective-permute-done.2.refs_2_), channel_id=1, source_target_pairs={{0,7},{1,0},{2,1},{3,2},{4,3},{5,4},{6,5},{7,6},{8,15},{9,8},{10,9... | collective-permute-start | bytes 614408 | tf_op jit(solution)/shard_map/ppermute | solution.py:500
  30.6 4.8 %collective-permute-done.3.refs_3_ = bf16[2,40,1280]{2,1,0:T(8,128)(2,1)S(1)} collective-permute-done((bf16[2,40,1280]{2,1,0:T(8,128)(2,1)S(1)}, bf16[2,40,1280]{2,1,0:T(8,128)(2,1)S(1)}, u32[]{:S(2)}, u32[]{:S(2)}) %collective-permute-start.3) | collective-permute-done | bytes 204832 | tf_op jit(solution)/shard_map/ppermute | solution.py:497
  35.4 2.3 %split_attn.1 = (bf16[16,40,192]{2,1,0:T(8,128)(2,1)}, bf16[16,40,192]{2,1,0:T(8,128)(2,1)}) custom-call(s32[1]{0:T(128)} %bitcast.18.c_ref, bf16[1,192,1280]{2,1,0:T(8,128)(2,1)} %a_ref), custom_call_target="tpu_custom_call" | custom-call | bytes 1000000 | tf_op jit(solution)/shard_map/split_attn/pallas_call | solution.py:83
  38.9 2.7 %collective-permute-start.6 = (bf16[2,40,1280]{2,1,0:T(8,128)(2,1)S(1)}, bf16[2,40,1280]{2,1,0:T(8,128)(2,1)S(1)}, u32[]{:S(2)}, u32[]{:S(2)}) collective-permute-start(bf16[2,40,1280]{2,1,0:T(8,128)(2,1)S(1)} %collective-permute-done.4.refs_4_), channel_id=1, source_target_pairs={{0,7},{1,0},{2,1},{3,2},{4,3},{5,4},{6,5},{7,6},{8,15},{9,8},{10,9... | collective-permute-start | bytes 614408 | tf_op jit(solution)/shard_map/ppermute | solution.py:500
  41.6 5.2 %collective-permute-done.5.refs_5_ = bf16[2,40,1280]{2,1,0:T(8,128)(2,1)S(1)} collective-permute-done((bf16[2,40,1280]{2,1,0:T(8,128)(2,1)S(1)}, bf16[2,40,1280]{2,1,0:T(8,128)(2,1)S(1)}, u32[]{:S(2)}, u32[]{:S(2)}) %collective-permute-start.5) | collective-permute-done | bytes 204832 | tf_op jit(solution)/shard_map/ppermute | solution.py:497
  46.8 4.3 %weight_share.1 = (bf16[8,40,1280]{2,1,0:T(8,128)(2,1)}, bf16[8,40,1280]{2,1,0:T(8,128)(2,1)}, bf16[384,1280]{1,0:T(8,128)(2,1)}, bf16[16,40,384]{2,1,0:T(8,128)(2,1)}) custom-call(s32[1]{0:T(128)} %bitcast.19.y_ref, bf16[1,192,1280]{2,1,0:T(8,128)(2,1)} %g_own, bf16[1,192,1280]{2,1,0:T(8,128)(2,1)} %copy-done.15, ...), custom_call_target="tpu_custom_call" | custom-call | flops 629145600 | bytes 6000000 | tf_op jit(solution)/shard_map/weight_share/pallas_call | solution.py:114
  52.1 6.0 %collective-permute-done.9.refs_7_ = bf16[2,40,1280]{2,1,0:T(8,128)(2,1)S(1)} collective-permute-done((bf16[2,40,1280]{2,1,0:T(8,128)(2,1)S(1)}, bf16[2,40,1280]{2,1,0:T(8,128)(2,1)S(1)}, u32[]{:S(2)}, u32[]{:S(2)}) %collective-permute-start.9) | collective-permute-done | bytes 204832 | tf_op jit(solution)/shard_map/ppermute | solution.py:497
  58.8 4.0 %out_grad.1 = bf16[16,48,384]{2,1,0:T(8,128)(2,1)} custom-call(s32[16]{0:T(128)} %stack.76.ids, bf16[2,40,1280]{2,1,0:T(8,128)(2,1)} %copy-done.6, bf16[2,40,1280]{2,1,0:T(8,128)(2,1)} %copy-done.8, bf16[2,40,1280]{2,1,0:T(8,128)(2,1)} %copy-done.7, bf16[2,40,1280]{2,1,0:T(8,128)(2,1)} %copy-done.9, bf16[2,40,1280]{2,1,0:T(8,128)(2,1)} %copy-done.10, ...), custom_call_target="tpu_custom_call" | custom-call | flops 629145600 | bytes 4000000 | tf_op jit(solution)/shard_map/out_grad/pallas_call | solution.py:196
  62.8 9.8 %all-to-all-start.1 = ((bf16[16,48,384]{2,1,0:T(8,128)(2,1)}), bf16[16,48,384]{2,1,0:T(8,128)(2,1)S(1)}, u32[]{:S(2)}, u32[]{:S(2)}) async-start(bf16[16,48,384]{2,1,0:T(8,128)(2,1)} %out_grad.1), calls=%async_computation.1 | async-start | bytes 1179648 | tf_op jit(solution)/shard_map/all_to_all | solution.py:486
  72.6 2.3 %add_convert_fusion = bf16[8,40,1280]{2,1,0:T(8,128)(2,1)} fusion(bf16[8,40,1280]{2,1,0:T(8,128)(2,1)} %collective-permute-done.10, bf16[8,40,1280]{2,1,0:T(8,128)(2,1)S(1)} %copy-done.5), kind=kLoop, calls=%fused_computation | loop fusion | flops 1638400 | bytes 2457600 | tf_op jit(solution)/shard_map/convert_element_type | solution.py:519
  74.9 16.0 %scores.1 = (bf16[3072,3072]{1,0:T(8,128)(2,1)}, f32[8,3072]{1,0:T(8,128)}, bf16[3072,80]{1,0:T(8,128)(2,1)}, bf16[80,3072]{1,0:T(8,128)(2,1)}, bf16[3072,96]{1,0:T(8,128)(2,1)}) custom-call(bf16[16,120,384]{2,1,0:T(8,128)(2,1)} %copy-done.4), custom_call_target="tpu_custom_call" | custom-call | flops 1509949440 | bytes 24000000 | tf_op jit(solution)/shard_map/scores/pallas_call | solution.py:283
  90.9 3.6 %all-to-all-start.2 = ((bf16[8,40,1280]{2,1,0:T(8,128)(2,1)}), bf16[8,40,1280]{2,1,0:T(8,128)(2,1)S(1)}, u32[]{:S(2)}, u32[]{:S(2)}) async-start(bf16[8,40,1280]{2,1,0:T(8,128)(2,1)} %add_convert_fusion), calls=%async_computation.2 | async-start | bytes 1638400 | tf_op jit(solution)/shard_map/all_to_all | solution.py:521
  94.5 17.5 %grads_a.1 = (bf16[16,96,256]{2,1,0:T(8,128)(2,1)}, f32[80,3072]{1,0:T(8,128)}, bf16[96,3072]{1,0:T(8,128)(2,1)}, bf16[3072,80]{1,0:T(8,128)(2,1)}) custom-call(bf16[16,48,384]{2,1,0:T(8,128)(2,1)} %copy-done.3, bf16[3072,3072]{1,0:T(8,128)(2,1)} %get-tuple-element.64.e_ref, f32[8,3072]{1,0:T(8,128)} %get-tuple-element.65.inv_ref, ...), custom_call_target="tpu_custom_call" | custom-call | flops 4026531840 | bytes 18000000 | tf_op jit(solution)/shard_map/grads_a/pallas_call | solution.py:358
  112.0 6.7 %all-to-all-done.2.x_ref = bf16[8,40,1280]{2,1,0:T(8,128)(2,1)S(1)} async-done(((bf16[8,40,1280]{2,1,0:T(8,128)(2,1)}), bf16[8,40,1280]{2,1,0:T(8,128)(2,1)S(1)}, u32[]{:S(2)}, u32[]{:S(2)}) %all-to-all-start.2) | async-done | bytes 819232 | tf_op jit(solution)/shard_map/all_to_all | solution.py:521
  123.2 7.3 %all-to-all-start.3 = ((bf16[16,96,256]{2,1,0:T(8,128)(2,1)}), bf16[16,96,256]{2,1,0:T(8,128)(2,1)S(1)}, u32[]{:S(2)}, u32[]{:S(2)}) async-start(bf16[16,96,256]{2,1,0:T(8,128)(2,1)} %constant_dynamic-update-slice_fusion.1), calls=%async_computation.3 | async-start | bytes 1572864 | tf_op jit(solution)/shard_map/all_to_all | solution.py:486
  130.5 10.7 %grads_b.1 = bf16[16,256,128]{2,1,0:T(8,128)(2,1)} custom-call(bf16[3072,3072]{1,0:T(8,128)(2,1)} %get-tuple-element.64.e_ref, f32[8,3072]{1,0:T(8,128)} %get-tuple-element.65.inv_ref, bf16[3072,80]{1,0:T(8,128)(2,1)} %get-tuple-element.66.qn_ref, bf16[80,3072]{1,0:T(8,128)(2,1)} %get-tuple-element.67.kt_ref, bf16[3072,96]{1,0:T(8,128)(2,1)} %get-tuple-element.68.vn_ref, ...), custom_call_target="tpu_custom_call" | custom-call | flops 2013265920 | bytes 11000000 | tf_op jit(solution)/shard_map/grads_b/pallas_call | solution.py:416
  141.2 3.8 %all-to-all-done.3.a_ref = bf16[16,96,256]{2,1,0:T(8,128)(2,1)S(1)} async-done(((bf16[16,96,256]{2,1,0:T(8,128)(2,1)}), bf16[16,96,256]{2,1,0:T(8,128)(2,1)S(1)}, u32[]{:S(2)}, u32[]{:S(2)}) %all-to-all-start.3) | async-done | bytes 786464 | tf_op jit(solution)/shard_map/all_to_all | solution.py:486
  149.1 22.0 %all_to_all.25.b_ref = bf16[16,256,128]{2,1,0:T(8,128)(2,1)} all-to-all(bf16[16,256,128]{2,1,0:T(8,128)(2,1)} %constant_dynamic-update-slice_fusion), channel_id=1, replica_groups=mesh['yh'=2,'x'=4,'c'=2,'yl'=2,'z'=8] {'yh','x','c'}, dimensions={0} | all-to-all | bytes 2097152 | tf_op jit(solution)/shard_map/all_to_all | solution.py:486
  171.1 3.1 %unpack.1 = (bf16[1,192,1280]{2,1,0:T(8,128)(2,1)}, bf16[1,192,1280]{2,1,0:T(8,128)(2,1)}, bf16[1,192,1280]{2,1,0:T(8,128)(2,1)}, f32[80,1280]{1,0:T(8,128)}) custom-call(bf16[16,96,256]{2,1,0:T(8,128)(2,1)} %copy-done.1, bf16[16,256,128]{2,1,0:T(8,128)(2,1)} %all_to_all.25.b_ref), custom_call_target="tpu_custom_call" | custom-call | bytes 3000000 | tf_op jit(solution)/shard_map/unpack/pallas_call | solution.py:466
  (57 shorter events, 14.7 us)
Async XLA Ops:
  1.6 4.3 %collective-permute-start = (bf16[40,1280]{1,0:T(8,128)(2,1)S(1)}, bf16[40,1280]{1,0:T(8,128)(2,1)S(1)}, u32[]{:S(2)}, u32[]{:S(2)}) collective-permute-start(bf16[40,1280]{1,0:T(8,128)(2,1)S(1)} %constant_dynamic-slice_fusion), channel_id=1, source_target_pairs={{0,8},{8,0},{1,9},{9,1},{2,10},{10,2},{3,11},{11,3},{4,12},{12,4},... | collective-permute-start | bytes 307208 | tf_op jit(solution)/shard_map/ppermute | solution.py:489
  5.9 9.0 %collective-permute-start.2 = (bf16[2,40,1280]{2,1,0:T(8,128)(2,1)S(1)}, bf16[2,40,1280]{2,1,0:T(8,128)(2,1)S(1)}, u32[]{:S(2)}, u32[]{:S(2)}) collective-permute-start(bf16[2,40,1280]{2,1,0:T(8,128)(2,1)S(1)} %pad_maximum_fusion.refs_0_), channel_id=1, source_target_pairs={{0,7},{1,0},{2,1},{3,2},{4,3},{5,4},{6,5},{7,6},{8,15},{9,8},{10,9... | collective-permute-start | bytes 614408 | tf_op jit(solution)/shard_map/ppermute | solution.py:500
  11.7 5.8 %collective-permute-start.1 = (bf16[2,40,1280]{2,1,0:T(8,128)(2,1)S(1)}, bf16[2,40,1280]{2,1,0:T(8,128)(2,1)S(1)}, u32[]{:S(2)}, u32[]{:S(2)}) collective-permute-start(bf16[2,40,1280]{2,1,0:T(8,128)(2,1)S(1)} %pad_maximum_fusion.refs_0_), channel_id=1, source_target_pairs={{0,1},{1,2},{2,3},{3,4},{4,5},{5,6},{6,7},{7,0},{8,9},{9,10},{10,1... | collective-permute-start | bytes 614408 | tf_op jit(solution)/shard_map/ppermute | solution.py:497
  14.9 12.8 %copy-start.14 = (bf16[1,192,1280]{2,1,0:T(8,128)(2,1)S(1)}, bf16[1,192,1280]{2,1,0:T(8,128)(2,1)}, u32[]{:S(2)}) copy-start(bf16[1,192,1280]{2,1,0:T(8,128)(2,1)} %g_own) | copy-start | bytes 1474564
  14.9 22.8 %copy-start.7 = (bf16[2,40,1280]{2,1,0:T(8,128)(2,1)}, bf16[2,40,1280]{2,1,0:T(8,128)(2,1)S(1)}, u32[]{:S(2)}) copy-start(bf16[2,40,1280]{2,1,0:T(8,128)(2,1)S(1)} %collective-permute-done.2.refs_2_) | copy-start | bytes 614404
  17.5 20.2 %copy-start.8 = (bf16[2,40,1280]{2,1,0:T(8,128)(2,1)}, bf16[2,40,1280]{2,1,0:T(8,128)(2,1)S(1)}, u32[]{:S(2)}) copy-start(bf16[2,40,1280]{2,1,0:T(8,128)(2,1)S(1)} %collective-permute-done.1.refs_1_) | copy-start | bytes 614404
  17.5 45.3 %all-to-all-start = ((bf16[16,120,384]{2,1,0:T(8,128)(2,1)}), bf16[16,120,384]{2,1,0:T(8,128)(2,1)S(1)}, u32[]{:S(2)}, u32[]{:S(2)}) async-start(bf16[16,120,384]{2,1,0:T(8,128)(2,1)} %pack_qkv.1), calls=%async_computation | async-start | bytes 2949120 | tf_op jit(solution)/shard_map/all_to_all | solution.py:486
  27.7 13.9 %collective-permute-start.8 = (bf16[1,192,1280]{2,1,0:T(8,128)(2,1)S(1)}, bf16[1,192,1280]{2,1,0:T(8,128)(2,1)S(1)}, u32[]{:S(2)}, u32[]{:S(2)}) collective-permute-start(bf16[1,192,1280]{2,1,0:T(8,128)(2,1)S(1)} %copy-done.14), channel_id=1, source_target_pairs={{0,16},{16,0},{1,17},{17,1},{2,18},{18,2},{3,19},{19,3},{4,20},{20... | collective-permute-start | bytes 1474568 | tf_op jit(solution)/shard_map/ppermute | solution.py:503
  27.9 7.5 %collective-permute-start.3 = (bf16[2,40,1280]{2,1,0:T(8,128)(2,1)S(1)}, bf16[2,40,1280]{2,1,0:T(8,128)(2,1)S(1)}, u32[]{:S(2)}, u32[]{:S(2)}) collective-permute-start(bf16[2,40,1280]{2,1,0:T(8,128)(2,1)S(1)} %collective-permute-done.1.refs_1_), channel_id=1, source_target_pairs={{0,1},{1,2},{2,3},{3,4},{4,5},{5,6},{6,7},{7,0},{8,9},{9,10},{10,1... | collective-permute-start | bytes 614408 | tf_op jit(solution)/shard_map/ppermute | solution.py:497
  27.9 7.5 %collective-permute-start.4 = (bf16[2,40,1280]{2,1,0:T(8,128)(2,1)S(1)}, bf16[2,40,1280]{2,1,0:T(8,128)(2,1)S(1)}, u32[]{:S(2)}, u32[]{:S(2)}) collective-permute-start(bf16[2,40,1280]{2,1,0:T(8,128)(2,1)S(1)} %collective-permute-done.2.refs_2_), channel_id=1, source_target_pairs={{0,7},{1,0},{2,1},{3,2},{4,3},{5,4},{6,5},{7,6},{8,15},{9,8},{10,9... | collective-permute-start | bytes 614408 | tf_op jit(solution)/shard_map/ppermute | solution.py:500
  35.4 23.4 %copy-start.9 = (bf16[2,40,1280]{2,1,0:T(8,128)(2,1)}, bf16[2,40,1280]{2,1,0:T(8,128)(2,1)S(1)}, u32[]{:S(2)}) copy-start(bf16[2,40,1280]{2,1,0:T(8,128)(2,1)S(1)} %collective-permute-done.3.refs_3_) | copy-start | bytes 614404
  35.4 23.4 %copy-start.10 = (bf16[2,40,1280]{2,1,0:T(8,128)(2,1)}, bf16[2,40,1280]{2,1,0:T(8,128)(2,1)S(1)}, u32[]{:S(2)}) copy-start(bf16[2,40,1280]{2,1,0:T(8,128)(2,1)S(1)} %collective-permute-done.4.refs_4_) | copy-start | bytes 614404
  37.7 9.1 %collective-permute-start.7 = (bf16[16,40,192]{2,1,0:T(8,128)(2,1)}, bf16[16,40,192]{2,1,0:T(8,128)(2,1)}, u32[]{:S(2)}, u32[]{:S(2)}) collective-permute-start(bf16[16,40,192]{2,1,0:T(8,128)(2,1)} %get-tuple-element.49), channel_id=1, source_target_pairs={{0,16},{16,0},{1,17},{17,1},{2,18},{18,2},{3,19},{19,3},{4,20},{20... | collective-permute-start | bytes 737288 | tf_op jit(solution)/shard_map/ppermute | solution.py:508
  38.9 7.9 %collective-permute-start.5 = (bf16[2,40,1280]{2,1,0:T(8,128)(2,1)S(1)}, bf16[2,40,1280]{2,1,0:T(8,128)(2,1)S(1)}, u32[]{:S(2)}, u32[]{:S(2)}) collective-permute-start(bf16[2,40,1280]{2,1,0:T(8,128)(2,1)S(1)} %collective-permute-done.3.refs_3_), channel_id=1, source_target_pairs={{0,1},{1,2},{2,3},{3,4},{4,5},{5,6},{6,7},{7,0},{8,9},{9,10},{10,1... | collective-permute-start | bytes 614408 | tf_op jit(solution)/shard_map/ppermute | solution.py:497
  38.9 7.9 %collective-permute-start.6 = (bf16[2,40,1280]{2,1,0:T(8,128)(2,1)S(1)}, bf16[2,40,1280]{2,1,0:T(8,128)(2,1)S(1)}, u32[]{:S(2)}, u32[]{:S(2)}) collective-permute-start(bf16[2,40,1280]{2,1,0:T(8,128)(2,1)S(1)} %collective-permute-done.4.refs_4_), channel_id=1, source_target_pairs={{0,7},{1,0},{2,1},{3,2},{4,3},{5,4},{6,5},{7,6},{8,15},{9,8},{10,9... | collective-permute-start | bytes 614408 | tf_op jit(solution)/shard_map/ppermute | solution.py:500
  46.8 12.1 %copy-start.11 = (bf16[2,40,1280]{2,1,0:T(8,128)(2,1)}, bf16[2,40,1280]{2,1,0:T(8,128)(2,1)S(1)}, u32[]{:S(2)}) copy-start(bf16[2,40,1280]{2,1,0:T(8,128)(2,1)S(1)} %collective-permute-done.5.refs_5_) | copy-start | bytes 614404
  51.1 21.5 %collective-permute-start.10 = (bf16[8,40,1280]{2,1,0:T(8,128)(2,1)}, bf16[8,40,1280]{2,1,0:T(8,128)(2,1)}, u32[]{:S(2)}, u32[]{:S(2)}) collective-permute-start(bf16[8,40,1280]{2,1,0:T(8,128)(2,1)} %get-tuple-element.61), channel_id=1, source_target_pairs={{0,8},{8,0},{1,9},{9,1},{2,10},{10,2},{3,11},{11,3},{4,12},{12,4},... | collective-permute-start | bytes 2457608 | tf_op jit(solution)/shard_map/ppermute | solution.py:510
  51.5 6.6 %collective-permute-start.9 = (bf16[2,40,1280]{2,1,0:T(8,128)(2,1)S(1)}, bf16[2,40,1280]{2,1,0:T(8,128)(2,1)S(1)}, u32[]{:S(2)}, u32[]{:S(2)}) collective-permute-start(bf16[2,40,1280]{2,1,0:T(8,128)(2,1)S(1)} %collective-permute-done.5.refs_5_), channel_id=1, source_target_pairs={{0,1},{1,2},{2,3},{3,4},{4,5},{5,6},{6,7},{7,0},{8,9},{9,10},{10,1... | collective-permute-start | bytes 614408 | tf_op jit(solution)/shard_map/ppermute | solution.py:497
  58.8 13.8 %copy-start.5 = (bf16[8,40,1280]{2,1,0:T(8,128)(2,1)S(1)}, bf16[8,40,1280]{2,1,0:T(8,128)(2,1)}, u32[]{:S(2)}) copy-start(bf16[8,40,1280]{2,1,0:T(8,128)(2,1)} %get-tuple-element.60) | copy-start | bytes 2457604
  62.8 12.1 %copy-start.4 = (bf16[16,120,384]{2,1,0:T(8,128)(2,1)}, bf16[16,120,384]{2,1,0:T(8,128)(2,1)S(1)}, u32[]{:S(2)}) copy-start(bf16[16,120,384]{2,1,0:T(8,128)(2,1)S(1)} %all-to-all-done.x_ref) | copy-start | bytes 4423684
  62.8 28.1 %all-to-all-start.1 = ((bf16[16,48,384]{2,1,0:T(8,128)(2,1)}), bf16[16,48,384]{2,1,0:T(8,128)(2,1)S(1)}, u32[]{:S(2)}, u32[]{:S(2)}) async-start(bf16[16,48,384]{2,1,0:T(8,128)(2,1)} %out_grad.1), calls=%async_computation.1 | async-start | bytes 1179648 | tf_op jit(solution)/shard_map/all_to_all | solution.py:486
  90.9 27.8 %all-to-all-start.2 = ((bf16[8,40,1280]{2,1,0:T(8,128)(2,1)}), bf16[8,40,1280]{2,1,0:T(8,128)(2,1)S(1)}, u32[]{:S(2)}, u32[]{:S(2)}) async-start(bf16[8,40,1280]{2,1,0:T(8,128)(2,1)} %add_convert_fusion), calls=%async_computation.2 | async-start | bytes 1638400 | tf_op jit(solution)/shard_map/all_to_all | solution.py:521
  123.2 21.8 %all-to-all-start.3 = ((bf16[16,96,256]{2,1,0:T(8,128)(2,1)}), bf16[16,96,256]{2,1,0:T(8,128)(2,1)S(1)}, u32[]{:S(2)}, u32[]{:S(2)}) async-start(bf16[16,96,256]{2,1,0:T(8,128)(2,1)} %constant_dynamic-update-slice_fusion.1), calls=%async_computation.3 | async-start | bytes 1572864 | tf_op jit(solution)/shard_map/all_to_all | solution.py:486
  145.0 26.1 %copy-start.1 = (bf16[16,96,256]{2,1,0:T(8,128)(2,1)}, bf16[16,96,256]{2,1,0:T(8,128)(2,1)S(1)}, u32[]{:S(2)}) copy-start(bf16[16,96,256]{2,1,0:T(8,128)(2,1)S(1)} %all-to-all-done.3.a_ref) | copy-start | bytes 2359300
  (7 other events, 35.0 us)

commit v2 on v1

--- a/solution.py
+++ b/solution.py
@@ -128,52 +128,6 @@
     )(y, g_own, g_oth, a_own, a_oth)
 
 
-def sum_z_body(x_ref, out_ref):
-    t = x_ref[0].astype(F32)
-    for k in range(1, 8):
-        t = t + x_ref[k].astype(F32)
-    pad = jnp.zeros((7, 128), F32)
-    for g in range(8):
-        rows = t[5 * g : 5 * g + 5]
-        for half in range(2):
-            a = half * 640
-            p = jnp.concatenate([rows[:, a + 128 * j : a + 128 * j + 128] for j in range(5)] + [pad], axis=0)
-            out_ref[2 * g + half] = jnp.concatenate([p[:16], p[16:]], axis=1).astype(BF)
-
-
-def sum_z(x):
-    return pl.pallas_call(
-        sum_z_body,
-        out_shape=jax.ShapeDtypeStruct((SRC, 16, 256), BF),
-        compiler_params=params(),
-        cost_estimate=cost(0, 10**6),
-        name="sum_z",
-    )(x)
-
-
-def sum_seq_body(x_ref, out_ref):
-    halves = []
-    for c in range(2):
-        t = x_ref[c].astype(F32)
-        for k in range(1, 8):
-            t = t + x_ref[2 * k + c].astype(F32)
-        halves.append(jnp.concatenate([t[:, :128], t[:9, 128:]], axis=0))
-    t = jnp.concatenate(halves + [jnp.zeros((6, 128), F32)], axis=0) * (1.0 / float(16 * N) ** 0.5)
-    low = t.astype(BF)
-    for s in range(SRC):
-        out_ref[s] = low
-
-
-def sum_seq(x):
-    return pl.pallas_call(
-        sum_seq_body,
-        out_shape=jax.ShapeDtypeStruct((SRC, 56, 128), BF),
-        compiler_params=params(),
-        cost_estimate=cost(0, 10**6),
-        name="sum_seq",
-    )(x)
-
-
 def out_grad_body(ids, *refs):
     w_refs, (gx_ref, ax_ref, out_ref, w, acc) = refs[:8], refs[8:]
     for r in range(8):
@@ -238,33 +192,51 @@
     return jnp.max(m, axis=0, keepdims=True), jnp.sum(total, axis=0, keepdims=True)
 
 
-def scores_body(cols, chunk, x_ref, e_ref, inv_ref, qn_ref, kt_ref, vn_ref, qt, kn, sa, sb, ma):
+def prepare_body(x_ref, qt_ref, kn_ref, qn_ref, kt_ref, vn_ref):
+    ones = jnp.concatenate([jnp.ones((8, 128), F32), jnp.zeros((8, 128), F32)], axis=0)
+
+    def put(a, pieces):
+        q = joined([piece(x_ref, s, slice(0, HD), 0, small) for s, small in pieces])
+        k = joined([piece(x_ref, s, slice(0, HD), 1, small) for s, small in pieces])
+        qt_ref[:, a : a + 128] = q
+        qn_ref[a : a + 128, :] = q.T
+        kt_ref[:, a : a + 128] = k
+        kn_ref[a : a + 128, :] = k.T
+        rows = slice(HD, HD + HALF)
+        low = joined([piece(x_ref, s, rows, 0, small).astype(F32) for s, small in pieces])
+        high = joined([piece(x_ref, s, rows, 1, small).astype(F32) for s, small in pieces])
+        v = jnp.concatenate([low, high, ones], axis=0)
+        vn_ref[a : a + 128, :] = v.T.astype(BF)
+
+    each_place(put)
+
+
+def prepare(qkv):
+    return pl.pallas_call(
+        prepare_body,
+        out_shape=[
+            jax.ShapeDtypeStruct((HD, N), BF),
+            jax.ShapeDtypeStruct((N, HD), BF),
+            jax.ShapeDtypeStruct((N, HD), BF),
+            jax.ShapeDtypeStruct((HD, N), BF),
+            jax.ShapeDtypeStruct((N, EXT), BF),
+        ],
+        compiler_params=params(),
+        cost_estimate=cost(0, 5 * 10**6),
+        name="prepare",
+    )(qkv)
+
+
+def scores_body(cols, chunk, begin, end, qt, kn, e_ref, inv_ref, sa, sb, ma):
     i = pl.program_id(0)
-    blocks = N // cols
 
     @pl.when(i == 0)
     def _():
-        ones = jnp.concatenate([jnp.ones((8, 128), F32), jnp.zeros((8, 128), F32)], axis=0)
-
-        def put(a, pieces):
-            q = joined([piece(x_ref, s, slice(0, HD), 0, small) for s, small in pieces])
-            k = joined([piece(x_ref, s, slice(0, HD), 1, small) for s, small in pieces])
-            qt[:, a : a + 128] = q
-            qn_ref[a : a + 128, :] = q.T
-            kt_ref[:, a : a + 128] = k
-            kn[a : a + 128, :] = k.T
-            rows = slice(HD, HD + HALF)
-            low = joined([piece(x_ref, s, rows, 0, small).astype(F32) for s, small in pieces])
-            high = joined([piece(x_ref, s, rows, 1, small).astype(F32) for s, small in pieces])
-            v = jnp.concatenate([low, high, ones], axis=0)
-            vn_ref[a : a + 128, :] = v.T.astype(BF)
-
-        each_place(put)
-        m, _ = score_half(kn, qt[:, 0:cols], sa, None, None, None, chunk, cols)
+        m, _ = score_half(kn, qt[:, begin : begin + cols], sa, None, None, None, chunk, cols)
         ma[...] = jnp.broadcast_to(m, ma.shape)
 
     def q_block(b):
-        return qt[:, pl.ds(pl.multiple_of(b * cols, cols), cols)]
+        return qt[:, pl.ds(pl.multiple_of(begin + b * cols, cols), cols)]
 
     def emit0(r, v):
         e_ref[r : r + chunk, 0:cols] = v
@@ -273,55 +245,57 @@
         e_ref[r : r + chunk, cols : 2 * cols] = v
 
     mb, l0 = score_half(kn, q_block(2 * i + 1), sb, sa, ma[0:1, :], emit0, chunk, cols)
-    nxt = jnp.minimum(2 * i + 2, blocks - 1)
+    nxt = jnp.minimum(2 * i + 2, (end - begin) // cols - 1)
     mn, l1 = score_half(kn, q_block(nxt), sa, sb, mb, emit1, chunk, cols)
     ma[...] = jnp.broadcast_to(mn, ma.shape)
     inv_ref[...] = jnp.broadcast_to(1.0 / jnp.concatenate([l0, l1], axis=1), (8, 2 * cols))
 
 
-def scores(qkv, cols=256, chunk=128):
-    return pl.pallas_call(
-        functools.partial(scores_body, cols, chunk),
-        grid=(N // cols // 2,),
-        in_specs=[whole(SRC, HD + HALF, 384)],
+def scores(qt, kn, begin, end, cols=256, chunk=128):
+    size = end - begin
+    return pl.pallas_call(
+        functools.partial(scores_body, cols, chunk, begin, end),
+        grid=(size // cols // 2,),
+        in_specs=[whole(HD, N), whole(N, HD)],
         out_specs=[
             pl.BlockSpec((N, 2 * cols), lambda i: (0, i)),
             pl.BlockSpec((8, 2 * cols), lambda i: (0, i)),
-            whole(N, HD),
-            whole(HD, N),
-            whole(N, EXT),
         ],
         out_shape=[
-            jax.ShapeDtypeStruct((N, N), BF),
-            jax.ShapeDtypeStruct((8, N), F32),
-            jax.ShapeDtypeStruct((N, HD), BF),
-            jax.ShapeDtypeStruct((HD, N), BF),
-            jax.ShapeDtypeStruct((N, EXT), BF),
+            jax.ShapeDtypeStruct((N, size), BF),
+            jax.ShapeDtypeStruct((8, size), F32),
         ],
         scratch_shapes=[
-            pltpu.VMEM((HD, N), BF),
-            pltpu.VMEM((N, HD), BF),
             pltpu.VMEM((N, cols), F32),
             pltpu.VMEM((N, cols), F32),
             pltpu.VMEM((8, cols), F32),
         ],
         compiler_params=params(),
-        cost_estimate=cost(2 * N * N * HD, 24 * 10**6, N * N),
+        cost_estimate=cost(2 * N * size * HD, 6 * size * N // 3, N * size),
         name="scores",
-    )(qkv)
-
-
-def grads_block(k0, rows, e_ref, inv_ref, qn_ref, kt_ref, vn, dot_t, dot_n, acc):
-    e = e_ref[...]
-    dp = dot(vn[pl.ds(k0, rows), :], dot_t[...], 1, 0)
-    ds = (e.astype(F32) * dp * inv_ref[0:1, :]).astype(BF)
-    dv = dot(e, dot_n[...], 1, 0)
-    dk = dot(ds, qn_ref[...], 1, 0) * SCALE
-    acc[...] += dot(kt_ref[:, pl.ds(k0, rows)], ds, 1, 0)
-    return dv.T.astype(BF), dk.T.astype(BF)
-
-
-def grads_a_body(rows, x_ref, e_ref, inv_ref, qn_ref, kt_ref, vn_ref, out_ref, dq_ref, dot_t, dot_n):
+    )(qt, kn)
+
+
+CUT = 2048
+
+
+def grads_block(k0, rows, e1, e2, inv1, inv2, qn, kt, vn, dot_t, dot_n, acc):
+    v = vn[pl.ds(k0, rows), :]
+    k = kt[:, pl.ds(k0, rows)]
+    dv = dk = None
+    for sl, e_ref, inv in ((slice(0, CUT), e1, inv1), (slice(CUT, N), e2, inv2)):
+        e = e_ref[...]
+        dp = dot(v, dot_t[:, sl], 1, 0)
+        ds = (e.astype(F32) * dp * inv[0:1, :]).astype(BF)
+        v_part = dot(e, dot_n[sl, :], 1, 0)
+        k_part = dot(ds, qn[sl, :], 1, 0)
+        dv = v_part if dv is None else dv + v_part
+        dk = k_part if dk is None else dk + k_part
+        acc[:, sl] += dot(k, ds, 1, 0)
+    return dv.T.astype(BF), (dk * SCALE).T.astype(BF)
+
+
+def grads_a_body(rows, x_ref, e1, e2, inv1, inv2, qn_ref, kt_ref, vn_ref, out_ref, dq_ref, dot_t, dot_n):
     i = pl.program_id(0)
 
     @pl.when(i == 0)
@@ -342,38 +316,43 @@
             f = joined(feats)
             t = joined(sums)
             dot_t[:, a : a + 128] = jnp.concatenate([f, t, jnp.zeros((8, 128), F32)], axis=0).astype(BF)
-            dot_n[a : a + 128, :] = (f * inv_ref[0:1, a : a + 128]).T.astype(BF)
+            inv = inv1[0:1, a : a + 128] if a < CUT else inv2[0:1, a - CUT : a - CUT + 128]
+            dot_n[a : a + 128, :] = (f * inv).T.astype(BF)
 
         each_place(put)
         dq_ref[...] = jnp.zeros_like(dq_ref)
 
     k0 = pl.multiple_of(i * rows, 128)
-    dv, dk = grads_block(k0, rows, e_ref, inv_ref, qn_ref, kt_ref, vn_ref, dot_t, dot_n, dq_ref)
+    dv, dk = grads_block(
+        k0, rows, e1, e2, inv1, inv2, qn_ref, kt_ref, vn_ref, dot_t, dot_n, dq_ref
+    )
     for j in range(rows // BIG):
         out_ref[j, 0:HD, 0:BIG] = dv[:, j * BIG : (j + 1) * BIG]
         out_ref[j, 0:HD, BIG : 2 * BIG] = dk[:, j * BIG : (j + 1) * BIG]
 
 
-def grads_a(dout, e, inv, qn, kt, vn, rows=256):
+def grads_a(dout, e1, e2, inv1, inv2, qn, kt, vn, rows=256):
     return pl.pallas_call(
         functools.partial(grads_a_body, rows),
         grid=(SRC * BIG // rows,),
         in_specs=[
             whole(SRC, 48, 384),
-            pl.BlockSpec((rows, N), lambda i: (i, 0)),
-            whole(8, N),
+            pl.BlockSpec((rows, CUT), lambda i: (i, 0)),
+            pl.BlockSpec((rows, N - CUT), lambda i: (i, 0)),
+            whole(8, CUT),
+            whole(8, N - CUT),
             whole(N, HD),
             whole(HD, N),
             whole(N, EXT),
         ],
         out_specs=[
-            pl.BlockSpec((rows // BIG, HD + 16, 2 * BIG), lambda i: (i, 0, 0)),
+            pl.BlockSpec((rows // BIG, HD, 2 * BIG), lambda i: (i, 0, 0)),
             whole(HD, N),
             whole(EXT, N),
             whole(N, HD),
         ],
         out_shape=[
-            jax.ShapeDtypeStruct((SRC, HD + 16, 2 * BIG), BF),
+            jax.ShapeDtypeStruct((SRC, HD, 2 * BIG), BF),
             jax.ShapeDtypeStruct((HD, N), F32),
             jax.ShapeDtypeStruct((EXT, N), BF),
             jax.ShapeDtypeStruct((N, HD), BF),
@@ -381,10 +360,10 @@
         compiler_params=params(),
         cost_estimate=cost(8 * N * SRC * BIG * HD, 18 * 10**6),
         name="grads_a",
-    )(dout, e, inv, qn, kt, vn)
-
-
-def grads_b_body(rows, e_ref, inv_ref, qn_ref, kt_ref, vn_ref, dot_t, dot_n, dq_ref, out_ref, acc):
+    )(dout, e1, e2, inv1, inv2, qn, kt, vn)
+
+
+def grads_b_body(rows, e1, e2, inv1, inv2, qn_ref, kt_ref, vn_ref, dot_t, dot_n, dq_ref, out_ref, acc):
     i = pl.program_id(0)
     base = SRC * BIG
 
@@ -393,7 +372,9 @@
         acc[...] = dq_ref[...]
 
     k0 = pl.multiple_of(base + i * rows, 128)
-    dv, dk = grads_block(k0, rows, e_ref, inv_ref, qn_ref, kt_ref, vn_ref, dot_t, dot_n, acc)
+    dv, dk = grads_block(
+        k0, rows, e1, e2, inv1, inv2, qn_ref, kt_ref, vn_ref, dot_t, dot_n, acc
+    )
     for j in range(rows // SMALL):
         a = j * SMALL
         out_ref[i * (rows // SMALL) + j, 0:HD, :] = jnp.concatenate(
@@ -411,14 +392,16 @@
             ).astype(BF)
 
 
-def grads_b(e, inv, qn, kt, vn, dot_t, dot_n, dq, rows=256):
+def grads_b(e1, e2, inv1, inv2, qn, kt, vn, dot_t, dot_n, dq, rows=256):
     off = SRC * BIG // rows
     return pl.pallas_call(
         functools.partial(grads_b_body, rows),
         grid=(SRC * SMALL // rows,),
         in_specs=[
-            pl.BlockSpec((rows, N), lambda i: (i + off, 0)),
-            whole(8, N),
+            pl.BlockSpec((rows, CUT), lambda i: (i + off, 0)),
+            pl.BlockSpec((rows, N - CUT), lambda i: (i + off, 0)),
+            whole(8, CUT),
+            whole(8, N - CUT),
             whole(N, HD),
             whole(HD, N),
             whole(N, EXT),
@@ -426,50 +409,72 @@
             whole(N, HD),
             whole(HD, N),
         ],
-        out_specs=whole(SRC, 256, 128),
-        out_shape=jax.ShapeDtypeStruct((SRC, 256, 128), BF),
+        out_specs=whole(SRC, 200, 128),
+        out_shape=jax.ShapeDtypeStruct((SRC, 200, 128), BF),
         scratch_shapes=[pltpu.VMEM((HD, N), F32)],
         compiler_params=params(),
         cost_estimate=cost(8 * N * SRC * SMALL * HD, 11 * 10**6),
         name="grads_b",
-    )(e, inv, qn, kt, vn, dot_t, dot_n, dq)
-
-
-def unpack_body(a_ref, b_ref, dq_ref, dk_ref, dv_ref, dw_ref):
-    def rows(ref, sl, lanes):
-        return jnp.concatenate([ref[h, sl, lanes] for h in range(HEADS)], axis=0).T
-
-    dv_ref[0, 0:BIG] = rows(a_ref, slice(0, HD), slice(0, BIG))
-    dk_ref[0, 0:BIG] = rows(a_ref, slice(0, HD), slice(BIG, 2 * BIG))
-    both = rows(b_ref, slice(0, HD), slice(0, BIG))
-    dv_ref[0, BIG:TOK] = both[:SMALL]
-    dk_ref[0, BIG:TOK] = both[SMALL:]
-    dq_ref[0, 0:BIG] = rows(b_ref, slice(HD, 2 * HD), slice(0, BIG))
+    )(e1, e2, inv1, inv2, qn, kt, vn, dot_t, dot_n, dq)
+
+
+def patch_rows(ref, sl, lanes):
+    return jnp.concatenate([ref[h, sl, lanes] for h in range(HEADS)], axis=0).T
+
+
+def unpack_a_body(a_ref, dk_ref, dv_ref):
+    dv_ref[0] = patch_rows(a_ref, slice(0, HD), slice(0, BIG))
+    dk_ref[0] = patch_rows(a_ref, slice(0, HD), slice(BIG, 2 * BIG))
+
+
+def unpack_a(a):
+    shape = jax.ShapeDtypeStruct((1, TOK, D), BF)
+    spec = pl.BlockSpec((1, BIG, D), lambda i: (0, 0, 0))
+    return pl.pallas_call(
+        unpack_a_body,
+        grid=(1,),
+        in_specs=[whole(HEADS, HD, 2 * BIG)],
+        out_specs=[spec, spec],
+        out_shape=[shape, shape],
+        compiler_params=params(),
+        cost_estimate=cost(0, 2 * 10**6),
+        name="unpack_a",
+    )(a)
+
+
+def unpack_b_body(at_ref, b_ref, w_own, w_oth, dk_in, dv_in, dq_ref, dk_ref, dv_ref, dw_ref):
+    both = patch_rows(b_ref, slice(0, HD), slice(0, BIG))
+    dv_ref[0] = both[:SMALL]
+    dk_ref[0] = both[SMALL:]
+    dq_ref[0, 0:BIG] = patch_rows(b_ref, slice(HD, 2 * HD), slice(0, BIG))
     tail = []
     for h in range(HEADS):
         t = b_ref[h, 2 * HD : 2 * HD + HALF, :].astype(F32)
         tail += [t[:, :SMALL], t[:, SMALL:]]
     dq_ref[0, BIG:TOK] = jnp.concatenate(tail, axis=0).T.astype(BF)
-    for half in range(2):
-        pieces = [b_ref[2 * g + half, 200:256, :].astype(F32) for g in range(8)]
-        for c in range(2):
-            for j in range(5):
-                r = c * 25 + j * 5
-                a = half * 640 + j * 128
-                dw_ref[c * HALF : (c + 1) * HALF, a : a + 128] = jnp.concatenate(
-                    [p[r : r + 5] for p in pieces], axis=0
-                )
-
-
-def unpack(a, b):
+    c = at_ref[0]
+    factor = 1.0 / float(16 * N) ** 0.5
+    for ref, row in ((w_own, c), (w_oth, 1 - c)):
+        dw_ref[pl.ds(pl.multiple_of(row * HALF, 8), HALF), :] = ref[...] * factor
+
+
+def unpack_b(at, b, parts, dk, dv):
     shape = jax.ShapeDtypeStruct((1, TOK, D), BF)
-    return pl.pallas_call(
-        unpack_body,
+    spec = pl.BlockSpec((1, SMALL, D), lambda i: (0, 2, 0))
+    hbm = pl.BlockSpec(memory_space=pl.ANY)
+    return pl.pallas_call(
+        unpack_b_body,
+        grid=(1,),
+        in_specs=[pl.BlockSpec(memory_space=pltpu.SMEM), whole(HEADS, 200, 128)]
+        + [whole(HALF, D)] * 2
+        + [hbm, hbm],
+        out_specs=[whole(1, TOK, D), spec, spec, whole(HD, D)],
         out_shape=[shape] * 3 + [jax.ShapeDtypeStruct((HD, D), F32)],
+        input_output_aliases={4: 1, 5: 2},
         compiler_params=params(),
         cost_estimate=cost(0, 3 * 10**6),
-        name="unpack",
-    )(a, b)
+        name="unpack_b",
+    )(at, b, *parts, dk, dv)
 
 
 UP = [(i, (i + 1) % 8) for i in range(8)]
@@ -485,46 +490,58 @@
     def exchange(x):
         return lax.all_to_all(x, SEQ, 0, 0, tiled=True)
 
+    hold = lax.optimization_barrier
+
+    def scalar(*i):
+        return jnp.stack(i).astype(jnp.int32)
+
+    def up(block):
+        return lax.ppermute(block, "z", UP)
+
+    def down(block):
+        return lax.ppermute(block, "z", DOWN)
+
     w_half = lax.dynamic_slice_in_dim(w_out, c * HALF, HALF, 0)
     pair = jnp.stack([w_half, lax.ppermute(w_half, "yl", swap)])
-    query, keys, values, attn, d_block, pair = lax.optimization_barrier(
-        (query, keys, values, attn, d_block, pair)
-    )
-    def scalar(i):
-        return i.reshape(1).astype(jnp.int32)
-
-    def up(block):
-        return lax.ppermute(block, "z", UP)
-
-    def down(block):
-        return lax.ppermute(block, "z", DOWN)
-
-    hold = lax.optimization_barrier
     g_oth = lax.ppermute(d_block, "c", swap)
-    f1, g1, packed = hold((up(pair), down(pair), pack_qkv(query, keys, values)))
+    packed = pack_qkv(query, keys, values)
+    pair, packed, g_oth, attn = hold((pair, packed, g_oth, attn))
     qkv = exchange(packed)
-    f2, g2, attn = hold((up(f1), down(g1), attn))
+    f1, g1, attn = hold((up(pair), down(pair), attn))
     a_own, a_send = split_attn(scalar(c), attn)
-    f3, g3, a_oth, g_oth = hold((up(f2), down(g2), lax.ppermute(a_send, "c", swap), g_oth))
+    f2, g2, a_send = hold((up(f1), down(g1), a_send))
+    a_oth = lax.ppermute(a_send, "c", swap)
+    f3, g3, a_oth = hold((up(f2), down(g2), a_oth))
     keep, give, gx, ax = weight_share(scalar(yl), d_block, g_oth, a_own, a_oth)
+    f4, give = hold((up(f3), give))
     came = lax.ppermute(give, "yl", swap)
-    blocks = [pair, f1, g1, f2, g2, f3, g3, up(f3)]
 
     zs = [(z + o) % 8 for o in OFFSETS]
-    ids = jnp.stack([y * 8 + k for k in zs for y in (yl, 1 - yl)]).astype(jnp.int32)
-    dout, qkv = lax.optimization_barrier((out_grad(ids, blocks, gx, ax), qkv))
+    ids = scalar(*[y * 8 + k for k in zs for y in (yl, 1 - yl)])
+    dout = out_grad(ids, [pair, f1, g1, f2, g2, f3, g3, f4], gx, ax)
+    dout, qkv = hold((dout, qkv))
     dout = exchange(dout)
 
-    e, inv, qn, kt, vn = scores(qkv)
-    both = (keep.astype(F32) + came.astype(F32)).astype(BF)
-    both, e = lax.optimization_barrier((both, e))
-    part = lax.all_to_all(both, "z", 0, 0, tiled=True)
-    first, dq, dot_t, dot_n = grads_a(dout, e, inv, qn, kt, vn)
-    first = exchange(lax.dynamic_update_slice(first, sum_z(part), (0, HD, 0)))
-    second = grads_b(e, inv, qn, kt, vn, dot_t, dot_n, dq)
-    second = exchange(lax.dynamic_update_slice(second, sum_seq(first[:, HD:]), (0, 200, 0)))
-    d_query, d_keys, d_values, d_weight = unpack(first, second)
-    return d_query, d_keys, d_values, d_weight
+    qt, kn, qn, kt, vn = prepare(qkv)
+    e1, inv1 = scores(qt, kn, 0, CUT)
+    came, qt, inv1 = hold((came, qt, inv1))
+    part = (keep.astype(F32) + came.astype(F32)).astype(BF)
+    part, dout, qt = hold((part, dout, qt))
+    part = lax.all_to_all(part, "z", 0, 0, tiled=True)
+    e2, inv2 = scores(qt, kn, CUT, N)
+    first, dq, dot_t, dot_n = grads_a(dout, e1, e2, inv1, inv2, qn, kt, vn)
+    first, part = hold((first, part))
+    first = exchange(first)
+    second = grads_b(e1, e2, inv1, inv2, qn, kt, vn, dot_t, dot_n, dq)
+    mine = jnp.sum(part.astype(F32), axis=0)
+    t = mine
+    for k in range(1, 4):
+        t = t + lax.ppermute(mine, "x", [(i, (i + k) % 4) for i in range(4)])
+    second, t = hold((second, t))
+    second = exchange(second)
+    u = t + lax.ppermute(t, "yh", swap)
+    d_keys, d_values = unpack_a(first)
+    return unpack_b(scalar(c), second, [u, lax.ppermute(u, "c", swap)], d_keys, d_values)
 
 
 def solution(mesh):

time: 175 us -> 160 us (0.914)
  blocking collectives: 22 us -> 0 us
  starting transfers between devices: 46.1 us -> 58.4 us
  local copies, waits for them, and re-layouts: 7.22 us -> 2.41 us
  Pallas kernels: 64.6 us -> 69.1 us
  waiting for transfers between devices: 31.1 us -> 26.8 us
    all_to_all x1 -> x0, blocking collectives: 22 us -> none  [exchange(): return lax.all_to_all(x, SEQ, 0, 0, tiled=True)]
    ppermute x1 -> x6, waiting for transfers between devices: 0.01 us -> 14.1 us  [the longest x1 14.1 us: body(): u = t + lax.ppermute(t, 'yh', swap)]
    ppermute x4, waiting for transfers between devices: 18.6 us -> 9.74 us  [up(): return lax.ppermute(block, 'z', UP)]
    ppermute x1 -> x6, starting transfers between devices: 1.24 us -> 8.83 us  [the longest x3 3.84 us: body(): t = t + lax.ppermute(mine, 'x', [(i, (i + k) % 4) for i in range(4)])]
    all_to_all x1, waiting for transfers between devices: 6.72 us -> 0.01 us  [body(): part = lax.all_to_all(part, 'z', 0, 0, tiled=True)]
    pallas_call x4 -> x5, Pallas kernels: 22.6 us -> 27.6 us  [the longest x2 18.6 us: scores(): pl.pallas_call(functools.partial(scores_body, cols, chunk, begin, end), g...]
    dynamic_update_slice x2 -> x0, local copies, waits for them, and re-layouts: 3.3 us -> none  [the longest x1 1.7 us: body(): lax.dynamic_update_slice(second, sum_seq(first[:, HD:]), (0, 200, 0))]
    ppermute x1, starting transfers between devices: 0.19 us -> 3.33 us  [body(): g_oth = lax.ppermute(d_block, 'c', swap)]
  transfers between devices with their start and end apart: 15 -> 21, of which waited for: 7 -> 6; matrix products, arithmetic and copies ran while one was open for 2% -> 1% of each run, Pallas kernels for 33% -> 42%
where the time goes in v2:
time: 160 us; the launch traced here: 159 us
  Pallas kernels  69.1 us (43%)
  starting transfers between devices  58.4 us (36%)
  waiting for transfers between devices  26.8 us (17%)
  local copies, waits for them, and re-layouts  2.41 us (2%)
    all_to_all x4, starting transfers between devices, exchange(): return lax.all_to_all(x, SEQ, 0, 0, tiled=True)  29.8 us
    pallas_call x2, Pallas kernels, scores(): pl.pallas_call(functools.partial(scores_body, cols, chunk, begin, end), g...  18.6 us
    pallas_call x1, Pallas kernels, grads_a(): pl.pallas_call(functools.partial(grads_a_body, rows), grid=(SRC * BIG //...  17.3 us
    ppermute x1, waiting for transfers between devices, body(): u = t + lax.ppermute(t, 'yh', swap)  14.1 us
    pallas_call x1, Pallas kernels, grads_b(): pl.pallas_call(functools.partial(grads_b_body, rows), grid=(SRC * SMALL /...  10.8 us
    ppermute x3, starting transfers between devices, down(): return lax.ppermute(block, 'z', DOWN)  10.8 us
    ppermute x4, waiting for transfers between devices, up(): return lax.ppermute(block, 'z', UP)  9.74 us
    pallas_call x1, Pallas kernels, prepare(): pl.pallas_call(prepare_body, out_shape=[jax.ShapeDtypeStruct((HD, N), BF)...  4.34 us
  transfers between devices with their start and end apart: 21, of which 6 were waited for; matrix products, arithmetic and copies ran while one was open for 1% of the time, Pallas kernels for 42%

profile of v2, /device:TPU:1, one launch (start us, length us, event | category | flops | bytes accessed | tf_op | source)
XLA Modules:
  0.0 158.9 jit_solution(13371775999977096356)
XLA Ops:
  0.6 3.3 %collective-permute-start.1 = (bf16[1,192,1280]{2,1,0:T(8,128)(2,1)}, bf16[1,192,1280]{2,1,0:T(8,128)(2,1)S(1)}, u32[]{:S(2)}, u32[]{:S(2)}) collective-permute-start(bf16[1,192,1280]{2,1,0:T(8,128)(2,1)} %g_own.1), channel_id=1, source_target_pairs={{0,16},{16,0},{1,17},{17,1},{2,18},{18,2},{3,19},{19,3},{4,20},{20... | collective-permute-start | bytes 1474568 | tf_op jit(solution)/shard_map/ppermute | solution.py:506
  4.1 3.2 %pack_qkv.1 = bf16[16,120,384]{2,1,0:T(8,128)(2,1)} custom-call(bf16[1,192,1280]{2,1,0:T(8,128)(2,1)} %q_ref.1, bf16[1,192,1280]{2,1,0:T(8,128)(2,1)} %k_ref.1, bf16[1,192,1280]{2,1,0:T(8,128)(2,1)} %v_ref.1), custom_call_target="tpu_custom_call" | custom-call | bytes 3000000 | tf_op jit(solution)/shard_map/pack_qkv/pallas_call | solution.py:61
  7.6 5.1 %collective-permute-start.3 = (bf16[2,40,1280]{2,1,0:T(8,128)(2,1)S(1)}, bf16[2,40,1280]{2,1,0:T(8,128)(2,1)S(1)}, u32[]{:S(2)}, u32[]{:S(2)}) collective-permute-start(bf16[2,40,1280]{2,1,0:T(8,128)(2,1)S(1)} %pad_maximum_fusion.refs_0_), channel_id=1, source_target_pairs={{0,7},{1,0},{2,1},{3,2},{4,3},{5,4},{6,5},{7,6},{8,15},{9,8},{10,9... | collective-permute-start | bytes 614408 | tf_op jit(solution)/shard_map/ppermute | solution.py:502
  12.7 8.1 %all-to-all-start = ((bf16[16,120,384]{2,1,0:T(8,128)(2,1)}), bf16[16,120,384]{2,1,0:T(8,128)(2,1)S(1)}, u32[]{:S(2)}, u32[]{:S(2)}) async-start(bf16[16,120,384]{2,1,0:T(8,128)(2,1)} %pack_qkv.1), calls=%async_computation | async-start | bytes 2949120 | tf_op jit(solution)/shard_map/all_to_all | solution.py:491
  20.9 3.0 %collective-permute-start.5 = (bf16[2,40,1280]{2,1,0:T(8,128)(2,1)S(1)}, bf16[2,40,1280]{2,1,0:T(8,128)(2,1)S(1)}, u32[]{:S(2)}, u32[]{:S(2)}) collective-permute-start(bf16[2,40,1280]{2,1,0:T(8,128)(2,1)S(1)} %collective-permute-done.3.refs_2_), channel_id=1, source_target_pairs={{0,7},{1,0},{2,1},{3,2},{4,3},{5,4},{6,5},{7,6},{8,15},{9,8},{10,9... | collective-permute-start | bytes 614408 | tf_op jit(solution)/shard_map/ppermute | solution.py:502
  26.1 2.8 %collective-permute-done.4.refs_3_ = bf16[2,40,1280]{2,1,0:T(8,128)(2,1)S(1)} collective-permute-done((bf16[2,40,1280]{2,1,0:T(8,128)(2,1)S(1)}, bf16[2,40,1280]{2,1,0:T(8,128)(2,1)S(1)}, u32[]{:S(2)}, u32[]{:S(2)}) %collective-permute-start.4) | collective-permute-done | bytes 204832 | tf_op jit(solution)/shard_map/ppermute | solution.py:499
  30.0 2.7 %collective-permute-start.7 = (bf16[2,40,1280]{2,1,0:T(8,128)(2,1)S(1)}, bf16[2,40,1280]{2,1,0:T(8,128)(2,1)S(1)}, u32[]{:S(2)}, u32[]{:S(2)}) collective-permute-start(bf16[2,40,1280]{2,1,0:T(8,128)(2,1)S(1)} %collective-permute-done.5.refs_4_), channel_id=1, source_target_pairs={{0,7},{1,0},{2,1},{3,2},{4,3},{5,4},{6,5},{7,6},{8,15},{9,8},{10,9... | collective-permute-start | bytes 614408 | tf_op jit(solution)/shard_map/ppermute | solution.py:502
  32.6 5.2 %collective-permute-done.6.refs_5_ = bf16[2,40,1280]{2,1,0:T(8,128)(2,1)S(1)} collective-permute-done((bf16[2,40,1280]{2,1,0:T(8,128)(2,1)S(1)}, bf16[2,40,1280]{2,1,0:T(8,128)(2,1)S(1)}, u32[]{:S(2)}, u32[]{:S(2)}) %collective-permute-start.6) | collective-permute-done | bytes 204832 | tf_op jit(solution)/shard_map/ppermute | solution.py:499
  38.9 4.2 %weight_share.1 = (bf16[8,40,1280]{2,1,0:T(8,128)(2,1)}, bf16[8,40,1280]{2,1,0:T(8,128)(2,1)}, bf16[384,1280]{1,0:T(8,128)(2,1)}, bf16[16,40,384]{2,1,0:T(8,128)(2,1)}) custom-call(s32[1]{0:T(128)} %bitcast.19.y_ref, bf16[1,192,1280]{2,1,0:T(8,128)(2,1)} %g_own.1, bf16[1,192,1280]{2,1,0:T(8,128)(2,1)} %copy-done.16, ...), custom_call_target="tpu_custom_call" | custom-call | flops 629145600 | bytes 6000000 | tf_op jit(solution)/shard_map/weight_share/pallas_call | solution.py:114
  46.6 3.9 %out_grad.1 = bf16[16,48,384]{2,1,0:T(8,128)(2,1)} custom-call(s32[16]{0:T(128)} %stack.84.ids, bf16[2,40,1280]{2,1,0:T(8,128)(2,1)} %copy-done.7, bf16[2,40,1280]{2,1,0:T(8,128)(2,1)} %copy-done.10, bf16[2,40,1280]{2,1,0:T(8,128)(2,1)} %copy-done.9, bf16[2,40,1280]{2,1,0:T(8,128)(2,1)} %copy-done.11, bf16[2,40,1280]{2,1,0:T(8,128)(2,1)} %copy-done.12, ...), custom_call_target="tpu_custom_call" | custom-call | flops 629145600 | bytes 4000000 | tf_op jit(solution)/shard_map/out_grad/pallas_call | solution.py:150
  50.5 9.5 %all-to-all-start.1 = ((bf16[16,48,384]{2,1,0:T(8,128)(2,1)}), bf16[16,48,384]{2,1,0:T(8,128)(2,1)S(1)}, u32[]{:S(2)}, u32[]{:S(2)}) async-start(bf16[16,48,384]{2,1,0:T(8,128)(2,1)} %out_grad.1), calls=%async_computation.1 | async-start | bytes 1179648 | tf_op jit(solution)/shard_map/all_to_all | solution.py:491
  60.1 4.3 %prepare.1 = (bf16[80,3072]{1,0:T(8,128)(2,1)}, bf16[3072,80]{1,0:T(8,128)(2,1)}, bf16[3072,80]{1,0:T(8,128)(2,1)}, bf16[80,3072]{1,0:T(8,128)(2,1)}, bf16[3072,96]{1,0:T(8,128)(2,1)}) custom-call(bf16[16,120,384]{2,1,0:T(8,128)(2,1)} %copy-done.1), custom_call_target="tpu_custom_call" | custom-call | bytes 5000000 | tf_op jit(solution)/shard_map/prepare/pallas_call | solution.py:215
  64.4 11.2 %scores.2 = (bf16[3072,2048]{1,0:T(8,128)(2,1)}, f32[8,2048]{1,0:T(8,128)}) custom-call(bf16[80,3072]{1,0:T(8,128)(2,1)} %get-tuple-element.81.qt, bf16[3072,80]{1,0:T(8,128)(2,1)} %get-tuple-element.73.kn), custom_call_target="tpu_custom_call" | custom-call | flops 1006632960 | bytes 12582912 | tf_op jit(solution)/shard_map/scores/pallas_call | solution.py:256
  76.8 4.1 %all-to-all-start.2 = ((bf16[8,40,1280]{2,1,0:T(8,128)(2,1)}), bf16[8,40,1280]{2,1,0:T(8,128)(2,1)S(1)}, u32[]{:S(2)}, u32[]{:S(2)}) async-start(bf16[8,40,1280]{2,1,0:T(8,128)(2,1)} %add_convert_fusion), calls=%async_computation.2 | async-start | bytes 1638400 | tf_op jit(solution)/shard_map/all_to_all | solution.py:530
  80.9 7.4 %scores.3 = (bf16[3072,1024]{1,0:T(8,128)(2,1)}, f32[8,1024]{1,0:T(8,128)}) custom-call(bf16[80,3072]{1,0:T(8,128)(2,1)} %get-tuple-element.81.qt, bf16[3072,80]{1,0:T(8,128)(2,1)} %get-tuple-element.73.kn), custom_call_target="tpu_custom_call" | custom-call | flops 503316480 | bytes 6291456 | tf_op jit(solution)/shard_map/scores/pallas_call | solution.py:256
  88.3 17.3 %grads_a.1 = (bf16[16,80,256]{2,1,0:T(8,128)(2,1)}, f32[80,3072]{1,0:T(8,128)}, bf16[96,3072]{1,0:T(8,128)(2,1)}, bf16[3072,80]{1,0:T(8,128)(2,1)}) custom-call(bf16[16,48,384]{2,1,0:T(8,128)(2,1)} %copy-done.4, bf16[3072,2048]{1,0:T(8,128)(2,1)} %get-tuple-element.74.e1, bf16[3072,1024]{1,0:T(8,128)(2,1)} %get-tuple-element.82.e2, ...), custom_call_target="tpu_custom_call" | custom-call | flops 4026531840 | bytes 18000000 | tf_op jit(solution)/shard_map/grads_a/pallas_call | solution.py:335
  105.7 2.7 %collective-permute-start.13 = (f32[40,1280]{1,0:T(8,128)S(1)}, f32[40,1280]{1,0:T(8,128)S(1)}, u32[]{:S(2)}, u32[]{:S(2)}) collective-permute-start(f32[40,1280]{1,0:T(8,128)S(1)} %convert_reduce_fusion), channel_id=1, source_target_pairs={{0,96},{32,0},{64,32},{96,64},{1,97},{33,1},{65,33},{97,65},{2,98}... | collective-permute-start | bytes 614408 | tf_op jit(solution)/shard_map/ppermute | solution.py:539
  109.5 7.5 %all-to-all-start.4 = ((bf16[16,80,256]{2,1,0:T(8,128)(2,1)}), bf16[16,80,256]{2,1,0:T(8,128)(2,1)S(1)}, u32[]{:S(2)}, u32[]{:S(2)}) async-start(bf16[16,80,256]{2,1,0:T(8,128)(2,1)} %get-tuple-element.97), calls=%async_computation.4 | async-start | bytes 1310720 | tf_op jit(solution)/shard_map/all_to_all | solution.py:491
  117.1 10.8 %grads_b.1 = bf16[16,200,128]{2,1,0:T(8,128)(2,1)} custom-call(bf16[3072,2048]{1,0:T(8,128)(2,1)} %get-tuple-element.74.e1, bf16[3072,1024]{1,0:T(8,128)(2,1)} %get-tuple-element.82.e2, f32[8,2048]{1,0:T(8,128)} %get-tuple-element.83.inv1, f32[8,1024]{1,0:T(8,128)} %get-tuple-element.84.inv2, bf16[3072,80]{1,0:T(8,128)(2,1)} %get-tuple-element.85.qn_ref, ...), custom_call_target="tpu_custom_call" | custom-call | flops 2013265920 | bytes 11000000 | tf_op jit(solution)/shard_map/grads_b/pallas_call | solution.py:397
  128.0 2.6 %all-to-all-done.4.a_ref = bf16[16,80,256]{2,1,0:T(8,128)(2,1)S(1)} async-done(((bf16[16,80,256]{2,1,0:T(8,128)(2,1)}), bf16[16,80,256]{2,1,0:T(8,128)(2,1)S(1)}, u32[]{:S(2)}, u32[]{:S(2)}) %all-to-all-start.4) | async-done | bytes 655392 | tf_op jit(solution)/shard_map/all_to_all | solution.py:491
  130.6 4.7 %all-to-all-start.3 = ((bf16[16,200,128]{2,1,0:T(8,128)(2,1)}), bf16[16,200,128]{2,1,0:T(8,128)(2,1)S(1)}, u32[]{:S(2)}, u32[]{:S(2)}) async-start(bf16[16,200,128]{2,1,0:T(8,128)(2,1)} %grads_b.1), calls=%async_computation.3 | async-start | bytes 1638400 | tf_op jit(solution)/shard_map/all_to_all | solution.py:491
  135.2 2.9 %collective-permute-start.14 = (f32[40,1280]{1,0:T(8,128)S(1)}, f32[40,1280]{1,0:T(8,128)S(1)}, u32[]{:S(2)}, u32[]{:S(2)}) collective-permute-start(f32[40,1280]{1,0:T(8,128)S(1)} %add_add_fusion), channel_id=1, source_target_pairs={{0,128},{128,0},{1,129},{129,1},{2,130},{130,2},{3,131},{131,3},{4... | collective-permute-start | bytes 614408 | tf_op jit(solution)/shard_map/ppermute | solution.py:542
  138.1 14.1 %collective-permute-done.14 = f32[40,1280]{1,0:T(8,128)S(1)} collective-permute-done((f32[40,1280]{1,0:T(8,128)S(1)}, f32[40,1280]{1,0:T(8,128)S(1)}, u32[]{:S(2)}, u32[]{:S(2)}) %collective-permute-start.14) | collective-permute-done | bytes 204832 | tf_op jit(solution)/shard_map/ppermute | solution.py:542
  156.3 2.6 %unpack_b.1 = (bf16[1,192,1280]{2,1,0:T(8,128)(2,1)}, bf16[1,192,1280]{2,1,0:T(8,128)(2,1)}, bf16[1,192,1280]{2,1,0:T(8,128)(2,1)}, f32[80,1280]{1,0:T(8,128)}) custom-call(s32[1]{0:T(128)} %bitcast.c_ref.at_ref, bf16[16,200,128]{2,1,0:T(8,128)(2,1)} %copy-done.2, f32[40,1280]{1,0:T(8,128)} %copy-done.5, ...), custom_call_target="tpu_custom_call", output_to_operand_aliasing={{1}: (4, {}), {2}: (5, {})} | custom-call | bytes 3000000 | tf_op jit(solution)/shard_map/unpack_b/pallas_call | solution.py:465
  (73 shorter events, 14.9 us)
Async XLA Ops:
  0.6 7.0 %collective-permute-start.1 = (bf16[1,192,1280]{2,1,0:T(8,128)(2,1)}, bf16[1,192,1280]{2,1,0:T(8,128)(2,1)S(1)}, u32[]{:S(2)}, u32[]{:S(2)}) collective-permute-start(bf16[1,192,1280]{2,1,0:T(8,128)(2,1)} %g_own.1), channel_id=1, source_target_pairs={{0,16},{16,0},{1,17},{17,1},{2,18},{18,2},{3,19},{19,3},{4,20},{20... | collective-permute-start | bytes 1474568 | tf_op jit(solution)/shard_map/ppermute | solution.py:506
  4.0 3.6 %collective-permute-start = (bf16[40,1280]{1,0:T(8,128)(2,1)S(1)}, bf16[40,1280]{1,0:T(8,128)(2,1)S(1)}, u32[]{:S(2)}, u32[]{:S(2)}) collective-permute-start(bf16[40,1280]{1,0:T(8,128)(2,1)S(1)} %constant_dynamic-slice_fusion), channel_id=1, source_target_pairs={{0,8},{8,0},{1,9},{9,1},{2,10},{10,2},{3,11},{11,3},{4,12},{12,4},... | collective-permute-start | bytes 307208 | tf_op jit(solution)/shard_map/ppermute | solution.py:505
  7.6 13.1 %collective-permute-start.3 = (bf16[2,40,1280]{2,1,0:T(8,128)(2,1)S(1)}, bf16[2,40,1280]{2,1,0:T(8,128)(2,1)S(1)}, u32[]{:S(2)}, u32[]{:S(2)}) collective-permute-start(bf16[2,40,1280]{2,1,0:T(8,128)(2,1)S(1)} %pad_maximum_fusion.refs_0_), channel_id=1, source_target_pairs={{0,7},{1,0},{2,1},{3,2},{4,3},{5,4},{6,5},{7,6},{8,15},{9,8},{10,9... | collective-permute-start | bytes 614408 | tf_op jit(solution)/shard_map/ppermute | solution.py:502
  12.7 8.1 %collective-permute-start.2 = (bf16[2,40,1280]{2,1,0:T(8,128)(2,1)S(1)}, bf16[2,40,1280]{2,1,0:T(8,128)(2,1)S(1)}, u32[]{:S(2)}, u32[]{:S(2)}) collective-permute-start(bf16[2,40,1280]{2,1,0:T(8,128)(2,1)S(1)} %pad_maximum_fusion.refs_0_), channel_id=1, source_target_pairs={{0,1},{1,2},{2,3},{3,4},{4,5},{5,6},{6,7},{7,0},{8,9},{9,10},{10,1... | collective-permute-start | bytes 614408 | tf_op jit(solution)/shard_map/ppermute | solution.py:499
  12.7 37.8 %all-to-all-start = ((bf16[16,120,384]{2,1,0:T(8,128)(2,1)}), bf16[16,120,384]{2,1,0:T(8,128)(2,1)S(1)}, u32[]{:S(2)}, u32[]{:S(2)}) async-start(bf16[16,120,384]{2,1,0:T(8,128)(2,1)} %pack_qkv.1), calls=%async_computation | async-start | bytes 2949120 | tf_op jit(solution)/shard_map/all_to_all | solution.py:491
  20.8 25.8 %copy-start.9 = (bf16[2,40,1280]{2,1,0:T(8,128)(2,1)}, bf16[2,40,1280]{2,1,0:T(8,128)(2,1)S(1)}, u32[]{:S(2)}) copy-start(bf16[2,40,1280]{2,1,0:T(8,128)(2,1)S(1)} %collective-permute-done.3.refs_2_) | copy-start | bytes 614404
  20.8 25.8 %copy-start.10 = (bf16[2,40,1280]{2,1,0:T(8,128)(2,1)}, bf16[2,40,1280]{2,1,0:T(8,128)(2,1)S(1)}, u32[]{:S(2)}) copy-start(bf16[2,40,1280]{2,1,0:T(8,128)(2,1)S(1)} %collective-permute-done.2.refs_1_) | copy-start | bytes 614404
  20.8 8.0 %collective-permute-start.4 = (bf16[2,40,1280]{2,1,0:T(8,128)(2,1)S(1)}, bf16[2,40,1280]{2,1,0:T(8,128)(2,1)S(1)}, u32[]{:S(2)}, u32[]{:S(2)}) collective-permute-start(bf16[2,40,1280]{2,1,0:T(8,128)(2,1)S(1)} %collective-permute-done.2.refs_1_), channel_id=1, source_target_pairs={{0,1},{1,2},{2,3},{3,4},{4,5},{5,6},{6,7},{7,0},{8,9},{9,10},{10,1... | collective-permute-start | bytes 614408 | tf_op jit(solution)/shard_map/ppermute | solution.py:499
  20.9 7.9 %collective-permute-start.5 = (bf16[2,40,1280]{2,1,0:T(8,128)(2,1)S(1)}, bf16[2,40,1280]{2,1,0:T(8,128)(2,1)S(1)}, u32[]{:S(2)}, u32[]{:S(2)}) collective-permute-start(bf16[2,40,1280]{2,1,0:T(8,128)(2,1)S(1)} %collective-permute-done.3.refs_2_), channel_id=1, source_target_pairs={{0,7},{1,0},{2,1},{3,2},{4,3},{5,4},{6,5},{7,6},{8,15},{9,8},{10,9... | collective-permute-start | bytes 614408 | tf_op jit(solution)/shard_map/ppermute | solution.py:502
  28.8 9.0 %collective-permute-start.8 = (bf16[16,40,192]{2,1,0:T(8,128)(2,1)}, bf16[16,40,192]{2,1,0:T(8,128)(2,1)S(1)}, u32[]{:S(2)}, u32[]{:S(2)}) collective-permute-start(bf16[16,40,192]{2,1,0:T(8,128)(2,1)} %get-tuple-element.60), channel_id=1, source_target_pairs={{0,16},{16,0},{1,17},{17,1},{2,18},{18,2},{3,19},{19,3},{4,20},{20... | collective-permute-start | bytes 737288 | tf_op jit(solution)/shard_map/ppermute | solution.py:513
  30.0 7.9 %collective-permute-start.6 = (bf16[2,40,1280]{2,1,0:T(8,128)(2,1)S(1)}, bf16[2,40,1280]{2,1,0:T(8,128)(2,1)S(1)}, u32[]{:S(2)}, u32[]{:S(2)}) collective-permute-start(bf16[2,40,1280]{2,1,0:T(8,128)(2,1)S(1)} %collective-permute-done.4.refs_3_), channel_id=1, source_target_pairs={{0,1},{1,2},{2,3},{3,4},{4,5},{5,6},{6,7},{7,0},{8,9},{9,10},{10,1... | collective-permute-start | bytes 614408 | tf_op jit(solution)/shard_map/ppermute | solution.py:499
  30.0 7.9 %collective-permute-start.7 = (bf16[2,40,1280]{2,1,0:T(8,128)(2,1)S(1)}, bf16[2,40,1280]{2,1,0:T(8,128)(2,1)S(1)}, u32[]{:S(2)}, u32[]{:S(2)}) collective-permute-start(bf16[2,40,1280]{2,1,0:T(8,128)(2,1)S(1)} %collective-permute-done.5.refs_4_), channel_id=1, source_target_pairs={{0,7},{1,0},{2,1},{3,2},{4,3},{5,4},{6,5},{7,6},{8,15},{9,8},{10,9... | collective-permute-start | bytes 614408 | tf_op jit(solution)/shard_map/ppermute | solution.py:502
  37.8 7.0 %collective-permute-start.9 = (bf16[2,40,1280]{2,1,0:T(8,128)(2,1)S(1)}, bf16[2,40,1280]{2,1,0:T(8,128)(2,1)S(1)}, u32[]{:S(2)}, u32[]{:S(2)}) collective-permute-start(bf16[2,40,1280]{2,1,0:T(8,128)(2,1)S(1)} %collective-permute-done.6.refs_5_), channel_id=1, source_target_pairs={{0,1},{1,2},{2,3},{3,4},{4,5},{5,6},{6,7},{7,0},{8,9},{9,10},{10,1... | collective-permute-start | bytes 614408 | tf_op jit(solution)/shard_map/ppermute | solution.py:499
  45.5 30.1 %collective-permute-start.10 = (bf16[8,40,1280]{2,1,0:T(8,128)(2,1)}, bf16[8,40,1280]{2,1,0:T(8,128)(2,1)S(1)}, u32[]{:S(2)}, u32[]{:S(2)}) collective-permute-start(bf16[8,40,1280]{2,1,0:T(8,128)(2,1)} %get-tuple-element.76), channel_id=1, source_target_pairs={{0,8},{8,0},{1,9},{9,1},{2,10},{10,2},{3,11},{11,3},{4,12},{12,4},... | collective-permute-start | bytes 2457608 | tf_op jit(solution)/shard_map/ppermute | solution.py:517
  50.5 26.2 %all-to-all-start.1 = ((bf16[16,48,384]{2,1,0:T(8,128)(2,1)}), bf16[16,48,384]{2,1,0:T(8,128)(2,1)S(1)}, u32[]{:S(2)}, u32[]{:S(2)}) async-start(bf16[16,48,384]{2,1,0:T(8,128)(2,1)} %out_grad.1), calls=%async_computation.1 | async-start | bytes 1179648 | tf_op jit(solution)/shard_map/all_to_all | solution.py:491
  76.8 28.8 %all-to-all-start.2 = ((bf16[8,40,1280]{2,1,0:T(8,128)(2,1)}), bf16[8,40,1280]{2,1,0:T(8,128)(2,1)S(1)}, u32[]{:S(2)}, u32[]{:S(2)}) async-start(bf16[8,40,1280]{2,1,0:T(8,128)(2,1)} %add_convert_fusion), calls=%async_computation.2 | async-start | bytes 1638400 | tf_op jit(solution)/shard_map/all_to_all | solution.py:530
  105.7 22.2 %collective-permute-start.13 = (f32[40,1280]{1,0:T(8,128)S(1)}, f32[40,1280]{1,0:T(8,128)S(1)}, u32[]{:S(2)}, u32[]{:S(2)}) collective-permute-start(f32[40,1280]{1,0:T(8,128)S(1)} %convert_reduce_fusion), channel_id=1, source_target_pairs={{0,96},{32,0},{64,32},{96,64},{1,97},{33,1},{65,33},{97,65},{2,98}... | collective-permute-start | bytes 614408 | tf_op jit(solution)/shard_map/ppermute | solution.py:539
  108.4 19.5 %collective-permute-start.12 = (f32[40,1280]{1,0:T(8,128)S(1)}, f32[40,1280]{1,0:T(8,128)S(1)}, u32[]{:S(2)}, u32[]{:S(2)}) collective-permute-start(f32[40,1280]{1,0:T(8,128)S(1)} %convert_reduce_fusion), channel_id=1, source_target_pairs={{0,64},{32,96},{64,0},{96,32},{1,65},{33,97},{65,1},{97,33},{2,66}... | collective-permute-start | bytes 614408 | tf_op jit(solution)/shard_map/ppermute | solution.py:539
  109.0 18.9 %collective-permute-start.11 = (f32[40,1280]{1,0:T(8,128)S(1)}, f32[40,1280]{1,0:T(8,128)S(1)}, u32[]{:S(2)}, u32[]{:S(2)}) collective-permute-start(f32[40,1280]{1,0:T(8,128)S(1)} %convert_reduce_fusion), channel_id=1, source_target_pairs={{0,32},{32,64},{64,96},{96,0},{1,33},{33,65},{65,97},{97,1},{2,34}... | collective-permute-start | bytes 614408 | tf_op jit(solution)/shard_map/ppermute | solution.py:539
  109.5 21.0 %all-to-all-start.4 = ((bf16[16,80,256]{2,1,0:T(8,128)(2,1)}), bf16[16,80,256]{2,1,0:T(8,128)(2,1)S(1)}, u32[]{:S(2)}, u32[]{:S(2)}) async-start(bf16[16,80,256]{2,1,0:T(8,128)(2,1)} %get-tuple-element.97), calls=%async_computation.4 | async-start | bytes 1310720 | tf_op jit(solution)/shard_map/all_to_all | solution.py:491
  130.6 22.7 %copy-start.3 = (bf16[16,80,256]{2,1,0:T(8,128)(2,1)}, bf16[16,80,256]{2,1,0:T(8,128)(2,1)S(1)}, u32[]{:S(2)}) copy-start(bf16[16,80,256]{2,1,0:T(8,128)(2,1)S(1)} %all-to-all-done.4.a_ref) | copy-start | bytes 1966084
  130.6 24.8 %all-to-all-start.3 = ((bf16[16,200,128]{2,1,0:T(8,128)(2,1)}), bf16[16,200,128]{2,1,0:T(8,128)(2,1)S(1)}, u32[]{:S(2)}, u32[]{:S(2)}) async-start(bf16[16,200,128]{2,1,0:T(8,128)(2,1)} %grads_b.1), calls=%async_computation.3 | async-start | bytes 1638400 | tf_op jit(solution)/shard_map/all_to_all | solution.py:491
  135.2 17.0 %collective-permute-start.14 = (f32[40,1280]{1,0:T(8,128)S(1)}, f32[40,1280]{1,0:T(8,128)S(1)}, u32[]{:S(2)}, u32[]{:S(2)}) collective-permute-start(f32[40,1280]{1,0:T(8,128)S(1)} %add_add_fusion), channel_id=1, source_target_pairs={{0,128},{128,0},{1,129},{129,1},{2,130},{130,2},{3,131},{131,3},{4... | collective-permute-start | bytes 614408 | tf_op jit(solution)/shard_map/ppermute | solution.py:542
  152.3 3.0 %collective-permute-start.15 = (f32[40,1280]{1,0:T(8,128)S(1)}, f32[40,1280]{1,0:T(8,128)S(1)}, u32[]{:S(2)}, u32[]{:S(2)}) collective-permute-start(f32[40,1280]{1,0:T(8,128)S(1)} %add.148.w_own), channel_id=1, source_target_pairs={{0,16},{16,0},{1,17},{17,1},{2,18},{18,2},{3,19},{19,3},{4,20},{20... | collective-permute-start | bytes 614408 | tf_op jit(solution)/shard_map/ppermute | solution.py:544
  (15 other events, 117.1 us)

commit v3 on v2

--- a/solution.py
+++ b/solution.py
@@ -22,7 +22,7 @@
 D = 1280
 SCALE = HD**-0.5
 LOG2E = 1.4426950408889634
-VMEM_LIMIT = 56 * 1024 * 1024
+VMEM_LIMIT = 28 * 1024 * 1024
 SEQ = ("yh", "x", "c")
 DP = ("yl", "z")
 OFFSETS = (0, -1, 1, -2, 2, -3, 3, -4)
@@ -192,14 +192,13 @@
     return jnp.max(m, axis=0, keepdims=True), jnp.sum(total, axis=0, keepdims=True)
 
 
-def prepare_body(x_ref, qt_ref, kn_ref, qn_ref, kt_ref, vn_ref):
+def prepare_body(x_ref, qt_ref, kn_ref, kt_ref, vn_ref):
     ones = jnp.concatenate([jnp.ones((8, 128), F32), jnp.zeros((8, 128), F32)], axis=0)
 
     def put(a, pieces):
         q = joined([piece(x_ref, s, slice(0, HD), 0, small) for s, small in pieces])
         k = joined([piece(x_ref, s, slice(0, HD), 1, small) for s, small in pieces])
         qt_ref[:, a : a + 128] = q
-        qn_ref[a : a + 128, :] = q.T
         kt_ref[:, a : a + 128] = k
         kn_ref[a : a + 128, :] = k.T
         rows = slice(HD, HD + HALF)
@@ -217,7 +216,6 @@
         out_shape=[
             jax.ShapeDtypeStruct((HD, N), BF),
             jax.ShapeDtypeStruct((N, HD), BF),
-            jax.ShapeDtypeStruct((N, HD), BF),
             jax.ShapeDtypeStruct((HD, N), BF),
             jax.ShapeDtypeStruct((N, EXT), BF),
         ],
@@ -279,7 +277,7 @@
 CUT = 2048
 
 
-def grads_block(k0, rows, e1, e2, inv1, inv2, qn, kt, vn, dot_t, dot_n, acc):
+def grads_block(k0, rows, e1, e2, inv1, inv2, qt, kt, vn, dot_t, dot_n, acc):
     v = vn[pl.ds(k0, rows), :]
     k = kt[:, pl.ds(k0, rows)]
     dv = dk = None
@@ -287,15 +285,15 @@
         e = e_ref[...]
         dp = dot(v, dot_t[:, sl], 1, 0)
         ds = (e.astype(F32) * dp * inv[0:1, :]).astype(BF)
-        v_part = dot(e, dot_n[sl, :], 1, 0)
-        k_part = dot(ds, qn[sl, :], 1, 0)
+        v_part = dot(e, dot_n[:, sl], 1, 1)
+        k_part = dot(ds, qt[:, sl], 1, 1)
         dv = v_part if dv is None else dv + v_part
         dk = k_part if dk is None else dk + k_part
         acc[:, sl] += dot(k, ds, 1, 0)
     return dv.T.astype(BF), (dk * SCALE).T.astype(BF)
 
 
-def grads_a_body(rows, x_ref, e1, e2, inv1, inv2, qn_ref, kt_ref, vn_ref, out_ref, dq_ref, dot_t, dot_n):
+def grads_a_body(rows, x_ref, e1, e2, inv1, inv2, qt_ref, kt_ref, vn_ref, out_ref, dq_ref, dot_t, dot_n):
     i = pl.program_id(0)
 
     @pl.when(i == 0)
@@ -317,21 +315,21 @@
             t = joined(sums)
             dot_t[:, a : a + 128] = jnp.concatenate([f, t, jnp.zeros((8, 128), F32)], axis=0).astype(BF)
             inv = inv1[0:1, a : a + 128] if a < CUT else inv2[0:1, a - CUT : a - CUT + 128]
-            dot_n[a : a + 128, :] = (f * inv).T.astype(BF)
+            dot_n[:, a : a + 128] = (f * inv).astype(BF)
 
         each_place(put)
         dq_ref[...] = jnp.zeros_like(dq_ref)
 
     k0 = pl.multiple_of(i * rows, 128)
     dv, dk = grads_block(
-        k0, rows, e1, e2, inv1, inv2, qn_ref, kt_ref, vn_ref, dot_t, dot_n, dq_ref
+        k0, rows, e1, e2, inv1, inv2, qt_ref, kt_ref, vn_ref, dot_t, dot_n, dq_ref
     )
     for j in range(rows // BIG):
         out_ref[j, 0:HD, 0:BIG] = dv[:, j * BIG : (j + 1) * BIG]
         out_ref[j, 0:HD, BIG : 2 * BIG] = dk[:, j * BIG : (j + 1) * BIG]
 
 
-def grads_a(dout, e1, e2, inv1, inv2, qn, kt, vn, rows=256):
+def grads_a(dout, e1, e2, inv1, inv2, qt, kt, vn, rows=512):
     return pl.pallas_call(
         functools.partial(grads_a_body, rows),
         grid=(SRC * BIG // rows,),
@@ -341,7 +339,7 @@
             pl.BlockSpec((rows, N - CUT), lambda i: (i, 0)),
             whole(8, CUT),
             whole(8, N - CUT),
-            whole(N, HD),
+            whole(HD, N),
             whole(HD, N),
             whole(N, EXT),
         ],
@@ -349,21 +347,21 @@
             pl.BlockSpec((rows // BIG, HD, 2 * BIG), lambda i: (i, 0, 0)),
             whole(HD, N),
             whole(EXT, N),
-            whole(N, HD),
+            whole(HD, N),
         ],
         out_shape=[
             jax.ShapeDtypeStruct((SRC, HD, 2 * BIG), BF),
             jax.ShapeDtypeStruct((HD, N), F32),
             jax.ShapeDtypeStruct((EXT, N), BF),
-            jax.ShapeDtypeStruct((N, HD), BF),
+            jax.ShapeDtypeStruct((HD, N), BF),
         ],
         compiler_params=params(),
         cost_estimate=cost(8 * N * SRC * BIG * HD, 18 * 10**6),
         name="grads_a",
-    )(dout, e1, e2, inv1, inv2, qn, kt, vn)
-
-
-def grads_b_body(rows, e1, e2, inv1, inv2, qn_ref, kt_ref, vn_ref, dot_t, dot_n, dq_ref, out_ref, acc):
+    )(dout, e1, e2, inv1, inv2, qt, kt, vn)
+
+
+def grads_b_body(rows, e1, e2, inv1, inv2, qt_ref, kt_ref, vn_ref, dot_t, dot_n, dq_ref, out_ref, acc):
     i = pl.program_id(0)
     base = SRC * BIG
 
@@ -373,7 +371,7 @@
 
     k0 = pl.multiple_of(base + i * rows, 128)
     dv, dk = grads_block(
-        k0, rows, e1, e2, inv1, inv2, qn_ref, kt_ref, vn_ref, dot_t, dot_n, acc
+        k0, rows, e1, e2, inv1, inv2, qt_ref, kt_ref, vn_ref, dot_t, dot_n, acc
     )
     for j in range(rows // SMALL):
         a = j * SMALL
@@ -392,7 +390,7 @@
             ).astype(BF)
 
 
-def grads_b(e1, e2, inv1, inv2, qn, kt, vn, dot_t, dot_n, dq, rows=256):
+def grads_b(e1, e2, inv1, inv2, qt, kt, vn, dot_t, dot_n, dq, rows=512):
     off = SRC * BIG // rows
     return pl.pallas_call(
         functools.partial(grads_b_body, rows),
@@ -402,11 +400,11 @@
             pl.BlockSpec((rows, N - CUT), lambda i: (i + off, 0)),
             whole(8, CUT),
             whole(8, N - CUT),
-            whole(N, HD),
+            whole(HD, N),
             whole(HD, N),
             whole(N, EXT),
             whole(EXT, N),
-            whole(N, HD),
+            whole(HD, N),
             whole(HD, N),
         ],
         out_specs=whole(SRC, 200, 128),
@@ -415,7 +413,7 @@
         compiler_params=params(),
         cost_estimate=cost(8 * N * SRC * SMALL * HD, 11 * 10**6),
         name="grads_b",
-    )(e1, e2, inv1, inv2, qn, kt, vn, dot_t, dot_n, dq)
+    )(e1, e2, inv1, inv2, qt, kt, vn, dot_t, dot_n, dq)
 
 
 def patch_rows(ref, sl, lanes):
@@ -522,25 +520,26 @@
     dout, qkv = hold((dout, qkv))
     dout = exchange(dout)
 
-    qt, kn, qn, kt, vn = prepare(qkv)
+    qt, kn, kt, vn = prepare(qkv)
     e1, inv1 = scores(qt, kn, 0, CUT)
     came, qt, inv1 = hold((came, qt, inv1))
     part = (keep.astype(F32) + came.astype(F32)).astype(BF)
     part, dout, qt = hold((part, dout, qt))
     part = lax.all_to_all(part, "z", 0, 0, tiled=True)
     e2, inv2 = scores(qt, kn, CUT, N)
-    first, dq, dot_t, dot_n = grads_a(dout, e1, e2, inv1, inv2, qn, kt, vn)
+    first, dq, dot_t, dot_n = grads_a(dout, e1, e2, inv1, inv2, qt, kt, vn)
     first, part = hold((first, part))
     first = exchange(first)
-    second = grads_b(e1, e2, inv1, inv2, qn, kt, vn, dot_t, dot_n, dq)
+    second = grads_b(e1, e2, inv1, inv2, qt, kt, vn, dot_t, dot_n, dq)
     mine = jnp.sum(part.astype(F32), axis=0)
     t = mine
     for k in range(1, 4):
         t = t + lax.ppermute(mine, "x", [(i, (i + k) % 4) for i in range(4)])
     second, t = hold((second, t))
     second = exchange(second)
-    u = t + lax.ppermute(t, "yh", swap)
-    d_keys, d_values = unpack_a(first)
+    other = lax.ppermute(t, "yh", swap)
+    other, d_keys, d_values = hold((other, *unpack_a(first)))
+    u = t + other
     return unpack_b(scalar(c), second, [u, lax.ppermute(u, "c", swap)], d_keys, d_values)
 
 

time: 160 us -> 179 us (1.12)
  local copies, waits for them, and re-layouts: 2.41 us -> 44.3 us
  Pallas kernels: 69.1 us -> 44.4 us
  waiting for transfers between devices: 26.8 us -> 22 us
  other arithmetic: 1.31 us -> 5.81 us
  starting transfers between devices: 58.4 us -> 60.4 us
    unnamed x36 -> x88, local copies, waits for them, and re-layouts: 1.71 us -> 44.2 us
    pallas_call x2, Pallas kernels: 18.6 us -> 13.3 us  [scores(): pl.pallas_call(functools.partial(scores_body, cols, chunk, begin, end), g...]
    pallas_call x1, Pallas kernels: 17.3 us -> 12.7 us  [grads_a(): pl.pallas_call(functools.partial(grads_a_body, rows), grid=(SRC * BIG //...]
    pallas_call x1, Pallas kernels: 10.8 us -> 7.63 us  [grads_b(): pl.pallas_call(functools.partial(grads_b_body, rows), grid=(SRC * SMALL /...]
    pallas_call x1, Pallas kernels: 4.34 us -> 1.16 us  [prepare(): pl.pallas_call(prepare_body, out_shape=[jax.ShapeDtypeStruct((HD, N), BF)...]
    all_to_all x4, waiting for transfers between devices: 2.61 us -> 0.01 us  [exchange(): return lax.all_to_all(x, SEQ, 0, 0, tiled=True)]
    reduce_sum x1, other arithmetic: 0.11 us -> 2.2 us  [body(): mine = jnp.sum(part.astype(F32), axis=0)]
    pallas_call x1, Pallas kernels: 4.16 us -> 2.11 us  [weight_share(): pl.pallas_call(weight_share_body, in_specs=[pl.BlockSpec(memory_space=plt...]
  transfers between devices with their start and end apart: 21 -> 21, of which waited for: 6 -> 4; matrix products, arithmetic and copies ran while one was open for 1% -> 2% of each run, Pallas kernels for 42% -> 24%
where the time goes in v3:
time: 179 us; the launch traced here: 178 us
  starting transfers between devices  60.4 us (34%)
  Pallas kernels  44.4 us (25%)
  local copies, waits for them, and re-layouts  44.3 us (25%)
  waiting for transfers between devices  22 us (12%)
  other arithmetic  5.81 us (3%)
    unnamed x88, local copies, waits for them, and re-layouts  44.2 us
    all_to_all x4, starting transfers between devices, exchange(): return lax.all_to_all(x, SEQ, 0, 0, tiled=True)  31.3 us
    pallas_call x2, Pallas kernels, scores(): pl.pallas_call(functools.partial(scores_body, cols, chunk, begin, end), g...  13.3 us
    ppermute x1, waiting for transfers between devices, body(): other = lax.ppermute(t, 'yh', swap)  13.2 us
    pallas_call x1, Pallas kernels, grads_a(): pl.pallas_call(functools.partial(grads_a_body, rows), grid=(SRC * BIG //...  12.7 us
    ppermute x3, starting transfers between devices, down(): return lax.ppermute(block, 'z', DOWN)  11 us
    ppermute x4, waiting for transfers between devices, up(): return lax.ppermute(block, 'z', UP)  7.72 us
    pallas_call x1, Pallas kernels, grads_b(): pl.pallas_call(functools.partial(grads_b_body, rows), grid=(SRC * SMALL /...  7.63 us
  transfers between devices with their start and end apart: 21, of which 4 were waited for; matrix products, arithmetic and copies ran while one was open for 2% of the time, Pallas kernels for 24%

profile of v3, /device:TPU:1, one launch (start us, length us, event | category | flops | bytes accessed | tf_op | source)
XLA Modules:
  0.0 177.8 jit_solution(2787770455648965196)
XLA Ops:
  0.6 3.3 %collective-permute-start.1 = (bf16[1,192,1280]{2,1,0:T(8,128)(2,1)}, bf16[1,192,1280]{2,1,0:T(8,128)(2,1)S(1)}, u32[]{:S(2)}, u32[]{:S(2)}) collective-permute-start(bf16[1,192,1280]{2,1,0:T(8,128)(2,1)} %g_own.1), channel_id=1, source_target_pairs={{0,16},{16,0},{1,17},{17,1},{2,18},{18,2},{3,19},{19,3},{4,20},{20... | collective-permute-start | bytes 1474568 | tf_op jit(solution)/shard_map/ppermute | solution.py:504
  9.9 5.3 %collective-permute-start.3 = (bf16[2,40,1280]{2,1,0:T(8,128)(2,1)S(1)}, bf16[2,40,1280]{2,1,0:T(8,128)(2,1)S(1)}, u32[]{:S(2)}, u32[]{:S(2)}) collective-permute-start(bf16[2,40,1280]{2,1,0:T(8,128)(2,1)S(1)} %pad_maximum_fusion.refs_0_), channel_id=1, source_target_pairs={{0,7},{1,0},{2,1},{3,2},{4,3},{5,4},{6,5},{7,6},{8,15},{9,8},{10,9... | collective-permute-start | bytes 614408 | tf_op jit(solution)/shard_map/ppermute | solution.py:500
  15.2 7.9 %all-to-all-start = ((bf16[16,120,384]{2,1,0:T(8,128)(2,1)}), bf16[16,120,384]{2,1,0:T(8,128)(2,1)S(1)}, u32[]{:S(2)}, u32[]{:S(2)}) async-start(bf16[16,120,384]{2,1,0:T(8,128)(2,1)} %pack_qkv.1), calls=%async_computation | async-start | bytes 2949120 | tf_op jit(solution)/shard_map/all_to_all | solution.py:489
  23.2 3.0 %collective-permute-start.5 = (bf16[2,40,1280]{2,1,0:T(8,128)(2,1)S(1)}, bf16[2,40,1280]{2,1,0:T(8,128)(2,1)S(1)}, u32[]{:S(2)}, u32[]{:S(2)}) collective-permute-start(bf16[2,40,1280]{2,1,0:T(8,128)(2,1)S(1)} %collective-permute-done.3.refs_2_), channel_id=1, source_target_pairs={{0,7},{1,0},{2,1},{3,2},{4,3},{5,4},{6,5},{7,6},{8,15},{9,8},{10,9... | collective-permute-start | bytes 614408 | tf_op jit(solution)/shard_map/ppermute | solution.py:500
  27.2 3.6 %collective-permute-done.4.refs_3_ = bf16[2,40,1280]{2,1,0:T(8,128)(2,1)S(1)} collective-permute-done((bf16[2,40,1280]{2,1,0:T(8,128)(2,1)S(1)}, bf16[2,40,1280]{2,1,0:T(8,128)(2,1)S(1)}, u32[]{:S(2)}, u32[]{:S(2)}) %collective-permute-start.4) | collective-permute-done | bytes 204832 | tf_op jit(solution)/shard_map/ppermute | solution.py:497
  32.8 2.8 %collective-permute-start.7 = (bf16[2,40,1280]{2,1,0:T(8,128)(2,1)S(1)}, bf16[2,40,1280]{2,1,0:T(8,128)(2,1)S(1)}, u32[]{:S(2)}, u32[]{:S(2)}) collective-permute-start(bf16[2,40,1280]{2,1,0:T(8,128)(2,1)S(1)} %collective-permute-done.5.refs_4_), channel_id=1, source_target_pairs={{0,7},{1,0},{2,1},{3,2},{4,3},{5,4},{6,5},{7,6},{8,15},{9,8},{10,9... | collective-permute-start | bytes 614408 | tf_op jit(solution)/shard_map/ppermute | solution.py:500
  36.3 4.1 %collective-permute-done.6.refs_5_ = bf16[2,40,1280]{2,1,0:T(8,128)(2,1)} collective-permute-done((bf16[2,40,1280]{2,1,0:T(8,128)(2,1)S(1)}, bf16[2,40,1280]{2,1,0:T(8,128)(2,1)}, u32[]{:S(2)}, u32[]{:S(2)}) %collective-permute-start.6) | collective-permute-done | bytes 204832 | tf_op jit(solution)/shard_map/ppermute | solution.py:497
  55.0 3.0 %out_grad.1 = bf16[16,48,384]{2,1,0:T(8,128)(2,1)} custom-call(s32[16]{0:T(128)S(1)} %stack.84.ids, bf16[2,40,1280]{2,1,0:T(8,128)(2,1)S(1)} %pad_maximum_fusion.refs_0_, bf16[2,40,1280]{2,1,0:T(8,128)(2,1)S(1)} %copy-done.26, bf16[2,40,1280]{2,1,0:T(8,128)(2,1)S(1)} %copy-done.24, bf16[2,40,1280]{2,1,0:T(8,128)(2,1)S(1)} %copy-done.28, ...), custom_call_target="tpu_custom_call" | custom-call | flops 629145600 | bytes 4000000 | tf_op jit(solution)/shard_map/out_grad/pallas_call | solution.py:150
  58.0 8.7 %all-to-all-start.1 = ((bf16[16,48,384]{2,1,0:T(8,128)(2,1)}), bf16[16,48,384]{2,1,0:T(8,128)(2,1)S(1)}, u32[]{:S(2)}, u32[]{:S(2)}) async-start(bf16[16,48,384]{2,1,0:T(8,128)(2,1)} %out_grad.1), calls=%async_computation.1 | async-start | bytes 1179648 | tf_op jit(solution)/shard_map/all_to_all | solution.py:489
  67.8 8.7 %scores.2 = (bf16[3072,2048]{1,0:T(8,128)(2,1)S(1)}, f32[8,2048]{1,0:T(8,128)S(1)}) custom-call(bf16[80,3072]{1,0:T(8,128)(2,1)S(1)} %get-tuple-element.83.qt.qt_ref, bf16[3072,80]{1,0:T(8,128)(2,1)S(1)} %get-tuple-element.75.kn), custom_call_target="tpu_custom_call" | custom-call | flops 1006632960 | bytes 12582912 | tf_op jit(solution)/shard_map/scores/pallas_call | solution.py:254
  76.6 4.6 %copy-done.1 = bf16[3072,2048]{1,0:T(8,128)(2,1)} copy-done((bf16[3072,2048]{1,0:T(8,128)(2,1)}, bf16[3072,2048]{1,0:T(8,128)(2,1)S(1)}, u32[]{:S(2)}) %copy-start.1) | copy-done | bytes 12582936
  83.4 4.3 %all-to-all-start.2 = ((bf16[8,40,1280]{2,1,0:T(8,128)(2,1)}), bf16[8,40,1280]{2,1,0:T(8,128)(2,1)}, u32[]{:S(2)}, u32[]{:S(2)}) async-start(bf16[8,40,1280]{2,1,0:T(8,128)(2,1)} %add_convert_fusion), calls=%async_computation.2 | async-start | bytes 1638400 | tf_op jit(solution)/shard_map/all_to_all | solution.py:528
  88.8 4.6 %scores.3 = (bf16[3072,1024]{1,0:T(8,128)(2,1)S(1)}, f32[8,1024]{1,0:T(8,128)S(1)}) custom-call(bf16[80,3072]{1,0:T(8,128)(2,1)S(1)} %get-tuple-element.83.qt.qt_ref, bf16[3072,80]{1,0:T(8,128)(2,1)S(1)} %copy-done.36), custom_call_target="tpu_custom_call" | custom-call | flops 503316480 | bytes 6291456 | tf_op jit(solution)/shard_map/scores/pallas_call | solution.py:254
  93.5 4.6 %copy-done.2 = bf16[3072,2048]{1,0:T(8,128)(2,1)S(1)} copy-done((bf16[3072,2048]{1,0:T(8,128)(2,1)S(1)}, bf16[3072,2048]{1,0:T(8,128)(2,1)}, u32[]{:S(2)}) %copy-start.2) | copy-done | bytes 12582936
  98.1 12.7 %grads_a.1 = (bf16[16,80,256]{2,1,0:T(8,128)(2,1)S(1)}, f32[80,3072]{1,0:T(8,128)S(1)}, bf16[96,3072]{1,0:T(8,128)(2,1)S(1)}, bf16[80,3072]{1,0:T(8,128)(2,1)S(1)}) custom-call(bf16[16,48,384]{2,1,0:T(8,128)(2,1)S(1)} %all-to-all-done.1.x_ref, bf16[3072,2048]{1,0:T(8,128)(2,1)S(1)} %copy-done.2, bf16[3072,1024]{1,0:T(8,128)(2,1)S(1)} %get-tuple-element.84.e2, ...), custom_call_target="tpu_custom_call" | custom-call | flops 4026531840 | bytes 18000000 | tf_op jit(solution)/shard_map/grads_a/pallas_call | solution.py:333
  110.8 2.6 %copy-done.4 = bf16[3072,1024]{1,0:T(8,128)(2,1)} copy-done((bf16[3072,1024]{1,0:T(8,128)(2,1)}, bf16[3072,1024]{1,0:T(8,128)(2,1)S(1)}, u32[]{:S(2)}) %copy-start.4) | copy-done | bytes 6291480
  118.8 2.6 %collective-permute-start.13 = (f32[40,1280]{1,0:T(8,128)}, f32[40,1280]{1,0:T(8,128)}, u32[]{:S(2)}, u32[]{:S(2)}) collective-permute-start(f32[40,1280]{1,0:T(8,128)} %convert_reduce_fusion), channel_id=1, source_target_pairs={{0,96},{32,0},{64,32},{96,64},{1,97},{33,1},{65,33},{97,65},{2,98}... | collective-permute-start | bytes 614408 | tf_op jit(solution)/shard_map/ppermute | solution.py:537
  122.5 7.6 %all-to-all-start.4 = ((bf16[16,80,256]{2,1,0:T(8,128)(2,1)}), bf16[16,80,256]{2,1,0:T(8,128)(2,1)S(1)}, u32[]{:S(2)}, u32[]{:S(2)}) async-start(bf16[16,80,256]{2,1,0:T(8,128)(2,1)} %copy-done.12), calls=%async_computation.4 | async-start | bytes 1310720 | tf_op jit(solution)/shard_map/all_to_all | solution.py:489
  130.1 4.6 %copy-done.3 = bf16[3072,2048]{1,0:T(8,128)(2,1)S(1)} copy-done((bf16[3072,2048]{1,0:T(8,128)(2,1)S(1)}, bf16[3072,2048]{1,0:T(8,128)(2,1)}, u32[]{:S(2)}) %copy-start.3) | copy-done | bytes 12582936
  134.7 2.8 %copy-done.5 = bf16[3072,1024]{1,0:T(8,128)(2,1)S(1)} copy-done((bf16[3072,1024]{1,0:T(8,128)(2,1)S(1)}, bf16[3072,1024]{1,0:T(8,128)(2,1)}, u32[]{:S(2)}) %copy-start.5) | copy-done | bytes 6291480
  141.3 7.6 %grads_b.1 = bf16[16,200,128]{2,1,0:T(8,128)(2,1)} custom-call(bf16[3072,2048]{1,0:T(8,128)(2,1)S(1)} %copy-done.3, bf16[3072,1024]{1,0:T(8,128)(2,1)S(1)} %copy-done.5, f32[8,2048]{1,0:T(8,128)S(1)} %copy-done.22, f32[8,1024]{1,0:T(8,128)S(1)} %copy-done.34, bf16[80,3072]{1,0:T(8,128)(2,1)S(1)} %get-tuple-element.83.qt.qt_ref, ...), custom_call_target="tpu_custom_call" | custom-call | flops 2013265920 | bytes 11000000 | tf_op jit(solution)/shard_map/grads_b/pallas_call | solution.py:395
  150.2 7.2 %all-to-all-start.3 = ((bf16[16,200,128]{2,1,0:T(8,128)(2,1)}), bf16[16,200,128]{2,1,0:T(8,128)(2,1)S(1)}, u32[]{:S(2)}, u32[]{:S(2)}) async-start(bf16[16,200,128]{2,1,0:T(8,128)(2,1)} %grads_b.1), calls=%async_computation.3 | async-start | bytes 1638400 | tf_op jit(solution)/shard_map/all_to_all | solution.py:489
  157.4 2.9 %collective-permute-start.14 = (f32[40,1280]{1,0:T(8,128)S(1)}, f32[40,1280]{1,0:T(8,128)S(1)}, u32[]{:S(2)}, u32[]{:S(2)}) collective-permute-start(f32[40,1280]{1,0:T(8,128)S(1)} %add_add_fusion), channel_id=1, source_target_pairs={{0,128},{128,0},{1,129},{129,1},{2,130},{130,2},{3,131},{131,3},{4... | collective-permute-start | bytes 614408 | tf_op jit(solution)/shard_map/ppermute | solution.py:540
  161.3 13.2 %collective-permute-done.14 = f32[40,1280]{1,0:T(8,128)S(1)} collective-permute-done((f32[40,1280]{1,0:T(8,128)S(1)}, f32[40,1280]{1,0:T(8,128)S(1)}, u32[]{:S(2)}, u32[]{:S(2)}) %collective-permute-start.14) | collective-permute-done | bytes 204832 | tf_op jit(solution)/shard_map/ppermute | solution.py:540
  (125 shorter events, 44.8 us)
Async XLA Ops:
  0.6 8.5 %collective-permute-start.1 = (bf16[1,192,1280]{2,1,0:T(8,128)(2,1)}, bf16[1,192,1280]{2,1,0:T(8,128)(2,1)S(1)}, u32[]{:S(2)}, u32[]{:S(2)}) collective-permute-start(bf16[1,192,1280]{2,1,0:T(8,128)(2,1)} %g_own.1), channel_id=1, source_target_pairs={{0,16},{16,0},{1,17},{17,1},{2,18},{18,2},{3,19},{19,3},{4,20},{20... | collective-permute-start | bytes 1474568 | tf_op jit(solution)/shard_map/ppermute | solution.py:504
  4.0 5.1 %collective-permute-start = (bf16[40,1280]{1,0:T(8,128)(2,1)S(1)}, bf16[40,1280]{1,0:T(8,128)(2,1)S(1)}, u32[]{:S(2)}, u32[]{:S(2)}) collective-permute-start(bf16[40,1280]{1,0:T(8,128)(2,1)S(1)} %constant_dynamic-slice_fusion), channel_id=1, source_target_pairs={{0,8},{8,0},{1,9},{9,1},{2,10},{10,2},{3,11},{11,3},{4,12},{12,4},... | collective-permute-start | bytes 307208 | tf_op jit(solution)/shard_map/ppermute | solution.py:503
  9.1 17.1 %copy-start.18 = (bf16[1,192,1280]{2,1,0:T(8,128)(2,1)S(1)}, bf16[1,192,1280]{2,1,0:T(8,128)(2,1)}, u32[]{:S(2)}) copy-start(bf16[1,192,1280]{2,1,0:T(8,128)(2,1)} %a_ref) | copy-start | bytes 1474564
  9.9 13.2 %collective-permute-start.3 = (bf16[2,40,1280]{2,1,0:T(8,128)(2,1)S(1)}, bf16[2,40,1280]{2,1,0:T(8,128)(2,1)S(1)}, u32[]{:S(2)}, u32[]{:S(2)}) collective-permute-start(bf16[2,40,1280]{2,1,0:T(8,128)(2,1)S(1)} %pad_maximum_fusion.refs_0_), channel_id=1, source_target_pairs={{0,7},{1,0},{2,1},{3,2},{4,3},{5,4},{6,5},{7,6},{8,15},{9,8},{10,9... | collective-permute-start | bytes 614408 | tf_op jit(solution)/shard_map/ppermute | solution.py:500
  15.1 7.9 %collective-permute-start.2 = (bf16[2,40,1280]{2,1,0:T(8,128)(2,1)S(1)}, bf16[2,40,1280]{2,1,0:T(8,128)(2,1)S(1)}, u32[]{:S(2)}, u32[]{:S(2)}) collective-permute-start(bf16[2,40,1280]{2,1,0:T(8,128)(2,1)S(1)} %pad_maximum_fusion.refs_0_), channel_id=1, source_target_pairs={{0,1},{1,2},{2,3},{3,4},{4,5},{5,6},{6,7},{7,0},{8,9},{9,10},{10,1... | collective-permute-start | bytes 614408 | tf_op jit(solution)/shard_map/ppermute | solution.py:497
  15.2 42.8 %all-to-all-start = ((bf16[16,120,384]{2,1,0:T(8,128)(2,1)}), bf16[16,120,384]{2,1,0:T(8,128)(2,1)S(1)}, u32[]{:S(2)}, u32[]{:S(2)}) async-start(bf16[16,120,384]{2,1,0:T(8,128)(2,1)} %pack_qkv.1), calls=%async_computation | async-start | bytes 2949120 | tf_op jit(solution)/shard_map/all_to_all | solution.py:489
  23.0 20.1 %copy-start.23 = (bf16[2,40,1280]{2,1,0:T(8,128)(2,1)}, bf16[2,40,1280]{2,1,0:T(8,128)(2,1)S(1)}, u32[]{:S(2)}) copy-start(bf16[2,40,1280]{2,1,0:T(8,128)(2,1)S(1)} %collective-permute-done.3.refs_2_) | copy-start | bytes 614404
  23.1 20.1 %copy-start.25 = (bf16[2,40,1280]{2,1,0:T(8,128)(2,1)}, bf16[2,40,1280]{2,1,0:T(8,128)(2,1)S(1)}, u32[]{:S(2)}) copy-start(bf16[2,40,1280]{2,1,0:T(8,128)(2,1)S(1)} %collective-permute-done.2.refs_1_) | copy-start | bytes 614404
  23.1 7.8 %collective-permute-start.4 = (bf16[2,40,1280]{2,1,0:T(8,128)(2,1)S(1)}, bf16[2,40,1280]{2,1,0:T(8,128)(2,1)S(1)}, u32[]{:S(2)}, u32[]{:S(2)}) collective-permute-start(bf16[2,40,1280]{2,1,0:T(8,128)(2,1)S(1)} %collective-permute-done.2.refs_1_), channel_id=1, source_target_pairs={{0,1},{1,2},{2,3},{3,4},{4,5},{5,6},{6,7},{7,0},{8,9},{9,10},{10,1... | collective-permute-start | bytes 614408 | tf_op jit(solution)/shard_map/ppermute | solution.py:497
  23.2 7.7 %collective-permute-start.5 = (bf16[2,40,1280]{2,1,0:T(8,128)(2,1)S(1)}, bf16[2,40,1280]{2,1,0:T(8,128)(2,1)S(1)}, u32[]{:S(2)}, u32[]{:S(2)}) collective-permute-start(bf16[2,40,1280]{2,1,0:T(8,128)(2,1)S(1)} %collective-permute-done.3.refs_2_), channel_id=1, source_target_pairs={{0,7},{1,0},{2,1},{3,2},{4,3},{5,4},{6,5},{7,6},{8,15},{9,8},{10,9... | collective-permute-start | bytes 614408 | tf_op jit(solution)/shard_map/ppermute | solution.py:500
  30.9 10.2 %collective-permute-start.8 = (bf16[16,40,192]{2,1,0:T(8,128)(2,1)S(1)}, bf16[16,40,192]{2,1,0:T(8,128)(2,1)S(1)}, u32[]{:S(2)}, u32[]{:S(2)}) collective-permute-start(bf16[16,40,192]{2,1,0:T(8,128)(2,1)S(1)} %get-tuple-element.62), channel_id=1, source_target_pairs={{0,16},{16,0},{1,17},{17,1},{2,18},{18,2},{3,19},{19,3},{4,20},{20... | collective-permute-start | bytes 737288 | tf_op jit(solution)/shard_map/ppermute | solution.py:511
  32.1 8.2 %collective-permute-start.6 = (bf16[2,40,1280]{2,1,0:T(8,128)(2,1)S(1)}, bf16[2,40,1280]{2,1,0:T(8,128)(2,1)}, u32[]{:S(2)}, u32[]{:S(2)}) collective-permute-start(bf16[2,40,1280]{2,1,0:T(8,128)(2,1)S(1)} %collective-permute-done.4.refs_3_), channel_id=1, source_target_pairs={{0,1},{1,2},{2,3},{3,4},{4,5},{5,6},{6,7},{7,0},{8,9},{9,10},{10,1... | collective-permute-start | bytes 614408 | tf_op jit(solution)/shard_map/ppermute | solution.py:497
  32.8 7.5 %collective-permute-start.7 = (bf16[2,40,1280]{2,1,0:T(8,128)(2,1)S(1)}, bf16[2,40,1280]{2,1,0:T(8,128)(2,1)S(1)}, u32[]{:S(2)}, u32[]{:S(2)}) collective-permute-start(bf16[2,40,1280]{2,1,0:T(8,128)(2,1)S(1)} %collective-permute-done.5.refs_4_), channel_id=1, source_target_pairs={{0,7},{1,0},{2,1},{3,2},{4,3},{5,4},{6,5},{7,6},{8,15},{9,8},{10,9... | collective-permute-start | bytes 614408 | tf_op jit(solution)/shard_map/ppermute | solution.py:500
  41.8 8.4 %collective-permute-start.9 = (bf16[2,40,1280]{2,1,0:T(8,128)(2,1)}, bf16[2,40,1280]{2,1,0:T(8,128)(2,1)}, u32[]{:S(2)}, u32[]{:S(2)}) collective-permute-start(bf16[2,40,1280]{2,1,0:T(8,128)(2,1)} %collective-permute-done.6.refs_5_), channel_id=1, source_target_pairs={{0,1},{1,2},{2,3},{3,4},{4,5},{5,6},{6,7},{7,0},{8,9},{9,10},{10,1... | collective-permute-start | bytes 614408 | tf_op jit(solution)/shard_map/ppermute | solution.py:497
  50.2 30.9 %collective-permute-start.10 = (bf16[8,40,1280]{2,1,0:T(8,128)(2,1)}, bf16[8,40,1280]{2,1,0:T(8,128)(2,1)}, u32[]{:S(2)}, u32[]{:S(2)}) collective-permute-start(bf16[8,40,1280]{2,1,0:T(8,128)(2,1)} %get-tuple-element.78), channel_id=1, source_target_pairs={{0,8},{8,0},{1,9},{9,1},{2,10},{10,2},{3,11},{11,3},{4,12},{12,4},... | collective-permute-start | bytes 2457608 | tf_op jit(solution)/shard_map/ppermute | solution.py:515
  58.0 25.5 %all-to-all-start.1 = ((bf16[16,48,384]{2,1,0:T(8,128)(2,1)}), bf16[16,48,384]{2,1,0:T(8,128)(2,1)S(1)}, u32[]{:S(2)}, u32[]{:S(2)}) async-start(bf16[16,48,384]{2,1,0:T(8,128)(2,1)} %out_grad.1), calls=%async_computation.1 | async-start | bytes 1179648 | tf_op jit(solution)/shard_map/all_to_all | solution.py:489
  83.4 33.1 %all-to-all-start.2 = ((bf16[8,40,1280]{2,1,0:T(8,128)(2,1)}), bf16[8,40,1280]{2,1,0:T(8,128)(2,1)}, u32[]{:S(2)}, u32[]{:S(2)}) async-start(bf16[8,40,1280]{2,1,0:T(8,128)(2,1)} %add_convert_fusion), calls=%async_computation.2 | async-start | bytes 1638400 | tf_op jit(solution)/shard_map/all_to_all | solution.py:528
  118.8 30.1 %collective-permute-start.13 = (f32[40,1280]{1,0:T(8,128)}, f32[40,1280]{1,0:T(8,128)}, u32[]{:S(2)}, u32[]{:S(2)}) collective-permute-start(f32[40,1280]{1,0:T(8,128)} %convert_reduce_fusion), channel_id=1, source_target_pairs={{0,96},{32,0},{64,32},{96,64},{1,97},{33,1},{65,33},{97,65},{2,98}... | collective-permute-start | bytes 614408 | tf_op jit(solution)/shard_map/ppermute | solution.py:537
  121.4 27.6 %collective-permute-start.12 = (f32[40,1280]{1,0:T(8,128)}, f32[40,1280]{1,0:T(8,128)}, u32[]{:S(2)}, u32[]{:S(2)}) collective-permute-start(f32[40,1280]{1,0:T(8,128)} %convert_reduce_fusion), channel_id=1, source_target_pairs={{0,64},{32,96},{64,0},{96,32},{1,65},{33,97},{65,1},{97,33},{2,66}... | collective-permute-start | bytes 614408 | tf_op jit(solution)/shard_map/ppermute | solution.py:537
  121.9 27.0 %collective-permute-start.11 = (f32[40,1280]{1,0:T(8,128)}, f32[40,1280]{1,0:T(8,128)}, u32[]{:S(2)}, u32[]{:S(2)}) collective-permute-start(f32[40,1280]{1,0:T(8,128)} %convert_reduce_fusion), channel_id=1, source_target_pairs={{0,32},{32,64},{64,96},{96,0},{1,33},{33,65},{65,97},{97,1},{2,34}... | collective-permute-start | bytes 614408 | tf_op jit(solution)/shard_map/ppermute | solution.py:537
  122.5 27.7 %all-to-all-start.4 = ((bf16[16,80,256]{2,1,0:T(8,128)(2,1)}), bf16[16,80,256]{2,1,0:T(8,128)(2,1)S(1)}, u32[]{:S(2)}, u32[]{:S(2)}) async-start(bf16[16,80,256]{2,1,0:T(8,128)(2,1)} %copy-done.12), calls=%async_computation.4 | async-start | bytes 1310720 | tf_op jit(solution)/shard_map/all_to_all | solution.py:489
  150.2 26.3 %all-to-all-start.3 = ((bf16[16,200,128]{2,1,0:T(8,128)(2,1)}), bf16[16,200,128]{2,1,0:T(8,128)(2,1)S(1)}, u32[]{:S(2)}, u32[]{:S(2)}) async-start(bf16[16,200,128]{2,1,0:T(8,128)(2,1)} %grads_b.1), calls=%async_computation.3 | async-start | bytes 1638400 | tf_op jit(solution)/shard_map/all_to_all | solution.py:489
  157.4 17.0 %collective-permute-start.14 = (f32[40,1280]{1,0:T(8,128)S(1)}, f32[40,1280]{1,0:T(8,128)S(1)}, u32[]{:S(2)}, u32[]{:S(2)}) collective-permute-start(f32[40,1280]{1,0:T(8,128)S(1)} %add_add_fusion), channel_id=1, source_target_pairs={{0,128},{128,0},{1,129},{129,1},{2,130},{130,2},{3,131},{131,3},{4... | collective-permute-start | bytes 614408 | tf_op jit(solution)/shard_map/ppermute | solution.py:540
  174.5 2.0 %collective-permute-start.15 = (f32[40,1280]{1,0:T(8,128)S(1)}, f32[40,1280]{1,0:T(8,128)S(1)}, u32[]{:S(2)}, u32[]{:S(2)}) collective-permute-start(f32[40,1280]{1,0:T(8,128)S(1)} %add.148.w_own), channel_id=1, source_target_pairs={{0,16},{16,0},{1,17},{17,1},{2,18},{18,2},{3,19},{19,3},{4,20},{20... | collective-permute-start | bytes 614408 | tf_op jit(solution)/shard_map/ppermute | solution.py:543
  (41 other events, 114.2 us)

commit v4 on v3

--- a/solution.py
+++ b/solution.py
@@ -22,7 +22,7 @@
 D = 1280
 SCALE = HD**-0.5
 LOG2E = 1.4426950408889634
-VMEM_LIMIT = 28 * 1024 * 1024
+VMEM_LIMIT = 56 * 1024 * 1024
 SEQ = ("yh", "x", "c")
 DP = ("yl", "z")
 OFFSETS = (0, -1, 1, -2, 2, -3, 3, -4)
@@ -192,13 +192,12 @@
     return jnp.max(m, axis=0, keepdims=True), jnp.sum(total, axis=0, keepdims=True)
 
 
-def prepare_body(x_ref, qt_ref, kn_ref, kt_ref, vn_ref):
+def prepare(x_ref, qt_ref, kn_ref, kt_ref, vn_ref):
     ones = jnp.concatenate([jnp.ones((8, 128), F32), jnp.zeros((8, 128), F32)], axis=0)
 
     def put(a, pieces):
-        q = joined([piece(x_ref, s, slice(0, HD), 0, small) for s, small in pieces])
+        qt_ref[:, a : a + 128] = joined([piece(x_ref, s, slice(0, HD), 0, small) for s, small in pieces])
         k = joined([piece(x_ref, s, slice(0, HD), 1, small) for s, small in pieces])
-        qt_ref[:, a : a + 128] = q
         kt_ref[:, a : a + 128] = k
         kn_ref[a : a + 128, :] = k.T
         rows = slice(HD, HD + HALF)
@@ -210,22 +209,7 @@
     each_place(put)
 
 
-def prepare(qkv):
-    return pl.pallas_call(
-        prepare_body,
-        out_shape=[
-            jax.ShapeDtypeStruct((HD, N), BF),
-            jax.ShapeDtypeStruct((N, HD), BF),
-            jax.ShapeDtypeStruct((HD, N), BF),
-            jax.ShapeDtypeStruct((N, EXT), BF),
-        ],
-        compiler_params=params(),
-        cost_estimate=cost(0, 5 * 10**6),
-        name="prepare",
-    )(qkv)
-
-
-def scores_body(cols, chunk, begin, end, qt, kn, e_ref, inv_ref, sa, sb, ma):
+def scores_step(cols, chunk, begin, end, qt, kn, e_ref, inv_ref, sa, sb, ma):
     i = pl.program_id(0)
 
     @pl.when(i == 0)
@@ -249,29 +233,51 @@
     inv_ref[...] = jnp.broadcast_to(1.0 / jnp.concatenate([l0, l1], axis=1), (8, 2 * cols))
 
 
-def scores(qt, kn, begin, end, cols=256, chunk=128):
-    size = end - begin
-    return pl.pallas_call(
-        functools.partial(scores_body, cols, chunk, begin, end),
+def scores_a_body(cols, chunk, x_ref, e_ref, inv_ref, qt, kn, kt_ref, vn_ref, sa, sb, ma):
+    @pl.when(pl.program_id(0) == 0)
+    def _():
+        prepare(x_ref, qt, kn, kt_ref, vn_ref)
+
+    scores_step(cols, chunk, 0, CUT, qt, kn, e_ref, inv_ref, sa, sb, ma)
+
+
+def scores_b_body(cols, chunk, qt, kn, e_ref, inv_ref, sa, sb, ma):
+    scores_step(cols, chunk, CUT, N, qt, kn, e_ref, inv_ref, sa, sb, ma)
+
+
+def scores_call(body, name, size, more, operands, cols=256):
+    return pl.pallas_call(
+        body,
         grid=(size // cols // 2,),
-        in_specs=[whole(HD, N), whole(N, HD)],
+        in_specs=[whole(*x.shape) for x in operands],
         out_specs=[
             pl.BlockSpec((N, 2 * cols), lambda i: (0, i)),
             pl.BlockSpec((8, 2 * cols), lambda i: (0, i)),
-        ],
+        ]
+        + [whole(*shape) for shape in more],
         out_shape=[
             jax.ShapeDtypeStruct((N, size), BF),
             jax.ShapeDtypeStruct((8, size), F32),
-        ],
+        ]
+        + [jax.ShapeDtypeStruct(shape, BF) for shape in more],
         scratch_shapes=[
             pltpu.VMEM((N, cols), F32),
             pltpu.VMEM((N, cols), F32),
             pltpu.VMEM((8, cols), F32),
         ],
         compiler_params=params(),
-        cost_estimate=cost(2 * N * size * HD, 6 * size * N // 3, N * size),
-        name="scores",
-    )(qt, kn)
+        cost_estimate=cost(2 * N * size * HD, 2 * size * N, N * size),
+        name=name,
+    )(*operands)
+
+
+def scores_a(qkv):
+    more = [(HD, N), (N, HD), (HD, N), (N, EXT)]
+    return scores_call(functools.partial(scores_a_body, 256, 128), "scores_a", CUT, more, [qkv])
+
+
+def scores_b(qt, kn):
+    return scores_call(functools.partial(scores_b_body, 256, 128), "scores_b", N - CUT, [], [qt, kn])
 
 
 CUT = 2048
@@ -520,13 +526,12 @@
     dout, qkv = hold((dout, qkv))
     dout = exchange(dout)
 
-    qt, kn, kt, vn = prepare(qkv)
-    e1, inv1 = scores(qt, kn, 0, CUT)
+    e1, inv1, qt, kn, kt, vn = scores_a(qkv)
     came, qt, inv1 = hold((came, qt, inv1))
     part = (keep.astype(F32) + came.astype(F32)).astype(BF)
     part, dout, qt = hold((part, dout, qt))
     part = lax.all_to_all(part, "z", 0, 0, tiled=True)
-    e2, inv2 = scores(qt, kn, CUT, N)
+    e2, inv2 = scores_b(qt, kn)
     first, dq, dot_t, dot_n = grads_a(dout, e1, e2, inv1, inv2, qt, kt, vn)
     first, part = hold((first, part))
     first = exchange(first)

time: 179 us -> 155 us (0.87)
  local copies, waits for them, and re-layouts: 44.3 us -> 3.03 us
  Pallas kernels: 44.4 us -> 64.5 us
  waiting for transfers between devices: 22 us -> 27.9 us
  other arithmetic: 5.81 us -> 1.3 us
  starting transfers between devices: 60.4 us -> 56.6 us
    unnamed x88 -> x36, local copies, waits for them, and re-layouts: 44.2 us -> 2.33 us
    pallas_call x3 -> x2, Pallas kernels: 14.5 us -> 19.4 us  [scores_call(): pl.pallas_call(body, grid=(size // cols // 2,), in_specs=[whole(*x.shape)...]
    all_to_all x4, waiting for transfers between devices: 0.01 us -> 4.28 us  [exchange(): return lax.all_to_all(x, SEQ, 0, 0, tiled=True)]
    pallas_call x1, Pallas kernels: 12.7 us -> 16.4 us  [grads_a(): pl.pallas_call(functools.partial(grads_a_body, rows), grid=(SRC * BIG //...]
    all_to_all x4, starting transfers between devices: 31.3 us -> 28.2 us  [exchange(): return lax.all_to_all(x, SEQ, 0, 0, tiled=True)]
    pallas_call x1, Pallas kernels: 7.63 us -> 10.7 us  [grads_b(): pl.pallas_call(functools.partial(grads_b_body, rows), grid=(SRC * SMALL /...]
    reduce_sum x1, other arithmetic: 2.2 us -> 0.11 us  [body(): mine = jnp.sum(part.astype(F32), axis=0)]
    pallas_call x1, Pallas kernels: 2.11 us -> 4.16 us  [weight_share(): pl.pallas_call(weight_share_body, in_specs=[pl.BlockSpec(memory_space=plt...]
  transfers between devices with their start and end apart: 21 -> 21, of which waited for: 4 -> 9; matrix products, arithmetic and copies ran while one was open for 2% -> 1% of each run, Pallas kernels for 24% -> 40%
where the time goes in v4:
time: 155 us; the launch traced here: 154 us
  Pallas kernels  64.5 us (42%)
  starting transfers between devices  56.6 us (37%)
  waiting for transfers between devices  27.9 us (18%)
  local copies, waits for them, and re-layouts  3.03 us (2%)
    all_to_all x4, starting transfers between devices, exchange(): return lax.all_to_all(x, SEQ, 0, 0, tiled=True)  28.2 us
    pallas_call x2, Pallas kernels, scores_call(): pl.pallas_call(body, grid=(size // cols // 2,), in_specs=[whole(*x.shape)...  19.4 us
    pallas_call x1, Pallas kernels, grads_a(): pl.pallas_call(functools.partial(grads_a_body, rows), grid=(SRC * BIG //...  16.4 us
    ppermute x1, waiting for transfers between devices, body(): other = lax.ppermute(t, 'yh', swap)  12.1 us
    ppermute x3, starting transfers between devices, down(): return lax.ppermute(block, 'z', DOWN)  10.8 us
    pallas_call x1, Pallas kernels, grads_b(): pl.pallas_call(functools.partial(grads_b_body, rows), grid=(SRC * SMALL /...  10.7 us
    ppermute x4, waiting for transfers between devices, up(): return lax.ppermute(block, 'z', UP)  9.73 us
    all_to_all x4, waiting for transfers between devices, exchange(): return lax.all_to_all(x, SEQ, 0, 0, tiled=True)  4.28 us
  transfers between devices with their start and end apart: 21, of which 9 were waited for; matrix products, arithmetic and copies ran while one was open for 1% of the time, Pallas kernels for 40%

profile of v4, /device:TPU:1, one launch (start us, length us, event | category | flops | bytes accessed | tf_op | source)
XLA Modules:
  0.0 154.2 jit_solution(18419851669498442031)
XLA Ops:
  0.6 3.3 %collective-permute-start.1 = (bf16[1,192,1280]{2,1,0:T(8,128)(2,1)}, bf16[1,192,1280]{2,1,0:T(8,128)(2,1)S(1)}, u32[]{:S(2)}, u32[]{:S(2)}) collective-permute-start(bf16[1,192,1280]{2,1,0:T(8,128)(2,1)} %g_own.1), channel_id=1, source_target_pairs={{0,16},{16,0},{1,17},{17,1},{2,18},{18,2},{3,19},{19,3},{4,20},{20... | collective-permute-start | bytes 1474568 | tf_op jit(solution)/shard_map/ppermute | solution.py:510
  4.1 3.2 %pack_qkv.1 = bf16[16,120,384]{2,1,0:T(8,128)(2,1)} custom-call(bf16[1,192,1280]{2,1,0:T(8,128)(2,1)} %q_ref.1, bf16[1,192,1280]{2,1,0:T(8,128)(2,1)} %k_ref.1, bf16[1,192,1280]{2,1,0:T(8,128)(2,1)} %v_ref.1), custom_call_target="tpu_custom_call" | custom-call | bytes 3000000 | tf_op jit(solution)/shard_map/pack_qkv/pallas_call | solution.py:61
  7.6 5.1 %collective-permute-start.3 = (bf16[2,40,1280]{2,1,0:T(8,128)(2,1)S(1)}, bf16[2,40,1280]{2,1,0:T(8,128)(2,1)S(1)}, u32[]{:S(2)}, u32[]{:S(2)}) collective-permute-start(bf16[2,40,1280]{2,1,0:T(8,128)(2,1)S(1)} %pad_maximum_fusion.refs_0_), channel_id=1, source_target_pairs={{0,7},{1,0},{2,1},{3,2},{4,3},{5,4},{6,5},{7,6},{8,15},{9,8},{10,9... | collective-permute-start | bytes 614408 | tf_op jit(solution)/shard_map/ppermute | solution.py:506
  12.7 8.1 %all-to-all-start = ((bf16[16,120,384]{2,1,0:T(8,128)(2,1)}), bf16[16,120,384]{2,1,0:T(8,128)(2,1)S(1)}, u32[]{:S(2)}, u32[]{:S(2)}) async-start(bf16[16,120,384]{2,1,0:T(8,128)(2,1)} %pack_qkv.1), calls=%async_computation | async-start | bytes 2949120 | tf_op jit(solution)/shard_map/all_to_all | solution.py:495
  20.9 3.0 %collective-permute-start.5 = (bf16[2,40,1280]{2,1,0:T(8,128)(2,1)S(1)}, bf16[2,40,1280]{2,1,0:T(8,128)(2,1)S(1)}, u32[]{:S(2)}, u32[]{:S(2)}) collective-permute-start(bf16[2,40,1280]{2,1,0:T(8,128)(2,1)S(1)} %collective-permute-done.3.refs_2_), channel_id=1, source_target_pairs={{0,7},{1,0},{2,1},{3,2},{4,3},{5,4},{6,5},{7,6},{8,15},{9,8},{10,9... | collective-permute-start | bytes 614408 | tf_op jit(solution)/shard_map/ppermute | solution.py:506
  23.9 2.1 %split_attn.1 = (bf16[16,40,192]{2,1,0:T(8,128)(2,1)}, bf16[16,40,192]{2,1,0:T(8,128)(2,1)}) custom-call(s32[1]{0:T(128)} %bitcast.c_ref.at_ref, bf16[1,192,1280]{2,1,0:T(8,128)(2,1)} %a_ref), custom_call_target="tpu_custom_call" | custom-call | bytes 1000000 | tf_op jit(solution)/shard_map/split_attn/pallas_call | solution.py:83
  26.1 2.8 %collective-permute-done.4.refs_3_ = bf16[2,40,1280]{2,1,0:T(8,128)(2,1)S(1)} collective-permute-done((bf16[2,40,1280]{2,1,0:T(8,128)(2,1)S(1)}, bf16[2,40,1280]{2,1,0:T(8,128)(2,1)S(1)}, u32[]{:S(2)}, u32[]{:S(2)}) %collective-permute-start.4) | collective-permute-done | bytes 204832 | tf_op jit(solution)/shard_map/ppermute | solution.py:503
  30.0 2.7 %collective-permute-start.7 = (bf16[2,40,1280]{2,1,0:T(8,128)(2,1)S(1)}, bf16[2,40,1280]{2,1,0:T(8,128)(2,1)S(1)}, u32[]{:S(2)}, u32[]{:S(2)}) collective-permute-start(bf16[2,40,1280]{2,1,0:T(8,128)(2,1)S(1)} %collective-permute-done.5.refs_4_), channel_id=1, source_target_pairs={{0,7},{1,0},{2,1},{3,2},{4,3},{5,4},{6,5},{7,6},{8,15},{9,8},{10,9... | collective-permute-start | bytes 614408 | tf_op jit(solution)/shard_map/ppermute | solution.py:506
  32.6 5.2 %collective-permute-done.6.refs_5_ = bf16[2,40,1280]{2,1,0:T(8,128)(2,1)S(1)} collective-permute-done((bf16[2,40,1280]{2,1,0:T(8,128)(2,1)S(1)}, bf16[2,40,1280]{2,1,0:T(8,128)(2,1)S(1)}, u32[]{:S(2)}, u32[]{:S(2)}) %collective-permute-start.6) | collective-permute-done | bytes 204832 | tf_op jit(solution)/shard_map/ppermute | solution.py:503
  38.9 4.2 %weight_share.1 = (bf16[8,40,1280]{2,1,0:T(8,128)(2,1)}, bf16[8,40,1280]{2,1,0:T(8,128)(2,1)}, bf16[384,1280]{1,0:T(8,128)(2,1)}, bf16[16,40,384]{2,1,0:T(8,128)(2,1)}) custom-call(s32[1]{0:T(128)} %bitcast.19.y_ref, bf16[1,192,1280]{2,1,0:T(8,128)(2,1)} %g_own.1, bf16[1,192,1280]{2,1,0:T(8,128)(2,1)} %copy-done.16, ...), custom_call_target="tpu_custom_call" | custom-call | flops 629145600 | bytes 6000000 | tf_op jit(solution)/shard_map/weight_share/pallas_call | solution.py:114
  46.6 3.9 %out_grad.1 = bf16[16,48,384]{2,1,0:T(8,128)(2,1)} custom-call(s32[16]{0:T(128)} %stack.84.ids, bf16[2,40,1280]{2,1,0:T(8,128)(2,1)} %copy-done.7, bf16[2,40,1280]{2,1,0:T(8,128)(2,1)} %copy-done.10, bf16[2,40,1280]{2,1,0:T(8,128)(2,1)} %copy-done.9, bf16[2,40,1280]{2,1,0:T(8,128)(2,1)} %copy-done.11, bf16[2,40,1280]{2,1,0:T(8,128)(2,1)} %copy-done.12, ...), custom_call_target="tpu_custom_call" | custom-call | flops 629145600 | bytes 4000000 | tf_op jit(solution)/shard_map/out_grad/pallas_call | solution.py:150
  50.6 9.5 %all-to-all-start.1 = ((bf16[16,48,384]{2,1,0:T(8,128)(2,1)}), bf16[16,48,384]{2,1,0:T(8,128)(2,1)S(1)}, u32[]{:S(2)}, u32[]{:S(2)}) async-start(bf16[16,48,384]{2,1,0:T(8,128)(2,1)} %out_grad.1), calls=%async_computation.1 | async-start | bytes 1179648 | tf_op jit(solution)/shard_map/all_to_all | solution.py:495
  60.1 12.0 %scores_a.1 = (bf16[3072,2048]{1,0:T(8,128)(2,1)}, f32[8,2048]{1,0:T(8,128)}, bf16[80,3072]{1,0:T(8,128)(2,1)}, bf16[3072,80]{1,0:T(8,128)(2,1)}, bf16[80,3072]{1,0:T(8,128)(2,1)}, /*index=5*/bf16[3072,96]{1,0:T(8,128)(2,1)}) custom-call(bf16[16,120,384]{2,1,0:T(8,128)(2,1)} %copy-done.4), custom_call_target="tpu_custom_call" | custom-call | flops 1006632960 | bytes 12582912 | tf_op jit(solution)/shard_map/scores_a/pallas_call | solution.py:249
  74.5 4.1 %all-to-all-start.2 = ((bf16[8,40,1280]{2,1,0:T(8,128)(2,1)}), bf16[8,40,1280]{2,1,0:T(8,128)(2,1)S(1)}, u32[]{:S(2)}, u32[]{:S(2)}) async-start(bf16[8,40,1280]{2,1,0:T(8,128)(2,1)} %add_convert_fusion), calls=%async_computation.2 | async-start | bytes 1638400 | tf_op jit(solution)/shard_map/all_to_all | solution.py:533
  78.5 7.4 %scores_b.1 = (bf16[3072,1024]{1,0:T(8,128)(2,1)}, f32[8,1024]{1,0:T(8,128)}) custom-call(bf16[80,3072]{1,0:T(8,128)(2,1)} %get-tuple-element.82.qt.qt_ref, bf16[3072,80]{1,0:T(8,128)(2,1)} %get-tuple-element.83.kn), custom_call_target="tpu_custom_call" | custom-call | flops 503316480 | bytes 6291456 | tf_op jit(solution)/shard_map/scores_b/pallas_call | solution.py:249
  86.0 16.4 %grads_a.1 = (bf16[16,80,256]{2,1,0:T(8,128)(2,1)}, f32[80,3072]{1,0:T(8,128)}, bf16[96,3072]{1,0:T(8,128)(2,1)}, bf16[80,3072]{1,0:T(8,128)(2,1)}) custom-call(bf16[16,48,384]{2,1,0:T(8,128)(2,1)} %copy-done.3, bf16[3072,2048]{1,0:T(8,128)(2,1)} %get-tuple-element.74.e1, bf16[3072,1024]{1,0:T(8,128)(2,1)} %get-tuple-element.84.e2, ...), custom_call_target="tpu_custom_call" | custom-call | flops 4026531840 | bytes 18000000 | tf_op jit(solution)/shard_map/grads_a/pallas_call | solution.py:339
  102.9 2.5 %collective-permute-start.13 = (f32[40,1280]{1,0:T(8,128)S(1)}, f32[40,1280]{1,0:T(8,128)S(1)}, u32[]{:S(2)}, u32[]{:S(2)}) collective-permute-start(f32[40,1280]{1,0:T(8,128)S(1)} %convert_reduce_fusion), channel_id=1, source_target_pairs={{0,96},{32,0},{64,32},{96,64},{1,97},{33,1},{65,33},{97,65},{2,98}... | collective-permute-start | bytes 614408 | tf_op jit(solution)/shard_map/ppermute | solution.py:542
  106.6 6.3 %all-to-all-start.4 = ((bf16[16,80,256]{2,1,0:T(8,128)(2,1)}), bf16[16,80,256]{2,1,0:T(8,128)(2,1)S(1)}, u32[]{:S(2)}, u32[]{:S(2)}) async-start(bf16[16,80,256]{2,1,0:T(8,128)(2,1)} %get-tuple-element.98), calls=%async_computation.4 | async-start | bytes 1310720 | tf_op jit(solution)/shard_map/all_to_all | solution.py:495
  112.9 10.7 %grads_b.1 = bf16[16,200,128]{2,1,0:T(8,128)(2,1)} custom-call(bf16[3072,2048]{1,0:T(8,128)(2,1)} %get-tuple-element.74.e1, bf16[3072,1024]{1,0:T(8,128)(2,1)} %get-tuple-element.84.e2, f32[8,2048]{1,0:T(8,128)} %get-tuple-element.85.inv1, f32[8,1024]{1,0:T(8,128)} %get-tuple-element.86.inv2, bf16[80,3072]{1,0:T(8,128)(2,1)} %get-tuple-element.82.qt.qt_ref, ...), custom_call_target="tpu_custom_call" | custom-call | flops 2013265920 | bytes 11000000 | tf_op jit(solution)/shard_map/grads_b/pallas_call | solution.py:401
  123.6 3.0 %all-to-all-done.4.a_ref = bf16[16,80,256]{2,1,0:T(8,128)(2,1)S(1)} async-done(((bf16[16,80,256]{2,1,0:T(8,128)(2,1)}), bf16[16,80,256]{2,1,0:T(8,128)(2,1)S(1)}, u32[]{:S(2)}, u32[]{:S(2)}) %all-to-all-start.4) | async-done | bytes 655392 | tf_op jit(solution)/shard_map/all_to_all | solution.py:495
  126.7 4.2 %all-to-all-start.3 = ((bf16[16,200,128]{2,1,0:T(8,128)(2,1)}), bf16[16,200,128]{2,1,0:T(8,128)(2,1)S(1)}, u32[]{:S(2)}, u32[]{:S(2)}) async-start(bf16[16,200,128]{2,1,0:T(8,128)(2,1)} %grads_b.1), calls=%async_computation.3 | async-start | bytes 1638400 | tf_op jit(solution)/shard_map/all_to_all | solution.py:495
  130.9 2.9 %collective-permute-start.14 = (f32[40,1280]{1,0:T(8,128)S(1)}, f32[40,1280]{1,0:T(8,128)S(1)}, u32[]{:S(2)}, u32[]{:S(2)}) collective-permute-start(f32[40,1280]{1,0:T(8,128)S(1)} %add_add_fusion), channel_id=1, source_target_pairs={{0,128},{128,0},{1,129},{129,1},{2,130},{130,2},{3,131},{131,3},{4... | collective-permute-start | bytes 614408 | tf_op jit(solution)/shard_map/ppermute | solution.py:545
  135.9 12.1 %collective-permute-done.14 = f32[40,1280]{1,0:T(8,128)S(1)} collective-permute-done((f32[40,1280]{1,0:T(8,128)S(1)}, f32[40,1280]{1,0:T(8,128)S(1)}, u32[]{:S(2)}, u32[]{:S(2)}) %collective-permute-start.14) | collective-permute-done | bytes 204832 | tf_op jit(solution)/shard_map/ppermute | solution.py:545
  151.6 2.6 %unpack_b.1 = (bf16[1,192,1280]{2,1,0:T(8,128)(2,1)}, bf16[1,192,1280]{2,1,0:T(8,128)(2,1)}, bf16[1,192,1280]{2,1,0:T(8,128)(2,1)}, f32[80,1280]{1,0:T(8,128)}) custom-call(s32[1]{0:T(128)} %bitcast.c_ref.at_ref, bf16[16,200,128]{2,1,0:T(8,128)(2,1)} %copy-done.1, f32[40,1280]{1,0:T(8,128)} %copy-done.5, ...), custom_call_target="tpu_custom_call", output_to_operand_aliasing={{1}: (4, {}), {2}: (5, {})} | custom-call | bytes 3000000 | tf_op jit(solution)/shard_map/unpack_b/pallas_call | solution.py:469
  (72 shorter events, 16.1 us)
Async XLA Ops:
  0.6 7.0 %collective-permute-start.1 = (bf16[1,192,1280]{2,1,0:T(8,128)(2,1)}, bf16[1,192,1280]{2,1,0:T(8,128)(2,1)S(1)}, u32[]{:S(2)}, u32[]{:S(2)}) collective-permute-start(bf16[1,192,1280]{2,1,0:T(8,128)(2,1)} %g_own.1), channel_id=1, source_target_pairs={{0,16},{16,0},{1,17},{17,1},{2,18},{18,2},{3,19},{19,3},{4,20},{20... | collective-permute-start | bytes 1474568 | tf_op jit(solution)/shard_map/ppermute | solution.py:510
  4.0 3.6 %collective-permute-start = (bf16[40,1280]{1,0:T(8,128)(2,1)S(1)}, bf16[40,1280]{1,0:T(8,128)(2,1)S(1)}, u32[]{:S(2)}, u32[]{:S(2)}) collective-permute-start(bf16[40,1280]{1,0:T(8,128)(2,1)S(1)} %constant_dynamic-slice_fusion), channel_id=1, source_target_pairs={{0,8},{8,0},{1,9},{9,1},{2,10},{10,2},{3,11},{11,3},{4,12},{12,4},... | collective-permute-start | bytes 307208 | tf_op jit(solution)/shard_map/ppermute | solution.py:509
  7.6 18.4 %copy-start.7 = (bf16[2,40,1280]{2,1,0:T(8,128)(2,1)}, bf16[2,40,1280]{2,1,0:T(8,128)(2,1)S(1)}, u32[]{:S(2)}) copy-start(bf16[2,40,1280]{2,1,0:T(8,128)(2,1)S(1)} %pad_maximum_fusion.refs_0_) | copy-start | bytes 614404
  7.6 13.1 %collective-permute-start.3 = (bf16[2,40,1280]{2,1,0:T(8,128)(2,1)S(1)}, bf16[2,40,1280]{2,1,0:T(8,128)(2,1)S(1)}, u32[]{:S(2)}, u32[]{:S(2)}) collective-permute-start(bf16[2,40,1280]{2,1,0:T(8,128)(2,1)S(1)} %pad_maximum_fusion.refs_0_), channel_id=1, source_target_pairs={{0,7},{1,0},{2,1},{3,2},{4,3},{5,4},{6,5},{7,6},{8,15},{9,8},{10,9... | collective-permute-start | bytes 614408 | tf_op jit(solution)/shard_map/ppermute | solution.py:506
  12.7 8.1 %collective-permute-start.2 = (bf16[2,40,1280]{2,1,0:T(8,128)(2,1)S(1)}, bf16[2,40,1280]{2,1,0:T(8,128)(2,1)S(1)}, u32[]{:S(2)}, u32[]{:S(2)}) collective-permute-start(bf16[2,40,1280]{2,1,0:T(8,128)(2,1)S(1)} %pad_maximum_fusion.refs_0_), channel_id=1, source_target_pairs={{0,1},{1,2},{2,3},{3,4},{4,5},{5,6},{6,7},{7,0},{8,9},{9,10},{10,1... | collective-permute-start | bytes 614408 | tf_op jit(solution)/shard_map/ppermute | solution.py:503
  12.7 37.9 %all-to-all-start = ((bf16[16,120,384]{2,1,0:T(8,128)(2,1)}), bf16[16,120,384]{2,1,0:T(8,128)(2,1)S(1)}, u32[]{:S(2)}, u32[]{:S(2)}) async-start(bf16[16,120,384]{2,1,0:T(8,128)(2,1)} %pack_qkv.1), calls=%async_computation | async-start | bytes 2949120 | tf_op jit(solution)/shard_map/all_to_all | solution.py:495
  20.8 25.8 %copy-start.9 = (bf16[2,40,1280]{2,1,0:T(8,128)(2,1)}, bf16[2,40,1280]{2,1,0:T(8,128)(2,1)S(1)}, u32[]{:S(2)}) copy-start(bf16[2,40,1280]{2,1,0:T(8,128)(2,1)S(1)} %collective-permute-done.3.refs_2_) | copy-start | bytes 614404
  20.8 25.8 %copy-start.10 = (bf16[2,40,1280]{2,1,0:T(8,128)(2,1)}, bf16[2,40,1280]{2,1,0:T(8,128)(2,1)S(1)}, u32[]{:S(2)}) copy-start(bf16[2,40,1280]{2,1,0:T(8,128)(2,1)S(1)} %collective-permute-done.2.refs_1_) | copy-start | bytes 614404
  20.8 8.0 %collective-permute-start.4 = (bf16[2,40,1280]{2,1,0:T(8,128)(2,1)S(1)}, bf16[2,40,1280]{2,1,0:T(8,128)(2,1)S(1)}, u32[]{:S(2)}, u32[]{:S(2)}) collective-permute-start(bf16[2,40,1280]{2,1,0:T(8,128)(2,1)S(1)} %collective-permute-done.2.refs_1_), channel_id=1, source_target_pairs={{0,1},{1,2},{2,3},{3,4},{4,5},{5,6},{6,7},{7,0},{8,9},{9,10},{10,1... | collective-permute-start | bytes 614408 | tf_op jit(solution)/shard_map/ppermute | solution.py:503
  20.9 7.9 %collective-permute-start.5 = (bf16[2,40,1280]{2,1,0:T(8,128)(2,1)S(1)}, bf16[2,40,1280]{2,1,0:T(8,128)(2,1)S(1)}, u32[]{:S(2)}, u32[]{:S(2)}) collective-permute-start(bf16[2,40,1280]{2,1,0:T(8,128)(2,1)S(1)} %collective-permute-done.3.refs_2_), channel_id=1, source_target_pairs={{0,7},{1,0},{2,1},{3,2},{4,3},{5,4},{6,5},{7,6},{8,15},{9,8},{10,9... | collective-permute-start | bytes 614408 | tf_op jit(solution)/shard_map/ppermute | solution.py:506
  28.8 9.0 %collective-permute-start.8 = (bf16[16,40,192]{2,1,0:T(8,128)(2,1)}, bf16[16,40,192]{2,1,0:T(8,128)(2,1)S(1)}, u32[]{:S(2)}, u32[]{:S(2)}) collective-permute-start(bf16[16,40,192]{2,1,0:T(8,128)(2,1)} %get-tuple-element.62), channel_id=1, source_target_pairs={{0,16},{16,0},{1,17},{17,1},{2,18},{18,2},{3,19},{19,3},{4,20},{20... | collective-permute-start | bytes 737288 | tf_op jit(solution)/shard_map/ppermute | solution.py:517
  30.0 7.9 %collective-permute-start.6 = (bf16[2,40,1280]{2,1,0:T(8,128)(2,1)S(1)}, bf16[2,40,1280]{2,1,0:T(8,128)(2,1)S(1)}, u32[]{:S(2)}, u32[]{:S(2)}) collective-permute-start(bf16[2,40,1280]{2,1,0:T(8,128)(2,1)S(1)} %collective-permute-done.4.refs_3_), channel_id=1, source_target_pairs={{0,1},{1,2},{2,3},{3,4},{4,5},{5,6},{6,7},{7,0},{8,9},{9,10},{10,1... | collective-permute-start | bytes 614408 | tf_op jit(solution)/shard_map/ppermute | solution.py:503
  30.0 7.9 %collective-permute-start.7 = (bf16[2,40,1280]{2,1,0:T(8,128)(2,1)S(1)}, bf16[2,40,1280]{2,1,0:T(8,128)(2,1)S(1)}, u32[]{:S(2)}, u32[]{:S(2)}) collective-permute-start(bf16[2,40,1280]{2,1,0:T(8,128)(2,1)S(1)} %collective-permute-done.5.refs_4_), channel_id=1, source_target_pairs={{0,7},{1,0},{2,1},{3,2},{4,3},{5,4},{6,5},{7,6},{8,15},{9,8},{10,9... | collective-permute-start | bytes 614408 | tf_op jit(solution)/shard_map/ppermute | solution.py:506
  37.8 7.0 %collective-permute-start.9 = (bf16[2,40,1280]{2,1,0:T(8,128)(2,1)S(1)}, bf16[2,40,1280]{2,1,0:T(8,128)(2,1)S(1)}, u32[]{:S(2)}, u32[]{:S(2)}) collective-permute-start(bf16[2,40,1280]{2,1,0:T(8,128)(2,1)S(1)} %collective-permute-done.6.refs_5_), channel_id=1, source_target_pairs={{0,1},{1,2},{2,3},{3,4},{4,5},{5,6},{6,7},{7,0},{8,9},{9,10},{10,1... | collective-permute-start | bytes 614408 | tf_op jit(solution)/shard_map/ppermute | solution.py:503
  45.5 26.6 %collective-permute-start.10 = (bf16[8,40,1280]{2,1,0:T(8,128)(2,1)}, bf16[8,40,1280]{2,1,0:T(8,128)(2,1)S(1)}, u32[]{:S(2)}, u32[]{:S(2)}) collective-permute-start(bf16[8,40,1280]{2,1,0:T(8,128)(2,1)} %get-tuple-element.76), channel_id=1, source_target_pairs={{0,8},{8,0},{1,9},{9,1},{2,10},{10,2},{3,11},{11,3},{4,12},{12,4},... | collective-permute-start | bytes 2457608 | tf_op jit(solution)/shard_map/ppermute | solution.py:521
  50.6 23.9 %all-to-all-start.1 = ((bf16[16,48,384]{2,1,0:T(8,128)(2,1)}), bf16[16,48,384]{2,1,0:T(8,128)(2,1)S(1)}, u32[]{:S(2)}, u32[]{:S(2)}) async-start(bf16[16,48,384]{2,1,0:T(8,128)(2,1)} %out_grad.1), calls=%async_computation.1 | async-start | bytes 1179648 | tf_op jit(solution)/shard_map/all_to_all | solution.py:495
  74.5 28.4 %all-to-all-start.2 = ((bf16[8,40,1280]{2,1,0:T(8,128)(2,1)}), bf16[8,40,1280]{2,1,0:T(8,128)(2,1)S(1)}, u32[]{:S(2)}, u32[]{:S(2)}) async-start(bf16[8,40,1280]{2,1,0:T(8,128)(2,1)} %add_convert_fusion), calls=%async_computation.2 | async-start | bytes 1638400 | tf_op jit(solution)/shard_map/all_to_all | solution.py:533
  102.9 20.6 %collective-permute-start.13 = (f32[40,1280]{1,0:T(8,128)S(1)}, f32[40,1280]{1,0:T(8,128)S(1)}, u32[]{:S(2)}, u32[]{:S(2)}) collective-permute-start(f32[40,1280]{1,0:T(8,128)S(1)} %convert_reduce_fusion), channel_id=1, source_target_pairs={{0,96},{32,0},{64,32},{96,64},{1,97},{33,1},{65,33},{97,65},{2,98}... | collective-permute-start | bytes 614408 | tf_op jit(solution)/shard_map/ppermute | solution.py:542
  105.4 18.2 %collective-permute-start.12 = (f32[40,1280]{1,0:T(8,128)S(1)}, f32[40,1280]{1,0:T(8,128)S(1)}, u32[]{:S(2)}, u32[]{:S(2)}) collective-permute-start(f32[40,1280]{1,0:T(8,128)S(1)} %convert_reduce_fusion), channel_id=1, source_target_pairs={{0,64},{32,96},{64,0},{96,32},{1,65},{33,97},{65,1},{97,33},{2,66}... | collective-permute-start | bytes 614408 | tf_op jit(solution)/shard_map/ppermute | solution.py:542
  106.0 17.6 %collective-permute-start.11 = (f32[40,1280]{1,0:T(8,128)S(1)}, f32[40,1280]{1,0:T(8,128)S(1)}, u32[]{:S(2)}, u32[]{:S(2)}) collective-permute-start(f32[40,1280]{1,0:T(8,128)S(1)} %convert_reduce_fusion), channel_id=1, source_target_pairs={{0,32},{32,64},{64,96},{96,0},{1,33},{33,65},{65,97},{97,1},{2,34}... | collective-permute-start | bytes 614408 | tf_op jit(solution)/shard_map/ppermute | solution.py:542
  106.6 20.1 %all-to-all-start.4 = ((bf16[16,80,256]{2,1,0:T(8,128)(2,1)}), bf16[16,80,256]{2,1,0:T(8,128)(2,1)S(1)}, u32[]{:S(2)}, u32[]{:S(2)}) async-start(bf16[16,80,256]{2,1,0:T(8,128)(2,1)} %get-tuple-element.98), calls=%async_computation.4 | async-start | bytes 1310720 | tf_op jit(solution)/shard_map/all_to_all | solution.py:495
  126.7 23.4 %all-to-all-start.3 = ((bf16[16,200,128]{2,1,0:T(8,128)(2,1)}), bf16[16,200,128]{2,1,0:T(8,128)(2,1)S(1)}, u32[]{:S(2)}, u32[]{:S(2)}) async-start(bf16[16,200,128]{2,1,0:T(8,128)(2,1)} %grads_b.1), calls=%async_computation.3 | async-start | bytes 1638400 | tf_op jit(solution)/shard_map/all_to_all | solution.py:495
  130.9 17.0 %collective-permute-start.14 = (f32[40,1280]{1,0:T(8,128)S(1)}, f32[40,1280]{1,0:T(8,128)S(1)}, u32[]{:S(2)}, u32[]{:S(2)}) collective-permute-start(f32[40,1280]{1,0:T(8,128)S(1)} %add_add_fusion), channel_id=1, source_target_pairs={{0,128},{128,0},{1,129},{129,1},{2,130},{130,2},{3,131},{131,3},{4... | collective-permute-start | bytes 614408 | tf_op jit(solution)/shard_map/ppermute | solution.py:545
  148.0 2.0 %collective-permute-start.15 = (f32[40,1280]{1,0:T(8,128)S(1)}, f32[40,1280]{1,0:T(8,128)S(1)}, u32[]{:S(2)}, u32[]{:S(2)}) collective-permute-start(f32[40,1280]{1,0:T(8,128)S(1)} %add.148.w_own), channel_id=1, source_target_pairs={{0,16},{16,0},{1,17},{17,1},{2,18},{18,2},{3,19},{19,3},{4,20},{20... | collective-permute-start | bytes 614408 | tf_op jit(solution)/shard_map/ppermute | solution.py:548
  (15 other events, 105.5 us)

commit v5 on v4

--- a/solution.py
+++ b/solution.py
@@ -23,6 +23,7 @@
 SCALE = HD**-0.5
 LOG2E = 1.4426950408889634
 VMEM_LIMIT = 56 * 1024 * 1024
+LESS = 28 * 1024 * 1024
 SEQ = ("yh", "x", "c")
 DP = ("yl", "z")
 OFFSETS = (0, -1, 1, -2, 2, -3, 3, -4)
@@ -440,13 +441,13 @@
         in_specs=[whole(HEADS, HD, 2 * BIG)],
         out_specs=[spec, spec],
         out_shape=[shape, shape],
-        compiler_params=params(),
+        compiler_params=params(LESS),
         cost_estimate=cost(0, 2 * 10**6),
         name="unpack_a",
     )(a)
 
 
-def unpack_b_body(at_ref, b_ref, w_own, w_oth, dk_in, dv_in, dq_ref, dk_ref, dv_ref, dw_ref):
+def unpack_b_body(at_ref, b_ref, w0, w1, w2, w3, dk_in, dv_in, dq_ref, dk_ref, dv_ref, dw_ref):
     both = patch_rows(b_ref, slice(0, HD), slice(0, BIG))
     dv_ref[0] = both[:SMALL]
     dk_ref[0] = both[SMALL:]
@@ -458,8 +459,8 @@
     dq_ref[0, BIG:TOK] = jnp.concatenate(tail, axis=0).T.astype(BF)
     c = at_ref[0]
     factor = 1.0 / float(16 * N) ** 0.5
-    for ref, row in ((w_own, c), (w_oth, 1 - c)):
-        dw_ref[pl.ds(pl.multiple_of(row * HALF, 8), HALF), :] = ref[...] * factor
+    for ref, more, row in ((w0, w1, c), (w2, w3, 1 - c)):
+        dw_ref[pl.ds(pl.multiple_of(row * HALF, 8), HALF), :] = (ref[...] + more[...]) * factor
 
 
 def unpack_b(at, b, parts, dk, dv):
@@ -470,12 +471,12 @@
         unpack_b_body,
         grid=(1,),
         in_specs=[pl.BlockSpec(memory_space=pltpu.SMEM), whole(HEADS, 200, 128)]
-        + [whole(HALF, D)] * 2
+        + [whole(HALF, D)] * 4
         + [hbm, hbm],
         out_specs=[whole(1, TOK, D), spec, spec, whole(HD, D)],
         out_shape=[shape] * 3 + [jax.ShapeDtypeStruct((HD, D), F32)],
-        input_output_aliases={4: 1, 5: 2},
-        compiler_params=params(),
+        input_output_aliases={6: 1, 7: 2},
+        compiler_params=params(LESS),
         cost_estimate=cost(0, 3 * 10**6),
         name="unpack_b",
     )(at, b, *parts, dk, dv)
@@ -509,7 +510,9 @@
     pair = jnp.stack([w_half, lax.ppermute(w_half, "yl", swap)])
     g_oth = lax.ppermute(d_block, "c", swap)
     packed = pack_qkv(query, keys, values)
-    pair, packed, g_oth, attn = hold((pair, packed, g_oth, attn))
+    zs = [(z + o) % 8 for o in OFFSETS]
+    ids = scalar(*[y * 8 + k for k in zs for y in (yl, 1 - yl)])
+    pair, packed, g_oth, attn, ids = hold((pair, packed, g_oth, attn, ids))
     qkv = exchange(packed)
     f1, g1, attn = hold((up(pair), down(pair), attn))
     a_own, a_send = split_attn(scalar(c), attn)
@@ -520,8 +523,6 @@
     f4, give = hold((up(f3), give))
     came = lax.ppermute(give, "yl", swap)
 
-    zs = [(z + o) % 8 for o in OFFSETS]
-    ids = scalar(*[y * 8 + k for k in zs for y in (yl, 1 - yl)])
     dout = out_grad(ids, [pair, f1, g1, f2, g2, f3, g3, f4], gx, ax)
     dout, qkv = hold((dout, qkv))
     dout = exchange(dout)
@@ -542,10 +543,13 @@
         t = t + lax.ppermute(mine, "x", [(i, (i + k) % 4) for i in range(4)])
     second, t = hold((second, t))
     second = exchange(second)
-    other = lax.ppermute(t, "yh", swap)
-    other, d_keys, d_values = hold((other, *unpack_a(first)))
-    u = t + other
-    return unpack_b(scalar(c), second, [u, lax.ppermute(u, "c", swap)], d_keys, d_values)
+    across = [(0, 3), (1, 2), (2, 1), (3, 0)]
+    came_y = lax.ppermute(t, "yh", swap)
+    came_c = lax.ppermute(t, "c", swap)
+    came_yc = lax.ppermute(t, ("yh", "c"), across)
+    d_keys, d_values = unpack_a(first)
+    came_y, came_c, came_yc, d_keys, d_values = hold((came_y, came_c, came_yc, d_keys, d_values))
+    return unpack_b(scalar(c), second, [t, came_y, came_c, came_yc], d_keys, d_values)
 
 
 def solution(mesh):

time: 155 us -> 153 us (0.987)
  waiting for transfers between devices: 27.9 us -> 31.2 us
  Pallas kernels: 64.5 us -> 62.2 us
  local copies, waits for them, and re-layouts: 3.03 us -> 1.32 us
    ppermute x2 -> x3, waiting for transfers between devices: 13.2 us -> 17.1 us  [the longest x1 13.3 us: body(): came_yc = lax.ppermute(t, ('yh', 'c'), across)]
    unnamed x36 -> x28, local copies, waits for them, and re-layouts: 2.33 us -> 0.68 us
    ppermute x2 -> x3, starting transfers between devices: 3.85 us -> 3.36 us  [the longest x1 3.14 us: body(): came_yc = lax.ppermute(t, ('yh', 'c'), across)]
  transfers between devices with their start and end apart: 21 -> 22, of which waited for: 9 -> 8; matrix products, arithmetic and copies ran while one was open for 1% -> 1% of each run, Pallas kernels for 40% -> 40%
where the time goes in v5:
time: 153 us
  Pallas kernels  62.2 us (41%)
  starting transfers between devices  55.7 us (36%)
  waiting for transfers between devices  31.2 us (20%)
    all_to_all x4, starting transfers between devices, exchange(): return lax.all_to_all(x, SEQ, 0, 0, tiled=True)  27.7 us
    pallas_call x2, Pallas kernels, scores_call(): pl.pallas_call(body, grid=(size // cols // 2,), in_specs=[whole(*x.shape)...  19.5 us
    pallas_call x1, Pallas kernels, grads_a(): pl.pallas_call(functools.partial(grads_a_body, rows), grid=(SRC * BIG //...  16.4 us
    ppermute x1, waiting for transfers between devices, body(): came_yc = lax.ppermute(t, ('yh', 'c'), across)  13.3 us
    ppermute x3, starting transfers between devices, down(): return lax.ppermute(block, 'z', DOWN)  11.1 us
    pallas_call x1, Pallas kernels, grads_b(): pl.pallas_call(functools.partial(grads_b_body, rows), grid=(SRC * SMALL /...  10.7 us
    ppermute x4, waiting for transfers between devices, up(): return lax.ppermute(block, 'z', UP)  9.53 us
    all_to_all x4, waiting for transfers between devices, exchange(): return lax.all_to_all(x, SEQ, 0, 0, tiled=True)  4.16 us
  transfers between devices with their start and end apart: 22, of which 8 were waited for; matrix products, arithmetic and copies ran while one was open for 1% of the time, Pallas kernels for 40%

profile of v5, /device:TPU:1, one launch (start us, length us, event | category | flops | bytes accessed | tf_op | source)
XLA Modules:
  0.0 152.7 jit_solution(15022535943871220281)
XLA Ops:
  0.6 3.3 %collective-permute-start.1 = (bf16[1,192,1280]{2,1,0:T(8,128)(2,1)}, bf16[1,192,1280]{2,1,0:T(8,128)(2,1)S(1)}, u32[]{:S(2)}, u32[]{:S(2)}) collective-permute-start(bf16[1,192,1280]{2,1,0:T(8,128)(2,1)} %g_own.1), channel_id=1, source_target_pairs={{0,16},{16,0},{1,17},{17,1},{2,18},{18,2},{3,19},{19,3},{4,20},{20... | collective-permute-start | bytes 1474568 | tf_op jit(solution)/shard_map/ppermute | solution.py:511
  4.2 3.2 %pack_qkv.1 = bf16[16,120,384]{2,1,0:T(8,128)(2,1)} custom-call(bf16[1,192,1280]{2,1,0:T(8,128)(2,1)} %q_ref.1, bf16[1,192,1280]{2,1,0:T(8,128)(2,1)} %k_ref.1, bf16[1,192,1280]{2,1,0:T(8,128)(2,1)} %v_ref.1), custom_call_target="tpu_custom_call" | custom-call | bytes 3000000 | tf_op jit(solution)/shard_map/pack_qkv/pallas_call | solution.py:62
  8.1 5.3 %collective-permute-start.3 = (bf16[2,40,1280]{2,1,0:T(8,128)(2,1)S(1)}, bf16[2,40,1280]{2,1,0:T(8,128)(2,1)S(1)}, u32[]{:S(2)}, u32[]{:S(2)}) collective-permute-start(bf16[2,40,1280]{2,1,0:T(8,128)(2,1)S(1)} %pad_maximum_fusion.refs_0_), channel_id=1, source_target_pairs={{0,7},{1,0},{2,1},{3,2},{4,3},{5,4},{6,5},{7,6},{8,15},{9,8},{10,9... | collective-permute-start | bytes 614408 | tf_op jit(solution)/shard_map/ppermute | solution.py:507
  13.4 7.9 %all-to-all-start = ((bf16[16,120,384]{2,1,0:T(8,128)(2,1)}), bf16[16,120,384]{2,1,0:T(8,128)(2,1)S(1)}, u32[]{:S(2)}, u32[]{:S(2)}) async-start(bf16[16,120,384]{2,1,0:T(8,128)(2,1)} %pack_qkv.1), calls=%async_computation | async-start | bytes 2949120 | tf_op jit(solution)/shard_map/all_to_all | solution.py:496
  21.5 3.0 %collective-permute-start.5 = (bf16[2,40,1280]{2,1,0:T(8,128)(2,1)S(1)}, bf16[2,40,1280]{2,1,0:T(8,128)(2,1)S(1)}, u32[]{:S(2)}, u32[]{:S(2)}) collective-permute-start(bf16[2,40,1280]{2,1,0:T(8,128)(2,1)S(1)} %collective-permute-done.3.refs_2_), channel_id=1, source_target_pairs={{0,7},{1,0},{2,1},{3,2},{4,3},{5,4},{6,5},{7,6},{8,15},{9,8},{10,9... | collective-permute-start | bytes 614408 | tf_op jit(solution)/shard_map/ppermute | solution.py:507
  24.5 2.1 %split_attn.1 = (bf16[16,40,192]{2,1,0:T(8,128)(2,1)}, bf16[16,40,192]{2,1,0:T(8,128)(2,1)}) custom-call(s32[1]{0:T(128)} %bitcast.c_ref.at_ref, bf16[1,192,1280]{2,1,0:T(8,128)(2,1)} %a_ref), custom_call_target="tpu_custom_call" | custom-call | bytes 1000000 | tf_op jit(solution)/shard_map/split_attn/pallas_call | solution.py:84
  26.6 2.5 %collective-permute-done.4.refs_3_ = bf16[2,40,1280]{2,1,0:T(8,128)(2,1)S(1)} collective-permute-done((bf16[2,40,1280]{2,1,0:T(8,128)(2,1)S(1)}, bf16[2,40,1280]{2,1,0:T(8,128)(2,1)S(1)}, u32[]{:S(2)}, u32[]{:S(2)}) %collective-permute-start.4) | collective-permute-done | bytes 204832 | tf_op jit(solution)/shard_map/ppermute | solution.py:504
  30.5 2.7 %collective-permute-start.7 = (bf16[2,40,1280]{2,1,0:T(8,128)(2,1)S(1)}, bf16[2,40,1280]{2,1,0:T(8,128)(2,1)S(1)}, u32[]{:S(2)}, u32[]{:S(2)}) collective-permute-start(bf16[2,40,1280]{2,1,0:T(8,128)(2,1)S(1)} %collective-permute-done.5.refs_4_), channel_id=1, source_target_pairs={{0,7},{1,0},{2,1},{3,2},{4,3},{5,4},{6,5},{7,6},{8,15},{9,8},{10,9... | collective-permute-start | bytes 614408 | tf_op jit(solution)/shard_map/ppermute | solution.py:507
  33.2 5.2 %collective-permute-done.6.refs_5_ = bf16[2,40,1280]{2,1,0:T(8,128)(2,1)S(1)} collective-permute-done((bf16[2,40,1280]{2,1,0:T(8,128)(2,1)S(1)}, bf16[2,40,1280]{2,1,0:T(8,128)(2,1)S(1)}, u32[]{:S(2)}, u32[]{:S(2)}) %collective-permute-start.6) | collective-permute-done | bytes 204832 | tf_op jit(solution)/shard_map/ppermute | solution.py:504
  39.4 4.2 %weight_share.1 = (bf16[8,40,1280]{2,1,0:T(8,128)(2,1)}, bf16[8,40,1280]{2,1,0:T(8,128)(2,1)}, bf16[384,1280]{1,0:T(8,128)(2,1)}, bf16[16,40,384]{2,1,0:T(8,128)(2,1)}) custom-call(s32[1]{0:T(128)} %bitcast.19.y_ref, bf16[1,192,1280]{2,1,0:T(8,128)(2,1)} %g_own.1, bf16[1,192,1280]{2,1,0:T(8,128)(2,1)} %copy-done.12, ...), custom_call_target="tpu_custom_call" | custom-call | flops 629145600 | bytes 6000000 | tf_op jit(solution)/shard_map/weight_share/pallas_call | solution.py:115
  46.1 3.9 %out_grad.1 = bf16[16,48,384]{2,1,0:T(8,128)(2,1)} custom-call(s32[16]{0:T(128)} %stack.87.ids, bf16[2,40,1280]{2,1,0:T(8,128)(2,1)} %copy-done.4, bf16[2,40,1280]{2,1,0:T(8,128)(2,1)} %copy-done.6, bf16[2,40,1280]{2,1,0:T(8,128)(2,1)} %copy-done.5, bf16[2,40,1280]{2,1,0:T(8,128)(2,1)} %copy-done.7, bf16[2,40,1280]{2,1,0:T(8,128)(2,1)} %copy-done.8, ...), custom_call_target="tpu_custom_call" | custom-call | flops 629145600 | bytes 4000000 | tf_op jit(solution)/shard_map/out_grad/pallas_call | solution.py:151
  50.0 8.8 %all-to-all-start.1 = ((bf16[16,48,384]{2,1,0:T(8,128)(2,1)}), bf16[16,48,384]{2,1,0:T(8,128)(2,1)S(1)}, u32[]{:S(2)}, u32[]{:S(2)}) async-start(bf16[16,48,384]{2,1,0:T(8,128)(2,1)} %out_grad.1), calls=%async_computation.1 | async-start | bytes 1179648 | tf_op jit(solution)/shard_map/all_to_all | solution.py:496
  58.8 12.1 %scores_a.1 = (bf16[3072,2048]{1,0:T(8,128)(2,1)}, f32[8,2048]{1,0:T(8,128)}, bf16[80,3072]{1,0:T(8,128)(2,1)}, bf16[3072,80]{1,0:T(8,128)(2,1)}, bf16[80,3072]{1,0:T(8,128)(2,1)}, /*index=5*/bf16[3072,96]{1,0:T(8,128)(2,1)}) custom-call(bf16[16,120,384]{2,1,0:T(8,128)(2,1)} %copy-done.2), custom_call_target="tpu_custom_call" | custom-call | flops 1006632960 | bytes 12582912 | tf_op jit(solution)/shard_map/scores_a/pallas_call | solution.py:250
  73.8 4.1 %all-to-all-start.2 = ((bf16[8,40,1280]{2,1,0:T(8,128)(2,1)}), bf16[8,40,1280]{2,1,0:T(8,128)(2,1)S(1)}, u32[]{:S(2)}, u32[]{:S(2)}) async-start(bf16[8,40,1280]{2,1,0:T(8,128)(2,1)} %add_convert_fusion), calls=%async_computation.2 | async-start | bytes 1638400 | tf_op jit(solution)/shard_map/all_to_all | solution.py:534
  77.9 7.4 %scores_b.1 = (bf16[3072,1024]{1,0:T(8,128)(2,1)}, f32[8,1024]{1,0:T(8,128)}) custom-call(bf16[80,3072]{1,0:T(8,128)(2,1)} %get-tuple-element.86.qt.qt_ref, bf16[3072,80]{1,0:T(8,128)(2,1)} %get-tuple-element.87.kn), custom_call_target="tpu_custom_call" | custom-call | flops 503316480 | bytes 6291456 | tf_op jit(solution)/shard_map/scores_b/pallas_call | solution.py:250
  85.3 16.4 %grads_a.1 = (bf16[16,80,256]{2,1,0:T(8,128)(2,1)}, f32[80,3072]{1,0:T(8,128)}, bf16[96,3072]{1,0:T(8,128)(2,1)}, bf16[80,3072]{1,0:T(8,128)(2,1)}) custom-call(bf16[16,48,384]{2,1,0:T(8,128)(2,1)} %copy-done.1, bf16[3072,2048]{1,0:T(8,128)(2,1)} %get-tuple-element.78.e1, bf16[3072,1024]{1,0:T(8,128)(2,1)} %get-tuple-element.88.e2, ...), custom_call_target="tpu_custom_call" | custom-call | flops 4026531840 | bytes 18000000 | tf_op jit(solution)/shard_map/grads_a/pallas_call | solution.py:340
  102.3 2.5 %collective-permute-start.13 = (f32[40,1280]{1,0:T(8,128)S(1)}, f32[40,1280]{1,0:T(8,128)S(1)}, u32[]{:S(2)}, u32[]{:S(2)}) collective-permute-start(f32[40,1280]{1,0:T(8,128)S(1)} %convert_reduce_fusion), channel_id=1, source_target_pairs={{0,96},{32,0},{64,32},{96,64},{1,97},{33,1},{65,33},{97,65},{2,98}... | collective-permute-start | bytes 614408 | tf_op jit(solution)/shard_map/ppermute | solution.py:543
  105.9 6.1 %all-to-all-start.4 = ((bf16[16,80,256]{2,1,0:T(8,128)(2,1)}), bf16[16,80,256]{2,1,0:T(8,128)(2,1)S(1)}, u32[]{:S(2)}, u32[]{:S(2)}) async-start(bf16[16,80,256]{2,1,0:T(8,128)(2,1)} %get-tuple-element.102), calls=%async_computation.4 | async-start | bytes 1310720 | tf_op jit(solution)/shard_map/all_to_all | solution.py:496
  112.0 10.7 %grads_b.1 = bf16[16,200,128]{2,1,0:T(8,128)(2,1)} custom-call(bf16[3072,2048]{1,0:T(8,128)(2,1)} %get-tuple-element.78.e1, bf16[3072,1024]{1,0:T(8,128)(2,1)} %get-tuple-element.88.e2, f32[8,2048]{1,0:T(8,128)} %get-tuple-element.89.inv1, f32[8,1024]{1,0:T(8,128)} %get-tuple-element.90.inv2, bf16[80,3072]{1,0:T(8,128)(2,1)} %get-tuple-element.86.qt.qt_ref, ...), custom_call_target="tpu_custom_call" | custom-call | flops 2013265920 | bytes 11000000 | tf_op jit(solution)/shard_map/grads_b/pallas_call | solution.py:402
  122.7 2.3 %all-to-all-done.4.a_ref = bf16[16,80,256]{2,1,0:T(8,128)(2,1)S(1)} async-done(((bf16[16,80,256]{2,1,0:T(8,128)(2,1)}), bf16[16,80,256]{2,1,0:T(8,128)(2,1)S(1)}, u32[]{:S(2)}, u32[]{:S(2)}) %all-to-all-start.4) | async-done | bytes 655392 | tf_op jit(solution)/shard_map/all_to_all | solution.py:496
  125.0 5.0 %all-to-all-start.3 = ((bf16[16,200,128]{2,1,0:T(8,128)(2,1)}), bf16[16,200,128]{2,1,0:T(8,128)(2,1)S(1)}, u32[]{:S(2)}, u32[]{:S(2)}) async-start(bf16[16,200,128]{2,1,0:T(8,128)(2,1)} %grads_b.1), calls=%async_computation.3 | async-start | bytes 1638400 | tf_op jit(solution)/shard_map/all_to_all | solution.py:496
  130.0 3.1 %collective-permute-start.16 = (f32[40,1280]{1,0:T(8,128)S(1)}, f32[40,1280]{1,0:T(8,128)S(1)}, u32[]{:S(2)}, u32[]{:S(2)}) collective-permute-start(f32[40,1280]{1,0:T(8,128)S(1)} %add_add_fusion.w0), channel_id=1, source_target_pairs={{0,144},{16,128},{128,16},{144,0},{1,145},{17,129},{129,17},{145,1... | collective-permute-start | bytes 614408 | tf_op jit(solution)/shard_map/ppermute | solution.py:549
  134.3 13.3 %collective-permute-done.16.w3 = f32[40,1280]{1,0:T(8,128)S(1)} collective-permute-done((f32[40,1280]{1,0:T(8,128)S(1)}, f32[40,1280]{1,0:T(8,128)S(1)}, u32[]{:S(2)}, u32[]{:S(2)}) %collective-permute-start.16) | collective-permute-done | bytes 204832 | tf_op jit(solution)/shard_map/ppermute | solution.py:549
  147.6 3.7 %collective-permute-done.14.w1 = f32[40,1280]{1,0:T(8,128)S(1)} collective-permute-done((f32[40,1280]{1,0:T(8,128)S(1)}, f32[40,1280]{1,0:T(8,128)S(1)}, u32[]{:S(2)}, u32[]{:S(2)}) %collective-permute-start.14) | collective-permute-done | bytes 204832 | tf_op jit(solution)/shard_map/ppermute | solution.py:547
  (65 shorter events, 13.0 us)
Async XLA Ops:
  0.6 7.4 %collective-permute-start.1 = (bf16[1,192,1280]{2,1,0:T(8,128)(2,1)}, bf16[1,192,1280]{2,1,0:T(8,128)(2,1)S(1)}, u32[]{:S(2)}, u32[]{:S(2)}) collective-permute-start(bf16[1,192,1280]{2,1,0:T(8,128)(2,1)} %g_own.1), channel_id=1, source_target_pairs={{0,16},{16,0},{1,17},{17,1},{2,18},{18,2},{3,19},{19,3},{4,20},{20... | collective-permute-start | bytes 1474568 | tf_op jit(solution)/shard_map/ppermute | solution.py:511
  4.0 4.1 %collective-permute-start = (bf16[40,1280]{1,0:T(8,128)(2,1)S(1)}, bf16[40,1280]{1,0:T(8,128)(2,1)S(1)}, u32[]{:S(2)}, u32[]{:S(2)}) collective-permute-start(bf16[40,1280]{1,0:T(8,128)(2,1)S(1)} %constant_dynamic-slice_fusion), channel_id=1, source_target_pairs={{0,8},{8,0},{1,9},{9,1},{2,10},{10,2},{3,11},{11,3},{4,12},{12,4},... | collective-permute-start | bytes 307208 | tf_op jit(solution)/shard_map/ppermute | solution.py:510
  8.1 13.2 %collective-permute-start.3 = (bf16[2,40,1280]{2,1,0:T(8,128)(2,1)S(1)}, bf16[2,40,1280]{2,1,0:T(8,128)(2,1)S(1)}, u32[]{:S(2)}, u32[]{:S(2)}) collective-permute-start(bf16[2,40,1280]{2,1,0:T(8,128)(2,1)S(1)} %pad_maximum_fusion.refs_0_), channel_id=1, source_target_pairs={{0,7},{1,0},{2,1},{3,2},{4,3},{5,4},{6,5},{7,6},{8,15},{9,8},{10,9... | collective-permute-start | bytes 614408 | tf_op jit(solution)/shard_map/ppermute | solution.py:507
  13.4 7.9 %collective-permute-start.2 = (bf16[2,40,1280]{2,1,0:T(8,128)(2,1)S(1)}, bf16[2,40,1280]{2,1,0:T(8,128)(2,1)S(1)}, u32[]{:S(2)}, u32[]{:S(2)}) collective-permute-start(bf16[2,40,1280]{2,1,0:T(8,128)(2,1)S(1)} %pad_maximum_fusion.refs_0_), channel_id=1, source_target_pairs={{0,1},{1,2},{2,3},{3,4},{4,5},{5,6},{6,7},{7,0},{8,9},{9,10},{10,1... | collective-permute-start | bytes 614408 | tf_op jit(solution)/shard_map/ppermute | solution.py:504
  13.4 36.6 %all-to-all-start = ((bf16[16,120,384]{2,1,0:T(8,128)(2,1)}), bf16[16,120,384]{2,1,0:T(8,128)(2,1)S(1)}, u32[]{:S(2)}, u32[]{:S(2)}) async-start(bf16[16,120,384]{2,1,0:T(8,128)(2,1)} %pack_qkv.1), calls=%async_computation | async-start | bytes 2949120 | tf_op jit(solution)/shard_map/all_to_all | solution.py:496
  21.3 24.1 %copy-start.5 = (bf16[2,40,1280]{2,1,0:T(8,128)(2,1)}, bf16[2,40,1280]{2,1,0:T(8,128)(2,1)S(1)}, u32[]{:S(2)}) copy-start(bf16[2,40,1280]{2,1,0:T(8,128)(2,1)S(1)} %collective-permute-done.3.refs_2_) | copy-start | bytes 614404
  21.4 24.1 %copy-start.6 = (bf16[2,40,1280]{2,1,0:T(8,128)(2,1)}, bf16[2,40,1280]{2,1,0:T(8,128)(2,1)S(1)}, u32[]{:S(2)}) copy-start(bf16[2,40,1280]{2,1,0:T(8,128)(2,1)S(1)} %collective-permute-done.2.refs_1_) | copy-start | bytes 614404
  21.4 7.8 %collective-permute-start.4 = (bf16[2,40,1280]{2,1,0:T(8,128)(2,1)S(1)}, bf16[2,40,1280]{2,1,0:T(8,128)(2,1)S(1)}, u32[]{:S(2)}, u32[]{:S(2)}) collective-permute-start(bf16[2,40,1280]{2,1,0:T(8,128)(2,1)S(1)} %collective-permute-done.2.refs_1_), channel_id=1, source_target_pairs={{0,1},{1,2},{2,3},{3,4},{4,5},{5,6},{6,7},{7,0},{8,9},{9,10},{10,1... | collective-permute-start | bytes 614408 | tf_op jit(solution)/shard_map/ppermute | solution.py:504
  21.5 7.7 %collective-permute-start.5 = (bf16[2,40,1280]{2,1,0:T(8,128)(2,1)S(1)}, bf16[2,40,1280]{2,1,0:T(8,128)(2,1)S(1)}, u32[]{:S(2)}, u32[]{:S(2)}) collective-permute-start(bf16[2,40,1280]{2,1,0:T(8,128)(2,1)S(1)} %collective-permute-done.3.refs_2_), channel_id=1, source_target_pairs={{0,7},{1,0},{2,1},{3,2},{4,3},{5,4},{6,5},{7,6},{8,15},{9,8},{10,9... | collective-permute-start | bytes 614408 | tf_op jit(solution)/shard_map/ppermute | solution.py:507
  29.2 9.2 %collective-permute-start.8 = (bf16[16,40,192]{2,1,0:T(8,128)(2,1)}, bf16[16,40,192]{2,1,0:T(8,128)(2,1)S(1)}, u32[]{:S(2)}, u32[]{:S(2)}) collective-permute-start(bf16[16,40,192]{2,1,0:T(8,128)(2,1)} %get-tuple-element.66), channel_id=1, source_target_pairs={{0,16},{16,0},{1,17},{17,1},{2,18},{18,2},{3,19},{19,3},{4,20},{20... | collective-permute-start | bytes 737288 | tf_op jit(solution)/shard_map/ppermute | solution.py:520
  30.5 7.9 %collective-permute-start.6 = (bf16[2,40,1280]{2,1,0:T(8,128)(2,1)S(1)}, bf16[2,40,1280]{2,1,0:T(8,128)(2,1)S(1)}, u32[]{:S(2)}, u32[]{:S(2)}) collective-permute-start(bf16[2,40,1280]{2,1,0:T(8,128)(2,1)S(1)} %collective-permute-done.4.refs_3_), channel_id=1, source_target_pairs={{0,1},{1,2},{2,3},{3,4},{4,5},{5,6},{6,7},{7,0},{8,9},{9,10},{10,1... | collective-permute-start | bytes 614408 | tf_op jit(solution)/shard_map/ppermute | solution.py:504
  30.5 7.9 %collective-permute-start.7 = (bf16[2,40,1280]{2,1,0:T(8,128)(2,1)S(1)}, bf16[2,40,1280]{2,1,0:T(8,128)(2,1)S(1)}, u32[]{:S(2)}, u32[]{:S(2)}) collective-permute-start(bf16[2,40,1280]{2,1,0:T(8,128)(2,1)S(1)} %collective-permute-done.5.refs_4_), channel_id=1, source_target_pairs={{0,7},{1,0},{2,1},{3,2},{4,3},{5,4},{6,5},{7,6},{8,15},{9,8},{10,9... | collective-permute-start | bytes 614408 | tf_op jit(solution)/shard_map/ppermute | solution.py:507
  38.4 7.0 %collective-permute-start.9 = (bf16[2,40,1280]{2,1,0:T(8,128)(2,1)S(1)}, bf16[2,40,1280]{2,1,0:T(8,128)(2,1)S(1)}, u32[]{:S(2)}, u32[]{:S(2)}) collective-permute-start(bf16[2,40,1280]{2,1,0:T(8,128)(2,1)S(1)} %collective-permute-done.6.refs_5_), channel_id=1, source_target_pairs={{0,1},{1,2},{2,3},{3,4},{4,5},{5,6},{6,7},{7,0},{8,9},{9,10},{10,1... | collective-permute-start | bytes 614408 | tf_op jit(solution)/shard_map/ppermute | solution.py:504
  45.4 25.4 %collective-permute-start.10 = (bf16[8,40,1280]{2,1,0:T(8,128)(2,1)}, bf16[8,40,1280]{2,1,0:T(8,128)(2,1)S(1)}, u32[]{:S(2)}, u32[]{:S(2)}) collective-permute-start(bf16[8,40,1280]{2,1,0:T(8,128)(2,1)} %get-tuple-element.80), channel_id=1, source_target_pairs={{0,8},{8,0},{1,9},{9,1},{2,10},{10,2},{3,11},{11,3},{4,12},{12,4},... | collective-permute-start | bytes 2457608 | tf_op jit(solution)/shard_map/ppermute | solution.py:524
  50.0 23.8 %all-to-all-start.1 = ((bf16[16,48,384]{2,1,0:T(8,128)(2,1)}), bf16[16,48,384]{2,1,0:T(8,128)(2,1)S(1)}, u32[]{:S(2)}, u32[]{:S(2)}) async-start(bf16[16,48,384]{2,1,0:T(8,128)(2,1)} %out_grad.1), calls=%async_computation.1 | async-start | bytes 1179648 | tf_op jit(solution)/shard_map/all_to_all | solution.py:496
  73.8 28.4 %all-to-all-start.2 = ((bf16[8,40,1280]{2,1,0:T(8,128)(2,1)}), bf16[8,40,1280]{2,1,0:T(8,128)(2,1)S(1)}, u32[]{:S(2)}, u32[]{:S(2)}) async-start(bf16[8,40,1280]{2,1,0:T(8,128)(2,1)} %add_convert_fusion), calls=%async_computation.2 | async-start | bytes 1638400 | tf_op jit(solution)/shard_map/all_to_all | solution.py:534
  102.3 20.4 %collective-permute-start.13 = (f32[40,1280]{1,0:T(8,128)S(1)}, f32[40,1280]{1,0:T(8,128)S(1)}, u32[]{:S(2)}, u32[]{:S(2)}) collective-permute-start(f32[40,1280]{1,0:T(8,128)S(1)} %convert_reduce_fusion), channel_id=1, source_target_pairs={{0,96},{32,0},{64,32},{96,64},{1,97},{33,1},{65,33},{97,65},{2,98}... | collective-permute-start | bytes 614408 | tf_op jit(solution)/shard_map/ppermute | solution.py:543
  104.7 17.9 %collective-permute-start.12 = (f32[40,1280]{1,0:T(8,128)S(1)}, f32[40,1280]{1,0:T(8,128)S(1)}, u32[]{:S(2)}, u32[]{:S(2)}) collective-permute-start(f32[40,1280]{1,0:T(8,128)S(1)} %convert_reduce_fusion), channel_id=1, source_target_pairs={{0,64},{32,96},{64,0},{96,32},{1,65},{33,97},{65,1},{97,33},{2,66}... | collective-permute-start | bytes 614408 | tf_op jit(solution)/shard_map/ppermute | solution.py:543
  105.3 17.3 %collective-permute-start.11 = (f32[40,1280]{1,0:T(8,128)S(1)}, f32[40,1280]{1,0:T(8,128)S(1)}, u32[]{:S(2)}, u32[]{:S(2)}) collective-permute-start(f32[40,1280]{1,0:T(8,128)S(1)} %convert_reduce_fusion), channel_id=1, source_target_pairs={{0,32},{32,64},{64,96},{96,0},{1,33},{33,65},{65,97},{97,1},{2,34}... | collective-permute-start | bytes 614408 | tf_op jit(solution)/shard_map/ppermute | solution.py:543
  105.9 19.1 %all-to-all-start.4 = ((bf16[16,80,256]{2,1,0:T(8,128)(2,1)}), bf16[16,80,256]{2,1,0:T(8,128)(2,1)S(1)}, u32[]{:S(2)}, u32[]{:S(2)}) async-start(bf16[16,80,256]{2,1,0:T(8,128)(2,1)} %get-tuple-element.102), calls=%async_computation.4 | async-start | bytes 1310720 | tf_op jit(solution)/shard_map/all_to_all | solution.py:496
  125.0 26.4 %all-to-all-start.3 = ((bf16[16,200,128]{2,1,0:T(8,128)(2,1)}), bf16[16,200,128]{2,1,0:T(8,128)(2,1)S(1)}, u32[]{:S(2)}, u32[]{:S(2)}) async-start(bf16[16,200,128]{2,1,0:T(8,128)(2,1)} %grads_b.1), calls=%async_computation.3 | async-start | bytes 1638400 | tf_op jit(solution)/shard_map/all_to_all | solution.py:496
  130.0 17.7 %collective-permute-start.16 = (f32[40,1280]{1,0:T(8,128)S(1)}, f32[40,1280]{1,0:T(8,128)S(1)}, u32[]{:S(2)}, u32[]{:S(2)}) collective-permute-start(f32[40,1280]{1,0:T(8,128)S(1)} %add_add_fusion.w0), channel_id=1, source_target_pairs={{0,144},{16,128},{128,16},{144,0},{1,145},{17,129},{129,17},{145,1... | collective-permute-start | bytes 614408 | tf_op jit(solution)/shard_map/ppermute | solution.py:549
  133.1 14.5 %collective-permute-start.15 = (f32[40,1280]{1,0:T(8,128)S(1)}, f32[40,1280]{1,0:T(8,128)S(1)}, u32[]{:S(2)}, u32[]{:S(2)}) collective-permute-start(f32[40,1280]{1,0:T(8,128)S(1)} %add_add_fusion.w0), channel_id=1, source_target_pairs={{0,16},{16,0},{1,17},{17,1},{2,18},{18,2},{3,19},{19,3},{4,20},{20... | collective-permute-start | bytes 614408 | tf_op jit(solution)/shard_map/ppermute | solution.py:548
  133.2 18.1 %collective-permute-start.14 = (f32[40,1280]{1,0:T(8,128)S(1)}, f32[40,1280]{1,0:T(8,128)S(1)}, u32[]{:S(2)}, u32[]{:S(2)}) collective-permute-start(f32[40,1280]{1,0:T(8,128)S(1)} %add_add_fusion.w0), channel_id=1, source_target_pairs={{0,128},{128,0},{1,129},{129,1},{2,130},{130,2},{3,131},{131,3},{4... | collective-permute-start | bytes 614408 | tf_op jit(solution)/shard_map/ppermute | solution.py:547
  (12 other events, 121.2 us)

commit v6 on v4

--- a/solution.py
+++ b/solution.py
@@ -23,6 +23,7 @@
 SCALE = HD**-0.5
 LOG2E = 1.4426950408889634
 VMEM_LIMIT = 56 * 1024 * 1024
+LESS = 28 * 1024 * 1024
 SEQ = ("yh", "x", "c")
 DP = ("yl", "z")
 OFFSETS = (0, -1, 1, -2, 2, -3, 3, -4)
@@ -440,7 +441,7 @@
         in_specs=[whole(HEADS, HD, 2 * BIG)],
         out_specs=[spec, spec],
         out_shape=[shape, shape],
-        compiler_params=params(),
+        compiler_params=params(LESS),
         cost_estimate=cost(0, 2 * 10**6),
         name="unpack_a",
     )(a)
@@ -475,7 +476,7 @@
         out_specs=[whole(1, TOK, D), spec, spec, whole(HD, D)],
         out_shape=[shape] * 3 + [jax.ShapeDtypeStruct((HD, D), F32)],
         input_output_aliases={4: 1, 5: 2},
-        compiler_params=params(),
+        compiler_params=params(LESS),
         cost_estimate=cost(0, 3 * 10**6),
         name="unpack_b",
     )(at, b, *parts, dk, dv)
@@ -509,7 +510,9 @@
     pair = jnp.stack([w_half, lax.ppermute(w_half, "yl", swap)])
     g_oth = lax.ppermute(d_block, "c", swap)
     packed = pack_qkv(query, keys, values)
-    pair, packed, g_oth, attn = hold((pair, packed, g_oth, attn))
+    zs = [(z + o) % 8 for o in OFFSETS]
+    ids = scalar(*[y * 8 + k for k in zs for y in (yl, 1 - yl)])
+    pair, packed, g_oth, attn, ids = hold((pair, packed, g_oth, attn, ids))
     qkv = exchange(packed)
     f1, g1, attn = hold((up(pair), down(pair), attn))
     a_own, a_send = split_attn(scalar(c), attn)
@@ -520,8 +523,6 @@
     f4, give = hold((up(f3), give))
     came = lax.ppermute(give, "yl", swap)
 
-    zs = [(z + o) % 8 for o in OFFSETS]
-    ids = scalar(*[y * 8 + k for k in zs for y in (yl, 1 - yl)])
     dout = out_grad(ids, [pair, f1, g1, f2, g2, f3, g3, f4], gx, ax)
     dout, qkv = hold((dout, qkv))
     dout = exchange(dout)

time: 155 us -> 151 us (0.974)
  Pallas kernels: 64.5 us -> 62.1 us
  local copies, waits for them, and re-layouts: 3.03 us -> 1.37 us
    unnamed x36 -> x28, local copies, waits for them, and re-layouts: 2.33 us -> 0.68 us
  transfers between devices with their start and end apart: 21 -> 21, of which waited for: 9 -> 8; matrix products, arithmetic and copies ran while one was open for 1% -> 1% of each run, Pallas kernels for 40% -> 40%
where the time goes in v6:
time: 151 us; the launch traced here: 150 us
  Pallas kernels  62.1 us (41%)
  starting transfers between devices  56.3 us (37%)
  waiting for transfers between devices  28.3 us (19%)
    all_to_all x4, starting transfers between devices, exchange(): return lax.all_to_all(x, SEQ, 0, 0, tiled=True)  27.8 us
    pallas_call x2, Pallas kernels, scores_call(): pl.pallas_call(body, grid=(size // cols // 2,), in_specs=[whole(*x.shape)...  19.4 us
    pallas_call x1, Pallas kernels, grads_a(): pl.pallas_call(functools.partial(grads_a_body, rows), grid=(SRC * BIG //...  16.4 us
    ppermute x1, waiting for transfers between devices, body(): other = lax.ppermute(t, 'yh', swap)  13.2 us
    ppermute x3, starting transfers between devices, down(): return lax.ppermute(block, 'z', DOWN)  11.1 us
    pallas_call x1, Pallas kernels, grads_b(): pl.pallas_call(functools.partial(grads_b_body, rows), grid=(SRC * SMALL /...  10.7 us
    ppermute x4, waiting for transfers between devices, up(): return lax.ppermute(block, 'z', UP)  9.54 us
    pallas_call x1, Pallas kernels, weight_share(): pl.pallas_call(weight_share_body, in_specs=[pl.BlockSpec(memory_space=plt...  4.15 us
  transfers between devices with their start and end apart: 21, of which 8 were waited for; matrix products, arithmetic and copies ran while one was open for 1% of the time, Pallas kernels for 40%

profile of v6, /device:TPU:1, one launch (start us, length us, event | category | flops | bytes accessed | tf_op | source)
XLA Modules:
  0.0 150.4 jit_solution(9995603801627829823)
XLA Ops:
  0.6 3.3 %collective-permute-start.1 = (bf16[1,192,1280]{2,1,0:T(8,128)(2,1)}, bf16[1,192,1280]{2,1,0:T(8,128)(2,1)S(1)}, u32[]{:S(2)}, u32[]{:S(2)}) collective-permute-start(bf16[1,192,1280]{2,1,0:T(8,128)(2,1)} %g_own.1), channel_id=1, source_target_pairs={{0,16},{16,0},{1,17},{17,1},{2,18},{18,2},{3,19},{19,3},{4,20},{20... | collective-permute-start | bytes 1474568 | tf_op jit(solution)/shard_map/ppermute | solution.py:511
  4.2 3.2 %pack_qkv.1 = bf16[16,120,384]{2,1,0:T(8,128)(2,1)} custom-call(bf16[1,192,1280]{2,1,0:T(8,128)(2,1)} %q_ref.1, bf16[1,192,1280]{2,1,0:T(8,128)(2,1)} %k_ref.1, bf16[1,192,1280]{2,1,0:T(8,128)(2,1)} %v_ref.1), custom_call_target="tpu_custom_call" | custom-call | bytes 3000000 | tf_op jit(solution)/shard_map/pack_qkv/pallas_call | solution.py:62
  8.1 5.3 %collective-permute-start.3 = (bf16[2,40,1280]{2,1,0:T(8,128)(2,1)S(1)}, bf16[2,40,1280]{2,1,0:T(8,128)(2,1)S(1)}, u32[]{:S(2)}, u32[]{:S(2)}) collective-permute-start(bf16[2,40,1280]{2,1,0:T(8,128)(2,1)S(1)} %pad_maximum_fusion.refs_0_), channel_id=1, source_target_pairs={{0,7},{1,0},{2,1},{3,2},{4,3},{5,4},{6,5},{7,6},{8,15},{9,8},{10,9... | collective-permute-start | bytes 614408 | tf_op jit(solution)/shard_map/ppermute | solution.py:507
  13.5 7.9 %all-to-all-start = ((bf16[16,120,384]{2,1,0:T(8,128)(2,1)}), bf16[16,120,384]{2,1,0:T(8,128)(2,1)S(1)}, u32[]{:S(2)}, u32[]{:S(2)}) async-start(bf16[16,120,384]{2,1,0:T(8,128)(2,1)} %pack_qkv.1), calls=%async_computation | async-start | bytes 2949120 | tf_op jit(solution)/shard_map/all_to_all | solution.py:496
  21.5 3.0 %collective-permute-start.5 = (bf16[2,40,1280]{2,1,0:T(8,128)(2,1)S(1)}, bf16[2,40,1280]{2,1,0:T(8,128)(2,1)S(1)}, u32[]{:S(2)}, u32[]{:S(2)}) collective-permute-start(bf16[2,40,1280]{2,1,0:T(8,128)(2,1)S(1)} %collective-permute-done.3.refs_2_), channel_id=1, source_target_pairs={{0,7},{1,0},{2,1},{3,2},{4,3},{5,4},{6,5},{7,6},{8,15},{9,8},{10,9... | collective-permute-start | bytes 614408 | tf_op jit(solution)/shard_map/ppermute | solution.py:507
  24.5 2.1 %split_attn.1 = (bf16[16,40,192]{2,1,0:T(8,128)(2,1)}, bf16[16,40,192]{2,1,0:T(8,128)(2,1)}) custom-call(s32[1]{0:T(128)} %bitcast.c_ref.at_ref, bf16[1,192,1280]{2,1,0:T(8,128)(2,1)} %a_ref), custom_call_target="tpu_custom_call" | custom-call | bytes 1000000 | tf_op jit(solution)/shard_map/split_attn/pallas_call | solution.py:84
  26.7 2.5 %collective-permute-done.4.refs_3_ = bf16[2,40,1280]{2,1,0:T(8,128)(2,1)S(1)} collective-permute-done((bf16[2,40,1280]{2,1,0:T(8,128)(2,1)S(1)}, bf16[2,40,1280]{2,1,0:T(8,128)(2,1)S(1)}, u32[]{:S(2)}, u32[]{:S(2)}) %collective-permute-start.4) | collective-permute-done | bytes 204832 | tf_op jit(solution)/shard_map/ppermute | solution.py:504
  30.6 2.7 %collective-permute-start.7 = (bf16[2,40,1280]{2,1,0:T(8,128)(2,1)S(1)}, bf16[2,40,1280]{2,1,0:T(8,128)(2,1)S(1)}, u32[]{:S(2)}, u32[]{:S(2)}) collective-permute-start(bf16[2,40,1280]{2,1,0:T(8,128)(2,1)S(1)} %collective-permute-done.5.refs_4_), channel_id=1, source_target_pairs={{0,7},{1,0},{2,1},{3,2},{4,3},{5,4},{6,5},{7,6},{8,15},{9,8},{10,9... | collective-permute-start | bytes 614408 | tf_op jit(solution)/shard_map/ppermute | solution.py:507
  33.3 5.2 %collective-permute-done.6.refs_5_ = bf16[2,40,1280]{2,1,0:T(8,128)(2,1)S(1)} collective-permute-done((bf16[2,40,1280]{2,1,0:T(8,128)(2,1)S(1)}, bf16[2,40,1280]{2,1,0:T(8,128)(2,1)S(1)}, u32[]{:S(2)}, u32[]{:S(2)}) %collective-permute-start.6) | collective-permute-done | bytes 204832 | tf_op jit(solution)/shard_map/ppermute | solution.py:504
  39.5 4.1 %weight_share.1 = (bf16[8,40,1280]{2,1,0:T(8,128)(2,1)}, bf16[8,40,1280]{2,1,0:T(8,128)(2,1)}, bf16[384,1280]{1,0:T(8,128)(2,1)}, bf16[16,40,384]{2,1,0:T(8,128)(2,1)}) custom-call(s32[1]{0:T(128)} %bitcast.19.y_ref, bf16[1,192,1280]{2,1,0:T(8,128)(2,1)} %g_own.1, bf16[1,192,1280]{2,1,0:T(8,128)(2,1)} %copy-done.12, ...), custom_call_target="tpu_custom_call" | custom-call | flops 629145600 | bytes 6000000 | tf_op jit(solution)/shard_map/weight_share/pallas_call | solution.py:115
  46.1 3.9 %out_grad.1 = bf16[16,48,384]{2,1,0:T(8,128)(2,1)} custom-call(s32[16]{0:T(128)} %stack.87.ids, bf16[2,40,1280]{2,1,0:T(8,128)(2,1)} %copy-done.4, bf16[2,40,1280]{2,1,0:T(8,128)(2,1)} %copy-done.6, bf16[2,40,1280]{2,1,0:T(8,128)(2,1)} %copy-done.5, bf16[2,40,1280]{2,1,0:T(8,128)(2,1)} %copy-done.7, bf16[2,40,1280]{2,1,0:T(8,128)(2,1)} %copy-done.8, ...), custom_call_target="tpu_custom_call" | custom-call | flops 629145600 | bytes 4000000 | tf_op jit(solution)/shard_map/out_grad/pallas_call | solution.py:151
  50.1 8.8 %all-to-all-start.1 = ((bf16[16,48,384]{2,1,0:T(8,128)(2,1)}), bf16[16,48,384]{2,1,0:T(8,128)(2,1)S(1)}, u32[]{:S(2)}, u32[]{:S(2)}) async-start(bf16[16,48,384]{2,1,0:T(8,128)(2,1)} %out_grad.1), calls=%async_computation.1 | async-start | bytes 1179648 | tf_op jit(solution)/shard_map/all_to_all | solution.py:496
  58.8 12.0 %scores_a.1 = (bf16[3072,2048]{1,0:T(8,128)(2,1)}, f32[8,2048]{1,0:T(8,128)}, bf16[80,3072]{1,0:T(8,128)(2,1)}, bf16[3072,80]{1,0:T(8,128)(2,1)}, bf16[80,3072]{1,0:T(8,128)(2,1)}, /*index=5*/bf16[3072,96]{1,0:T(8,128)(2,1)}) custom-call(bf16[16,120,384]{2,1,0:T(8,128)(2,1)} %copy-done.2), custom_call_target="tpu_custom_call" | custom-call | flops 1006632960 | bytes 12582912 | tf_op jit(solution)/shard_map/scores_a/pallas_call | solution.py:250
  71.9 1.9 %all-to-all-done.1.x_ref = bf16[16,48,384]{2,1,0:T(8,128)(2,1)S(1)} async-done(((bf16[16,48,384]{2,1,0:T(8,128)(2,1)}), bf16[16,48,384]{2,1,0:T(8,128)(2,1)S(1)}, u32[]{:S(2)}, u32[]{:S(2)}) %all-to-all-start.1) | async-done | bytes 589856 | tf_op jit(solution)/shard_map/all_to_all | solution.py:496
  73.8 4.1 %all-to-all-start.2 = ((bf16[8,40,1280]{2,1,0:T(8,128)(2,1)}), bf16[8,40,1280]{2,1,0:T(8,128)(2,1)S(1)}, u32[]{:S(2)}, u32[]{:S(2)}) async-start(bf16[8,40,1280]{2,1,0:T(8,128)(2,1)} %add_convert_fusion), calls=%async_computation.2 | async-start | bytes 1638400 | tf_op jit(solution)/shard_map/all_to_all | solution.py:534
  77.9 7.4 %scores_b.1 = (bf16[3072,1024]{1,0:T(8,128)(2,1)}, f32[8,1024]{1,0:T(8,128)}) custom-call(bf16[80,3072]{1,0:T(8,128)(2,1)} %get-tuple-element.84.qt.qt_ref, bf16[3072,80]{1,0:T(8,128)(2,1)} %get-tuple-element.85.kn), custom_call_target="tpu_custom_call" | custom-call | flops 503316480 | bytes 6291456 | tf_op jit(solution)/shard_map/scores_b/pallas_call | solution.py:250
  85.3 16.4 %grads_a.1 = (bf16[16,80,256]{2,1,0:T(8,128)(2,1)}, f32[80,3072]{1,0:T(8,128)}, bf16[96,3072]{1,0:T(8,128)(2,1)}, bf16[80,3072]{1,0:T(8,128)(2,1)}) custom-call(bf16[16,48,384]{2,1,0:T(8,128)(2,1)} %copy-done.1, bf16[3072,2048]{1,0:T(8,128)(2,1)} %get-tuple-element.76.e1, bf16[3072,1024]{1,0:T(8,128)(2,1)} %get-tuple-element.86.e2, ...), custom_call_target="tpu_custom_call" | custom-call | flops 4026531840 | bytes 18000000 | tf_op jit(solution)/shard_map/grads_a/pallas_call | solution.py:340
  102.3 2.5 %collective-permute-start.13 = (f32[40,1280]{1,0:T(8,128)S(1)}, f32[40,1280]{1,0:T(8,128)S(1)}, u32[]{:S(2)}, u32[]{:S(2)}) collective-permute-start(f32[40,1280]{1,0:T(8,128)S(1)} %convert_reduce_fusion), channel_id=1, source_target_pairs={{0,96},{32,0},{64,32},{96,64},{1,97},{33,1},{65,33},{97,65},{2,98}... | collective-permute-start | bytes 614408 | tf_op jit(solution)/shard_map/ppermute | solution.py:543
  105.9 6.1 %all-to-all-start.4 = ((bf16[16,80,256]{2,1,0:T(8,128)(2,1)}), bf16[16,80,256]{2,1,0:T(8,128)(2,1)S(1)}, u32[]{:S(2)}, u32[]{:S(2)}) async-start(bf16[16,80,256]{2,1,0:T(8,128)(2,1)} %get-tuple-element.100), calls=%async_computation.4 | async-start | bytes 1310720 | tf_op jit(solution)/shard_map/all_to_all | solution.py:496
  112.0 10.7 %grads_b.1 = bf16[16,200,128]{2,1,0:T(8,128)(2,1)} custom-call(bf16[3072,2048]{1,0:T(8,128)(2,1)} %get-tuple-element.76.e1, bf16[3072,1024]{1,0:T(8,128)(2,1)} %get-tuple-element.86.e2, f32[8,2048]{1,0:T(8,128)} %get-tuple-element.87.inv1, f32[8,1024]{1,0:T(8,128)} %get-tuple-element.88.inv2, bf16[80,3072]{1,0:T(8,128)(2,1)} %get-tuple-element.84.qt.qt_ref, ...), custom_call_target="tpu_custom_call" | custom-call | flops 2013265920 | bytes 11000000 | tf_op jit(solution)/shard_map/grads_b/pallas_call | solution.py:402
  122.8 2.2 %all-to-all-done.4.a_ref = bf16[16,80,256]{2,1,0:T(8,128)(2,1)S(1)} async-done(((bf16[16,80,256]{2,1,0:T(8,128)(2,1)}), bf16[16,80,256]{2,1,0:T(8,128)(2,1)S(1)}, u32[]{:S(2)}, u32[]{:S(2)}) %all-to-all-start.4) | async-done | bytes 655392 | tf_op jit(solution)/shard_map/all_to_all | solution.py:496
  124.9 5.1 %all-to-all-start.3 = ((bf16[16,200,128]{2,1,0:T(8,128)(2,1)}), bf16[16,200,128]{2,1,0:T(8,128)(2,1)S(1)}, u32[]{:S(2)}, u32[]{:S(2)}) async-start(bf16[16,200,128]{2,1,0:T(8,128)(2,1)} %grads_b.1), calls=%async_computation.3 | async-start | bytes 1638400 | tf_op jit(solution)/shard_map/all_to_all | solution.py:496
  130.0 2.9 %collective-permute-start.14 = (f32[40,1280]{1,0:T(8,128)S(1)}, f32[40,1280]{1,0:T(8,128)S(1)}, u32[]{:S(2)}, u32[]{:S(2)}) collective-permute-start(f32[40,1280]{1,0:T(8,128)S(1)} %add_add_fusion), channel_id=1, source_target_pairs={{0,128},{128,0},{1,129},{129,1},{2,130},{130,2},{3,131},{131,3},{4... | collective-permute-start | bytes 614408 | tf_op jit(solution)/shard_map/ppermute | solution.py:546
  133.9 13.2 %collective-permute-done.14 = f32[40,1280]{1,0:T(8,128)S(1)} collective-permute-done((f32[40,1280]{1,0:T(8,128)S(1)}, f32[40,1280]{1,0:T(8,128)S(1)}, u32[]{:S(2)}, u32[]{:S(2)}) %collective-permute-start.14) | collective-permute-done | bytes 204832 | tf_op jit(solution)/shard_map/ppermute | solution.py:546
  (64 shorter events, 13.0 us)
Async XLA Ops:
  0.6 7.5 %collective-permute-start.1 = (bf16[1,192,1280]{2,1,0:T(8,128)(2,1)}, bf16[1,192,1280]{2,1,0:T(8,128)(2,1)S(1)}, u32[]{:S(2)}, u32[]{:S(2)}) collective-permute-start(bf16[1,192,1280]{2,1,0:T(8,128)(2,1)} %g_own.1), channel_id=1, source_target_pairs={{0,16},{16,0},{1,17},{17,1},{2,18},{18,2},{3,19},{19,3},{4,20},{20... | collective-permute-start | bytes 1474568 | tf_op jit(solution)/shard_map/ppermute | solution.py:511
  4.0 4.1 %collective-permute-start = (bf16[40,1280]{1,0:T(8,128)(2,1)S(1)}, bf16[40,1280]{1,0:T(8,128)(2,1)S(1)}, u32[]{:S(2)}, u32[]{:S(2)}) collective-permute-start(bf16[40,1280]{1,0:T(8,128)(2,1)S(1)} %constant_dynamic-slice_fusion), channel_id=1, source_target_pairs={{0,8},{8,0},{1,9},{9,1},{2,10},{10,2},{3,11},{11,3},{4,12},{12,4},... | collective-permute-start | bytes 307208 | tf_op jit(solution)/shard_map/ppermute | solution.py:510
  8.1 18.5 %copy-start.4 = (bf16[2,40,1280]{2,1,0:T(8,128)(2,1)}, bf16[2,40,1280]{2,1,0:T(8,128)(2,1)S(1)}, u32[]{:S(2)}) copy-start(bf16[2,40,1280]{2,1,0:T(8,128)(2,1)S(1)} %pad_maximum_fusion.refs_0_) | copy-start | bytes 614404
  8.1 13.2 %collective-permute-start.3 = (bf16[2,40,1280]{2,1,0:T(8,128)(2,1)S(1)}, bf16[2,40,1280]{2,1,0:T(8,128)(2,1)S(1)}, u32[]{:S(2)}, u32[]{:S(2)}) collective-permute-start(bf16[2,40,1280]{2,1,0:T(8,128)(2,1)S(1)} %pad_maximum_fusion.refs_0_), channel_id=1, source_target_pairs={{0,7},{1,0},{2,1},{3,2},{4,3},{5,4},{6,5},{7,6},{8,15},{9,8},{10,9... | collective-permute-start | bytes 614408 | tf_op jit(solution)/shard_map/ppermute | solution.py:507
  13.5 7.9 %collective-permute-start.2 = (bf16[2,40,1280]{2,1,0:T(8,128)(2,1)S(1)}, bf16[2,40,1280]{2,1,0:T(8,128)(2,1)S(1)}, u32[]{:S(2)}, u32[]{:S(2)}) collective-permute-start(bf16[2,40,1280]{2,1,0:T(8,128)(2,1)S(1)} %pad_maximum_fusion.refs_0_), channel_id=1, source_target_pairs={{0,1},{1,2},{2,3},{3,4},{4,5},{5,6},{6,7},{7,0},{8,9},{9,10},{10,1... | collective-permute-start | bytes 614408 | tf_op jit(solution)/shard_map/ppermute | solution.py:504
  13.5 36.6 %all-to-all-start = ((bf16[16,120,384]{2,1,0:T(8,128)(2,1)}), bf16[16,120,384]{2,1,0:T(8,128)(2,1)S(1)}, u32[]{:S(2)}, u32[]{:S(2)}) async-start(bf16[16,120,384]{2,1,0:T(8,128)(2,1)} %pack_qkv.1), calls=%async_computation | async-start | bytes 2949120 | tf_op jit(solution)/shard_map/all_to_all | solution.py:496
  21.4 24.1 %copy-start.5 = (bf16[2,40,1280]{2,1,0:T(8,128)(2,1)}, bf16[2,40,1280]{2,1,0:T(8,128)(2,1)S(1)}, u32[]{:S(2)}) copy-start(bf16[2,40,1280]{2,1,0:T(8,128)(2,1)S(1)} %collective-permute-done.3.refs_2_) | copy-start | bytes 614404
  21.4 24.1 %copy-start.6 = (bf16[2,40,1280]{2,1,0:T(8,128)(2,1)}, bf16[2,40,1280]{2,1,0:T(8,128)(2,1)S(1)}, u32[]{:S(2)}) copy-start(bf16[2,40,1280]{2,1,0:T(8,128)(2,1)S(1)} %collective-permute-done.2.refs_1_) | copy-start | bytes 614404
  21.4 7.8 %collective-permute-start.4 = (bf16[2,40,1280]{2,1,0:T(8,128)(2,1)S(1)}, bf16[2,40,1280]{2,1,0:T(8,128)(2,1)S(1)}, u32[]{:S(2)}, u32[]{:S(2)}) collective-permute-start(bf16[2,40,1280]{2,1,0:T(8,128)(2,1)S(1)} %collective-permute-done.2.refs_1_), channel_id=1, source_target_pairs={{0,1},{1,2},{2,3},{3,4},{4,5},{5,6},{6,7},{7,0},{8,9},{9,10},{10,1... | collective-permute-start | bytes 614408 | tf_op jit(solution)/shard_map/ppermute | solution.py:504
  21.5 7.7 %collective-permute-start.5 = (bf16[2,40,1280]{2,1,0:T(8,128)(2,1)S(1)}, bf16[2,40,1280]{2,1,0:T(8,128)(2,1)S(1)}, u32[]{:S(2)}, u32[]{:S(2)}) collective-permute-start(bf16[2,40,1280]{2,1,0:T(8,128)(2,1)S(1)} %collective-permute-done.3.refs_2_), channel_id=1, source_target_pairs={{0,7},{1,0},{2,1},{3,2},{4,3},{5,4},{6,5},{7,6},{8,15},{9,8},{10,9... | collective-permute-start | bytes 614408 | tf_op jit(solution)/shard_map/ppermute | solution.py:507
  29.2 9.2 %collective-permute-start.8 = (bf16[16,40,192]{2,1,0:T(8,128)(2,1)}, bf16[16,40,192]{2,1,0:T(8,128)(2,1)S(1)}, u32[]{:S(2)}, u32[]{:S(2)}) collective-permute-start(bf16[16,40,192]{2,1,0:T(8,128)(2,1)} %get-tuple-element.64), channel_id=1, source_target_pairs={{0,16},{16,0},{1,17},{17,1},{2,18},{18,2},{3,19},{19,3},{4,20},{20... | collective-permute-start | bytes 737288 | tf_op jit(solution)/shard_map/ppermute | solution.py:520
  30.6 7.9 %collective-permute-start.6 = (bf16[2,40,1280]{2,1,0:T(8,128)(2,1)S(1)}, bf16[2,40,1280]{2,1,0:T(8,128)(2,1)S(1)}, u32[]{:S(2)}, u32[]{:S(2)}) collective-permute-start(bf16[2,40,1280]{2,1,0:T(8,128)(2,1)S(1)} %collective-permute-done.4.refs_3_), channel_id=1, source_target_pairs={{0,1},{1,2},{2,3},{3,4},{4,5},{5,6},{6,7},{7,0},{8,9},{9,10},{10,1... | collective-permute-start | bytes 614408 | tf_op jit(solution)/shard_map/ppermute | solution.py:504
  30.6 7.9 %collective-permute-start.7 = (bf16[2,40,1280]{2,1,0:T(8,128)(2,1)S(1)}, bf16[2,40,1280]{2,1,0:T(8,128)(2,1)S(1)}, u32[]{:S(2)}, u32[]{:S(2)}) collective-permute-start(bf16[2,40,1280]{2,1,0:T(8,128)(2,1)S(1)} %collective-permute-done.5.refs_4_), channel_id=1, source_target_pairs={{0,7},{1,0},{2,1},{3,2},{4,3},{5,4},{6,5},{7,6},{8,15},{9,8},{10,9... | collective-permute-start | bytes 614408 | tf_op jit(solution)/shard_map/ppermute | solution.py:507
  38.4 7.0 %collective-permute-start.9 = (bf16[2,40,1280]{2,1,0:T(8,128)(2,1)S(1)}, bf16[2,40,1280]{2,1,0:T(8,128)(2,1)S(1)}, u32[]{:S(2)}, u32[]{:S(2)}) collective-permute-start(bf16[2,40,1280]{2,1,0:T(8,128)(2,1)S(1)} %collective-permute-done.6.refs_5_), channel_id=1, source_target_pairs={{0,1},{1,2},{2,3},{3,4},{4,5},{5,6},{6,7},{7,0},{8,9},{9,10},{10,1... | collective-permute-start | bytes 614408 | tf_op jit(solution)/shard_map/ppermute | solution.py:504
  45.5 25.4 %collective-permute-start.10 = (bf16[8,40,1280]{2,1,0:T(8,128)(2,1)}, bf16[8,40,1280]{2,1,0:T(8,128)(2,1)S(1)}, u32[]{:S(2)}, u32[]{:S(2)}) collective-permute-start(bf16[8,40,1280]{2,1,0:T(8,128)(2,1)} %get-tuple-element.78), channel_id=1, source_target_pairs={{0,8},{8,0},{1,9},{9,1},{2,10},{10,2},{3,11},{11,3},{4,12},{12,4},... | collective-permute-start | bytes 2457608 | tf_op jit(solution)/shard_map/ppermute | solution.py:524
  50.1 23.8 %all-to-all-start.1 = ((bf16[16,48,384]{2,1,0:T(8,128)(2,1)}), bf16[16,48,384]{2,1,0:T(8,128)(2,1)S(1)}, u32[]{:S(2)}, u32[]{:S(2)}) async-start(bf16[16,48,384]{2,1,0:T(8,128)(2,1)} %out_grad.1), calls=%async_computation.1 | async-start | bytes 1179648 | tf_op jit(solution)/shard_map/all_to_all | solution.py:496
  73.8 28.4 %all-to-all-start.2 = ((bf16[8,40,1280]{2,1,0:T(8,128)(2,1)}), bf16[8,40,1280]{2,1,0:T(8,128)(2,1)S(1)}, u32[]{:S(2)}, u32[]{:S(2)}) async-start(bf16[8,40,1280]{2,1,0:T(8,128)(2,1)} %add_convert_fusion), calls=%async_computation.2 | async-start | bytes 1638400 | tf_op jit(solution)/shard_map/all_to_all | solution.py:534
  102.3 20.4 %collective-permute-start.13 = (f32[40,1280]{1,0:T(8,128)S(1)}, f32[40,1280]{1,0:T(8,128)S(1)}, u32[]{:S(2)}, u32[]{:S(2)}) collective-permute-start(f32[40,1280]{1,0:T(8,128)S(1)} %convert_reduce_fusion), channel_id=1, source_target_pairs={{0,96},{32,0},{64,32},{96,64},{1,97},{33,1},{65,33},{97,65},{2,98}... | collective-permute-start | bytes 614408 | tf_op jit(solution)/shard_map/ppermute | solution.py:543
  104.8 17.9 %collective-permute-start.12 = (f32[40,1280]{1,0:T(8,128)S(1)}, f32[40,1280]{1,0:T(8,128)S(1)}, u32[]{:S(2)}, u32[]{:S(2)}) collective-permute-start(f32[40,1280]{1,0:T(8,128)S(1)} %convert_reduce_fusion), channel_id=1, source_target_pairs={{0,64},{32,96},{64,0},{96,32},{1,65},{33,97},{65,1},{97,33},{2,66}... | collective-permute-start | bytes 614408 | tf_op jit(solution)/shard_map/ppermute | solution.py:543
  105.4 17.3 %collective-permute-start.11 = (f32[40,1280]{1,0:T(8,128)S(1)}, f32[40,1280]{1,0:T(8,128)S(1)}, u32[]{:S(2)}, u32[]{:S(2)}) collective-permute-start(f32[40,1280]{1,0:T(8,128)S(1)} %convert_reduce_fusion), channel_id=1, source_target_pairs={{0,32},{32,64},{64,96},{96,0},{1,33},{33,65},{65,97},{97,1},{2,34}... | collective-permute-start | bytes 614408 | tf_op jit(solution)/shard_map/ppermute | solution.py:543
  105.9 19.0 %all-to-all-start.4 = ((bf16[16,80,256]{2,1,0:T(8,128)(2,1)}), bf16[16,80,256]{2,1,0:T(8,128)(2,1)S(1)}, u32[]{:S(2)}, u32[]{:S(2)}) async-start(bf16[16,80,256]{2,1,0:T(8,128)(2,1)} %get-tuple-element.100), calls=%async_computation.4 | async-start | bytes 1310720 | tf_op jit(solution)/shard_map/all_to_all | solution.py:496
  124.9 24.2 %all-to-all-start.3 = ((bf16[16,200,128]{2,1,0:T(8,128)(2,1)}), bf16[16,200,128]{2,1,0:T(8,128)(2,1)S(1)}, u32[]{:S(2)}, u32[]{:S(2)}) async-start(bf16[16,200,128]{2,1,0:T(8,128)(2,1)} %grads_b.1), calls=%async_computation.3 | async-start | bytes 1638400 | tf_op jit(solution)/shard_map/all_to_all | solution.py:496
  130.0 17.0 %collective-permute-start.14 = (f32[40,1280]{1,0:T(8,128)S(1)}, f32[40,1280]{1,0:T(8,128)S(1)}, u32[]{:S(2)}, u32[]{:S(2)}) collective-permute-start(f32[40,1280]{1,0:T(8,128)S(1)} %add_add_fusion), channel_id=1, source_target_pairs={{0,128},{128,0},{1,129},{129,1},{2,130},{130,2},{3,131},{131,3},{4... | collective-permute-start | bytes 614408 | tf_op jit(solution)/shard_map/ppermute | solution.py:546
  147.1 2.0 %collective-permute-start.15 = (f32[40,1280]{1,0:T(8,128)S(1)}, f32[40,1280]{1,0:T(8,128)S(1)}, u32[]{:S(2)}, u32[]{:S(2)}) collective-permute-start(f32[40,1280]{1,0:T(8,128)S(1)} %add.148.w_own), channel_id=1, source_target_pairs={{0,16},{16,0},{1,17},{17,1},{2,18},{18,2},{3,19},{19,3},{4,20},{20... | collective-permute-start | bytes 614408 | tf_op jit(solution)/shard_map/ppermute | solution.py:549
  (11 other events, 102.6 us)
